TPU v7x, 32 devices: a whole 2x2x4 slice. The times are simulated.
32 devices in a mesh: groups: 2 (over y), ctx: 8 (over z, x), col: 2 (over core).
Axes of the slice: x: 2, y: 2, z: 4, core: 2. Of those that a mesh axis runs over, the one named last changes fastest.
Arguments:
- activations: bfloat16 [2048, 4096], P(('groups', 'ctx'), 'col'), parts along dimension 0, may hold values from -6 to 6
- gradients: bfloat16 [2048, 14336], P(('groups', 'ctx'), 'col'), parts along dimension 0, may hold values from -6 to 6
- doc_ids: int32 [2048], P(('groups', 'ctx')), parts along dimension 0, may hold values from 0 to 11, as said below
- proj_in: bfloat16 [4096, 64], P('col'), may hold values from -0.046875 to 0.046875
- proj_out: bfloat16 [14336, 64], P('col'), may hold values from -0.0234375 to 0.0234375
- inverse: float32 [4096, 4096], P('col', 'ctx')
- store_rows: bfloat16 [2048, 4096], P(('groups', 'ctx', 'col')), parts along dimension 0, may hold values from -0.09375 to 0.09375
Outputs:
- scores: float32 [12, 2048], P(None, ('groups', 'ctx', 'col')), parts along dimension 1
There are 2 independent parts, one for each index of `groups`. A program takes and returns all parts, laid end to end along the dimension named above; an argument that names none is the same for every part. Nothing has to cross between parts.
Inputs may be any that keep to these rules, and one draw needn't show every extreme that they name: `doc_ids`: document numbers never fall and rise by at most one from a token to the next, starting at 0. Every aligned block of 128 tokens holds the last token of one or two documents; the last token of the sequence ends document 12 - 1.
All inputs are finite; a program needn't handle non-finite values.
Results may differ from a plain program's by a relative error of at most 0.0029.
Values may be sent and summed in bfloat16 or wider, within the bound.
No kernel may reach another device: no remote copies, remote signals or barrier semaphores. Data moves between devices by JAX's collectives and lax.ppermute only.
A program may use at most 64 MiB of HBM per device.

v0:
```python
import jax
import jax.numpy as jnp
from jax import lax
from jax.sharding import PartitionSpec as P


def from_behind(block, axis, distance):
    devices = range(lax.axis_size(axis))
    route = [(i - distance, i) for i in devices if i - distance in devices]
    return lax.ppermute(block, axis, route)


def shards(activations, gradients, doc_ids, proj_in, proj_out, inverse, store_rows):
    left_part = jnp.dot(activations, proj_in, preferred_element_type=jnp.float32)
    right_part = jnp.dot(gradients, proj_out, preferred_element_type=jnp.float32)
    proj_left, proj_right = lax.psum((left_part, right_part), "col")
    proj_rank = proj_right.shape[1]
    half_rank = proj_rank // lax.axis_size("col")
    own_half = lax.dynamic_slice_in_dim(proj_left, lax.axis_index("col") * half_rank, half_rank, 1)
    first_doc = doc_ids[0]
    slot_index = doc_ids - first_doc
    onehot = (slot_index[:, None] == jnp.arange(3, dtype=jnp.int32)[None, :]).astype(jnp.float32)
    weighted = (onehot[:, :, None] * own_half[:, None, :]).reshape(own_half.shape[0], 3 * half_rank)
    local_sums = lax.dot_general(
        weighted,
        proj_right,
        (((0,), (0,)), ((), ())),
        precision=lax.Precision.HIGHEST,
        preferred_element_type=jnp.float32,
    ).reshape(3, half_rank * proj_rank)
    doc_count = 3 * lax.axis_size("ctx") // 2
    last_row = lax.dynamic_index_in_dim(local_sums, slot_index[-1], 0, keepdims=False)
    incoming, incoming_id = from_behind((last_row, doc_ids[-1].astype(jnp.float32)), "ctx", 1)
    matches = (incoming_id == first_doc.astype(jnp.float32)).astype(jnp.float32)
    head_row = local_sums[0] + matches * incoming
    owned_rows = jnp.stack([head_row, local_sums[1]])
    owned_ids = (first_doc + jnp.arange(2, dtype=jnp.int32)).astype(jnp.float32)
    gathered, gathered_ids = (
        lax.all_gather(owned_rows, "ctx", axis=0, tiled=True),
        lax.all_gather(owned_ids, "ctx", axis=0, tiled=True),
    )
    positions = jnp.arange(gathered.shape[0], dtype=jnp.int32)
    wanted = jnp.arange(doc_count, dtype=jnp.int32).astype(jnp.float32)
    found = gathered_ids[None, :] == wanted[:, None]
    chosen = jnp.max(jnp.where(found, positions[None, :], -1), axis=1)
    doc_grads = jnp.take(gathered, chosen, axis=0)
    partial_q = jnp.dot(
        doc_grads, inverse, precision=lax.Precision.HIGHEST, preferred_element_type=jnp.float32
    )
    precond = lax.psum(partial_q, "col").astype(jnp.bfloat16)
    return lax.dot_general(
        lax.all_gather(precond, "ctx", axis=1, tiled=True),
        store_rows,
        (((1,), (1,)), ((), ())),
        preferred_element_type=jnp.float32,
    )


def solution(mesh):
    in_specs = (
        P(("groups", "ctx"), "col"),
        P(("groups", "ctx"), "col"),
        P(("groups", "ctx")),
        P("col", None),
        P("col", None),
        P("col", "ctx"),
        P(("groups", "ctx", "col"), None),
    )
    out_specs = P(None, ("groups", "ctx", "col"))
    return jax.shard_map(shards, mesh=mesh, in_specs=in_specs, out_specs=out_specs, check_vma=False)
```

profile of v0, /device:TPU:0, one launch (start us, length us, event | category | flops | bytes accessed | tf_op | source)
XLA Modules:
  0.0 129.1 jit_solution(9993455877551389465)
XLA Ops:
  6.5 0.0 copy-start
  6.5 0.0 all-reduce.4.cloned.1.call-start
  6.5 1.4 %fusion.8 = (s32[1]{0:T(128)}, s32[1]{0:T(128)}) fusion(s32[128]{0:T(128)} %param.9), kind=kLoop, calls=%fused_computation.23 | loop fusion | bytes 16 | tf_op jit(solution)/shard_map/slice | solution.py:33
  8.6 6.2 %collective-permute-start = (f32[]{:T(128)}, f32[]{:T(128)}, u32[]{:S(2)}, u32[]{:S(2)}) collective-permute-start(f32[]{:T(128)} %bitcast.3), channel_id=1, source_target_pairs={{0,2},{2,4},{4,6},{6,8},{8,10},{10,12},{12,14},{1,3},{3,5},{5,7},{... | collective-permute-start | bytes 20 | tf_op jit(solution)/shard_map/ppermute | solution.py:10
  14.7 2.0 %fusion.9 = f32[128,64]{0,1:T(8,128)} fusion(bf16[128,2048]{1,0:T(8,128)(2,1)} %param.7, bf16[2048,64]{0,1:T(8,128)(2,1)} %param.10), kind=kOutput, calls=%fused_computation.24 | convolution fusion | flops 33554432 | bytes 819200 | tf_op jit(solution)/shard_map/dot_general | solution.py:14
  16.7 0.0 copy-done
  16.7 2.5 %fusion.10 = f32[128,64]{0,1:T(8,128)} fusion(bf16[128,7168]{1,0:T(8,128)(2,1)S(1)} %copy-done, bf16[7168,64]{0,1:T(8,128)(2,1)} %param.11), kind=kOutput, calls=%fused_computation.25 | convolution fusion | flops 117440512 | bytes 2785280 | tf_op jit(solution)/shard_map/dot_general | solution.py:15
  19.3 0.0 copy-start.1
  19.3 0.0 all-reduce.4.cloned.1.call-update
  19.3 1.3 broadcast_subtract_fusion
  20.6 1.2 dynamic-slice
  22.5 0.7 convert_dynamic-update-slice_fusion
  23.7 18.9 %all-reduce = f32[16]{0:T(128)S(1)} all-reduce(f32[16]{0:T(128)S(1)} %convert_dynamic-update-slice_fusion), channel_id=1, replica_groups=mesh['groups'=2,'ctx'=8,'col'=2] {'ctx'}, use_global_device_ids=true, to_apply=%add | all-reduce | flops 16 | bytes 128
  42.6 0.2 select_reduce_fusion
  42.8 0.6 slice.22
  45.4 0.0 collective-permute-done
  46.0 0.0 all-reduce.4.cloned.1.call-done
  46.0 0.7 constant_dynamic-slice_fusion.1
  46.8 1.0 fusion.11
  47.7 0.1 copy.16
  47.8 0.1 reshape.57
  48.0 2.5 %collective-permute-start.1 = (f32[2048]{0:T(1024)S(1)}, f32[2048]{0:T(1024)S(1)}, u32[]{:S(2)}, u32[]{:S(2)}) collective-permute-start(f32[2048]{0:T(1024)S(1)} %bitcast.24), channel_id=1, source_target_pairs={{0,2},{2,4},{4,6},{6,8},{8,10},{10,12},{12,14},{1,3},{3,5},{5,7},{... | collective-permute-start | bytes 24584 | tf_op jit(solution)/shard_map/ppermute | solution.py:10
  50.5 0.1 fusion.7
  50.5 0.1 copy.15
  50.6 0.1 squeeze.15
  50.7 0.1 copy.17
  50.7 0.1 slice.24
  50.8 1.0 collective-permute-done.1
  51.8 30.7 %all-gather = f32[8,2,2048]{2,1,0:T(2,128)S(1)} all-gather(f32[1,2,2048]{2,1,0:T(2,128)S(1)} %maximum_bitcast_fusion), channel_id=1, replica_groups=mesh['groups'=2,'ctx'=8,'col'=2] {'ctx'}, dimensions={0}, use_global_device_ids=true | all-gather | bytes 147456 | tf_op jit(solution)/shard_map/all_gather | solution.py:39
  82.5 0.1 reshape.70
  82.6 0.6 gather_fusion
  83.2 4.3 %fusion = f32[12,512]{1,0:T(8,128)S(1)} fusion(f32[2048,512]{1,0:T(8,128)} %param.12, f32[12,2048]{1,0:T(8,128)S(1)} %gather_fusion, pred[12]{0:T(512)(128)(4,1)S(1)} %compare_and_fusion), kind=kOutput, calls=%fused_computation.1 | convolution fusion | flops 151019520 | bytes 4317196 | tf_op jit(solution)/shard_map/dot_general | solution.py:47
  87.5 3.4 %psum.23 = bf16[12,512]{1,0:T(8,128)(2,1)S(1)} all-reduce(f32[12,512]{1,0:T(8,128)S(1)} %fusion), channel_id=1, replica_groups=mesh['groups'=2,'ctx'=8,'col'=2] {'col'}, use_global_device_ids=true, to_apply=%region_3.4 | all-reduce | flops 6144 | bytes 36864 | tf_op jit(solution)/shard_map/psum | solution.py:50
  90.9 30.5 %all_gather.11 = bf16[12,4096]{1,0:T(8,128)(2,1)S(1)} all-gather(bf16[12,512]{1,0:T(8,128)(2,1)S(1)} %psum.23), channel_id=1, replica_groups=mesh['groups'=2,'ctx'=8,'col'=2] {'ctx'}, dimensions={1}, use_global_device_ids=true | all-gather | bytes 110592 | tf_op jit(solution)/shard_map/all_gather | solution.py:52
  121.4 0.0 copy-done.1
  121.4 0.9 fusion.12
  (10 shorter events, 0.1 us)
Async XLA Ops:
  6.5 10.2 %copy-start = (bf16[128,7168]{1,0:T(8,128)(2,1)S(1)}, bf16[128,7168]{1,0:T(8,128)(2,1)}, u32[]{:S(2)}) copy-start(bf16[128,7168]{1,0:T(8,128)(2,1)} %param.8) | copy-start | bytes 5505028
  6.5 39.5 %all-reduce.4.cloned.1.call-start = ((), (), s32[]{:S(2)}) async-start(), calls=%async_computation | async-start | bytes 131072 | tf_op jit(solution)/shard_map/psum | solution.py:16
  8.6 36.8 %collective-permute-start = (f32[]{:T(128)}, f32[]{:T(128)}, u32[]{:S(2)}, u32[]{:S(2)}) collective-permute-start(f32[]{:T(128)} %bitcast.3), channel_id=1, source_target_pairs={{0,2},{2,4},{4,6},{6,8},{8,10},{10,12},{12,14},{1,3},{3,5},{5,7},{... | collective-permute-start | bytes 20 | tf_op jit(solution)/shard_map/ppermute | solution.py:10
  19.3 102.1 %copy-start.1 = (bf16[64,4096]{1,0:T(8,128)(2,1)S(1)}, bf16[64,4096]{1,0:T(8,128)(2,1)}, u32[]{:S(2)}) copy-start(bf16[64,4096]{1,0:T(8,128)(2,1)} %param.13) | copy-start | bytes 1572868
  48.0 3.9 %collective-permute-start.1 = (f32[2048]{0:T(1024)S(1)}, f32[2048]{0:T(1024)S(1)}, u32[]{:S(2)}, u32[]{:S(2)}) collective-permute-start(f32[2048]{0:T(1024)S(1)} %bitcast.24), channel_id=1, source_target_pairs={{0,2},{2,4},{4,6},{6,8},{8,10},{10,12},{12,14},{1,3},{3,5},{5,7},{... | collective-permute-start | bytes 24584 | tf_op jit(solution)/shard_map/ppermute | solution.py:10
Sparse Core Ops, SparseCore 0:
  19.4 18.0 all-reduce.3
where the time goes:
time: 130 us; the launch traced here: 129 us
  blocking collectives  83.5 us (64%)
  between operations  18 us (14%)
  matrix products  10.7 us (8%)
  starting transfers between devices  8.66 us (7%)
  local copies, waits for them, and re-layouts  5.17 us (4%)
  other arithmetic  2.17 us (2%)
    all_gather x1, blocking collectives, shards(): lax.all_gather(owned_rows, 'ctx', axis=0, tiled=True)  30.7 us
    all_gather x1, blocking collectives, shards(): lax.all_gather(precond, 'ctx', axis=1, tiled=True)  30.5 us
    unnamed x1, blocking collectives  18.9 us
    ppermute x2, starting transfers between devices, from_behind(): return lax.ppermute(block, axis, route)  8.66 us
    dot_general x1, matrix products, shards(): jnp.dot(doc_grads, inverse, precision=lax.Precision.HIGHEST, preferred_el...  4.29 us
    psum x1, blocking collectives, shards(): precond = lax.psum(partial_q, 'col').astype(jnp.bfloat16)  3.4 us
  transfers between devices with their start and end apart: 3, of which 1 were waited for; matrix products, arithmetic and copies ran while one was open for 7% of the time, Pallas kernels for 0%

commit v1 on v0

v1 whole, which is shorter than its diff:
```python
import jax
import jax.numpy as jnp
from jax import lax
from jax.sharding import PartitionSpec as P


def swap(block, axis, distance):
    size = lax.axis_size(axis)
    return lax.ppermute(block, axis, [(i, i ^ distance) for i in range(size)])


def gather_blocks(block, axis):
    index = lax.axis_index(axis)
    distance = 1
    while distance < lax.axis_size(axis):
        other = swap(block, axis, distance)
        upper = (index & distance) != 0
        block = jnp.where(
            upper, jnp.concatenate([other, block]), jnp.concatenate([block, other])
        )
        distance *= 2
    return block


def shards(activations, gradients, doc_ids, proj_in, proj_out, inverse, store_rows):
    left_part = jnp.dot(activations, proj_in, preferred_element_type=jnp.float32)
    right_part = jnp.dot(gradients, proj_out, preferred_element_type=jnp.float32)
    parts = jnp.concatenate([left_part, right_part], 1)
    both = parts + swap(parts, "col", 1)
    rank = proj_in.shape[1]
    proj_left, proj_right = both[:, :rank], both[:, rank:]
    half = rank // lax.axis_size("col")
    own_half = lax.dynamic_slice_in_dim(proj_left, lax.axis_index("col") * half, half, 1)
    first_doc = doc_ids[0]
    slot = doc_ids - first_doc
    onehot = (slot[:, None] == jnp.arange(3, dtype=jnp.int32)[None, :]).astype(jnp.float32)
    weighted = (onehot[:, :, None] * own_half[:, None, :]).reshape(own_half.shape[0], 3 * half)
    local = lax.dot_general(
        weighted,
        proj_right,
        (((0,), (0,)), ((), ())),
        precision=lax.Precision.HIGHEST,
        preferred_element_type=jnp.float32,
    ).reshape(3, half * rank)
    ctx = lax.axis_size("ctx")
    numbers = jnp.full((1, half * rank), first_doc.astype(jnp.float32))
    rows = jnp.concatenate([local, numbers])[None]
    gathered = gather_blocks(rows, "ctx")
    owners = gathered[:, 3, 0]
    doc_count = 3 * ctx // 2
    docs = jnp.arange(doc_count, dtype=jnp.int32).astype(jnp.float32)
    slots = jnp.arange(3, dtype=jnp.int32).astype(jnp.float32)
    pick = (owners[None, :, None] + slots[None, None, :] == docs[:, None, None]).astype(jnp.float32)
    doc_grads = lax.dot_general(
        pick.reshape(doc_count, ctx * 3),
        gathered[:, :3].reshape(ctx * 3, half * rank),
        (((1,), (0,)), ((), ())),
        precision=lax.Precision.HIGHEST,
        preferred_element_type=jnp.float32,
    )
    partial_q = jnp.dot(
        doc_grads, inverse, precision=lax.Precision.HIGHEST, preferred_element_type=jnp.float32
    )
    precond = (partial_q + swap(partial_q, "col", 1)).astype(jnp.bfloat16)
    whole = gather_blocks(precond[None], "ctx")
    whole = whole.transpose(1, 0, 2).reshape(doc_count, -1)
    return lax.dot_general(
        whole, store_rows, (((1,), (1,)), ((), ())), preferred_element_type=jnp.float32
    )


def solution(mesh):
    in_specs = (
        P(("groups", "ctx"), "col"),
        P(("groups", "ctx"), "col"),
        P(("groups", "ctx")),
        P("col", None),
        P("col", None),
        P("col", "ctx"),
        P(("groups", "ctx", "col"), None),
    )
    out_specs = P(None, ("groups", "ctx", "col"))
    return jax.shard_map(shards, mesh=mesh, in_specs=in_specs, out_specs=out_specs, check_vma=False)
```

time: 130 us -> 44.8 us (0.34)
  blocking collectives: 83.5 us -> 0 us
  waiting for transfers between devices: 1.03 us -> 20 us
  between operations: 18 us -> 0.82 us
  local copies, waits for them, and re-layouts: 5.17 us -> 0.58 us
  starting transfers between devices: 8.66 us -> 12.3 us
  matrix products: 10.7 us -> 9.14 us
    all_gather x2 -> x0, blocking collectives: 61.2 us -> none  [the longest x1 30.7 us: shards(): lax.all_gather(owned_rows, 'ctx', axis=0, tiled=True)]
    ppermute x2 -> x8, waiting for transfers between devices: 0.99 us -> 20 us  [swap(): return lax.ppermute(block, axis, [(i, i ^ distance) for i in range(size)])]
    unnamed x1 -> x0, blocking collectives: 18.9 us -> none
    ppermute x2 -> x8, starting transfers between devices: 8.66 us -> 12.3 us  [swap(): return lax.ppermute(block, axis, [(i, i ^ distance) for i in range(size)])]
    psum x1 -> x0, blocking collectives: 3.4 us -> none  [shards(): precond = lax.psum(partial_q, 'col').astype(jnp.bfloat16)]
    slice x6 -> x2, local copies, waits for them, and re-layouts: 2.26 us -> 0.12 us  [the longest x1 0.11 us: shards(): owners = gathered[:, 3, 0]]
  transfers between devices with their start and end apart: 3 -> 8, of which waited for: 1 -> 7; matrix products, arithmetic and copies ran while one was open for 7% -> 3% of each run, Pallas kernels for 0% -> 0%
where the time goes in v1:
time: 44.8 us; the launch traced here: 44.5 us
  waiting for transfers between devices  20 us (45%)
  starting transfers between devices  12.3 us (27%)
  matrix products  9.14 us (20%)
  other arithmetic  1.77 us (4%)
  between operations  0.82 us (2%)
  local copies, waits for them, and re-layouts  0.58 us (1%)
    ppermute x8, waiting for transfers between devices, swap(): return lax.ppermute(block, axis, [(i, i ^ distance) for i in range(size)])  20 us
    ppermute x8, starting transfers between devices, swap(): return lax.ppermute(block, axis, [(i, i ^ distance) for i in range(size)])  12.3 us
    dot_general x1, matrix products, shards(): jnp.dot(doc_grads, inverse, precision=lax.Precision.HIGHEST, preferred_el...  4.29 us
    dot_general x1, matrix products, shards(): jnp.dot(gradients, proj_out, preferred_element_type=jnp.float32)  1.92 us
    dot_general x1, matrix products, shards(): jnp.dot(activations, proj_in, preferred_element_type=jnp.float32)  1.54 us
    sub x1, other arithmetic, shards(): slot = doc_ids - first_doc  1.3 us
  transfers between devices with their start and end apart: 8, of which 7 were waited for; matrix products, arithmetic and copies ran while one was open for 3% of the time, Pallas kernels for 0%

profile of v1, /device:TPU:0, one launch (start us, length us, event | category | flops | bytes accessed | tf_op | source)
XLA Modules:
  0.0 44.5 jit_solution(7329151668759342247)
XLA Ops:
  0.0 0.0 copy-start
  0.0 1.5 %fusion.10 = f32[128,64]{0,1:T(8,128)S(1)} fusion(bf16[128,2048]{1,0:T(8,128)(2,1)} %param.7, bf16[2048,64]{0,1:T(8,128)(2,1)} %param.10), kind=kOutput, calls=%fused_computation.28 | convolution fusion | flops 33554432 | bytes 819200 | tf_op jit(solution)/shard_map/dot_general | solution.py:26
  1.5 0.2 copy-done
  1.7 1.9 %fusion.11 = f32[128,64]{0,1:T(8,128)S(1)} fusion(bf16[128,7168]{1,0:T(8,128)(2,1)S(1)} %copy-done, bf16[7168,64]{0,1:T(8,128)(2,1)} %param.11), kind=kOutput, calls=%fused_computation.29 | convolution fusion | flops 117440512 | bytes 2785280 | tf_op jit(solution)/shard_map/dot_general | solution.py:27
  3.7 0.0 copy-start.1
  3.7 0.6 %collective-permute-start = (f32[128,128]{0,1:T(8,128)S(1)}, f32[128,128]{0,1:T(8,128)S(1)}, u32[]{:S(2)}, u32[]{:S(2)}) collective-permute-start(f32[128,128]{0,1:T(8,128)S(1)} %pad_maximum_fusion), channel_id=1, source_target_pairs={{0,1},{1,0},{2,3},{3,2},{4,5},{5,4},{6,7},{7,6},{8,9},{9,8},{10,11... | collective-permute-start | bytes 196616 | tf_op jit(solution)/shard_map/ppermute | solution.py:9
  4.3 1.3 %broadcast_subtract_fusion = s32[128]{0:T(128)S(1)} fusion(s32[128]{0:T(128)} %param.9, s32[]{:T(128)} %bitcast.26), kind=kLoop, calls=%fused_computation.25 | loop fusion | flops 128 | bytes 1028 | tf_op jit(solution)/shard_map/sub | solution.py:35
  6.2 0.0 collective-permute-done
  6.3 0.2 fusion.2
  6.5 0.1 reshape.77
  6.6 2.6 %collective-permute-start.1 = (f32[1,4,2048]{2,0,1:T(1,128)S(1)}, f32[1,4,2048]{2,0,1:T(1,128)S(1)}, u32[]{:S(2)}, u32[]{:S(2)}) collective-permute-start(f32[1,4,2048]{2,0,1:T(1,128)S(1)} %copy.12), channel_id=1, source_target_pairs={{0,2},{2,0},{4,6},{6,4},{8,10},{10,8},{12,14},{14,12},{1,3},{3,1},... | collective-permute-start | bytes 98312 | tf_op jit(solution)/shard_map/ppermute | solution.py:9
  9.3 2.0 %collective-permute-done.1 = f32[1,4,2048]{2,0,1:T(1,128)S(1)} collective-permute-done((f32[1,4,2048]{2,0,1:T(1,128)S(1)}, f32[1,4,2048]{2,0,1:T(1,128)S(1)}, u32[]{:S(2)}, u32[]{:S(2)}) %collective-permute-start.1) | collective-permute-done | bytes 32800 | tf_op jit(solution)/shard_map/ppermute | solution.py:9
  11.3 0.1 maximum_select_fusion.3
  11.4 2.1 %collective-permute-start.2 = (f32[2,4,2048]{2,0,1:T(2,128)S(1)}, f32[2,4,2048]{2,0,1:T(2,128)S(1)}, u32[]{:S(2)}, u32[]{:S(2)}) collective-permute-start(f32[2,4,2048]{2,0,1:T(2,128)S(1)} %maximum_select_fusion.3), channel_id=1, source_target_pairs={{0,4},{2,6},{4,0},{6,2},{8,12},{10,14},{12,8},{14,10},{1,5},{3,7},... | collective-permute-start | bytes 196616 | tf_op jit(solution)/shard_map/ppermute | solution.py:9
  13.4 2.3 %collective-permute-done.2 = f32[2,4,2048]{2,0,1:T(2,128)S(1)} collective-permute-done((f32[2,4,2048]{2,0,1:T(2,128)S(1)}, f32[2,4,2048]{2,0,1:T(2,128)S(1)}, u32[]{:S(2)}, u32[]{:S(2)}) %collective-permute-start.2) | collective-permute-done | bytes 65568 | tf_op jit(solution)/shard_map/ppermute | solution.py:9
  15.7 0.1 maximum_select_fusion.1
  15.8 3.1 %collective-permute-start.3 = (f32[4,4,2048]{2,0,1:T(4,128)S(1)}, f32[4,4,2048]{2,0,1:T(4,128)S(1)}, u32[]{:S(2)}, u32[]{:S(2)}) collective-permute-start(f32[4,4,2048]{2,0,1:T(4,128)S(1)} %maximum_select_fusion.1), channel_id=1, source_target_pairs={{0,8},{2,10},{4,12},{6,14},{8,0},{10,2},{12,4},{14,6},{1,9},{3,11}... | collective-permute-start | bytes 393224 | tf_op jit(solution)/shard_map/ppermute | solution.py:9
  18.9 4.8 %collective-permute-done.3 = f32[4,4,2048]{2,0,1:T(4,128)S(1)} collective-permute-done((f32[4,4,2048]{2,0,1:T(4,128)S(1)}, f32[4,4,2048]{2,0,1:T(4,128)S(1)}, u32[]{:S(2)}, u32[]{:S(2)}) %collective-permute-start.3) | collective-permute-done | bytes 131104 | tf_op jit(solution)/shard_map/ppermute | solution.py:9
  23.7 0.1 maximum_select_fusion
  23.8 0.1 slice_reduce_fusion
  23.9 0.1 broadcast_add_fusion
  24.0 0.3 convolution_bitcast_fusion
  24.3 4.3 %fusion.12 = f32[12,512]{1,0:T(8,128)S(1)} fusion(f32[12,2048]{1,0:T(8,128)S(1)} %convolution_bitcast_fusion, f32[2048,512]{1,0:T(8,128)} %param.12), kind=kOutput, calls=%fused_computation.30 | convolution fusion | flops 150994944 | bytes 4317184 | tf_op jit(solution)/shard_map/dot_general | solution.py:61
  28.6 0.0 collective-permute-start.4
  28.6 1.2 %collective-permute-done.4 = f32[12,512]{1,0:T(8,128)S(1)} collective-permute-done((f32[12,512]{1,0:T(8,128)S(1)}, f32[12,512]{1,0:T(8,128)S(1)}, u32[]{:S(2)}, u32[]{:S(2)}) %collective-permute-start.4) | collective-permute-done | bytes 24608 | tf_op jit(solution)/shard_map/ppermute | solution.py:9
  29.8 1.4 %collective-permute-start.5 = (bf16[1,12,512]{2,1,0:T(8,128)(2,1)S(1)}, bf16[1,12,512]{2,1,0:T(8,128)(2,1)S(1)}, u32[]{:S(2)}, u32[]{:S(2)}) collective-permute-start(bf16[1,12,512]{2,1,0:T(8,128)(2,1)S(1)} %fusion.4), channel_id=1, source_target_pairs={{0,2},{2,0},{4,6},{6,4},{8,10},{10,8},{12,14},{14,12},{1,3},{3,1},... | collective-permute-start | bytes 36872 | tf_op jit(solution)/shard_map/ppermute | solution.py:9
  31.2 2.4 %collective-permute-done.5 = bf16[1,12,512]{2,1,0:T(8,128)(2,1)S(1)} collective-permute-done((bf16[1,12,512]{2,1,0:T(8,128)(2,1)S(1)}, bf16[1,12,512]{2,1,0:T(8,128)(2,1)S(1)}, u32[]{:S(2)}, u32[]{:S(2)}) %collective-permute-start.5) | collective-permute-done | bytes 12320 | tf_op jit(solution)/shard_map/ppermute | solution.py:9
  33.6 0.6 %collective-permute-start.6 = (bf16[2,12,512]{2,1,0:T(8,128)(2,1)S(1)}, bf16[2,12,512]{2,1,0:T(8,128)(2,1)S(1)}, u32[]{:S(2)}, u32[]{:S(2)}) collective-permute-start(bf16[2,12,512]{2,1,0:T(8,128)(2,1)S(1)} %maximum_select_fusion.5), channel_id=1, source_target_pairs={{0,4},{2,6},{4,0},{6,2},{8,12},{10,14},{12,8},{14,10},{1,5},{3,7},... | collective-permute-start | bytes 73736 | tf_op jit(solution)/shard_map/ppermute | solution.py:9
  34.2 3.4 %collective-permute-done.6 = bf16[2,12,512]{2,1,0:T(8,128)(2,1)S(1)} collective-permute-done((bf16[2,12,512]{2,1,0:T(8,128)(2,1)S(1)}, bf16[2,12,512]{2,1,0:T(8,128)(2,1)S(1)}, u32[]{:S(2)}, u32[]{:S(2)}) %collective-permute-start.6) | collective-permute-done | bytes 24608 | tf_op jit(solution)/shard_map/ppermute | solution.py:9
  37.6 2.0 %collective-permute-start.7 = (bf16[4,12,512]{2,1,0:T(8,128)(2,1)S(1)}, bf16[4,12,512]{2,1,0:T(8,128)(2,1)S(1)}, u32[]{:S(2)}, u32[]{:S(2)}) collective-permute-start(bf16[4,12,512]{2,1,0:T(8,128)(2,1)S(1)} %maximum_select_fusion.4), channel_id=1, source_target_pairs={{0,8},{2,10},{4,12},{6,14},{8,0},{10,2},{12,4},{14,6},{1,9},{3,11}... | collective-permute-start | bytes 147464 | tf_op jit(solution)/shard_map/ppermute | solution.py:9
  39.5 4.0 %collective-permute-done.7 = bf16[4,12,512]{2,1,0:T(8,128)(2,1)S(1)} collective-permute-done((bf16[4,12,512]{2,1,0:T(8,128)(2,1)S(1)}, bf16[4,12,512]{2,1,0:T(8,128)(2,1)S(1)}, u32[]{:S(2)}, u32[]{:S(2)}) %collective-permute-start.7) | collective-permute-done | bytes 49184 | tf_op jit(solution)/shard_map/ppermute | solution.py:9
  43.5 0.1 copy.15
  43.7 0.0 copy-done.1
  43.7 0.9 %fusion.13 = f32[12,64]{1,0:T(8,128)} fusion(bf16[12,4096]{1,0:T(8,128)(2,1)S(1)} %bitcast.24, bf16[64,4096]{1,0:T(8,128)(2,1)S(1)} %copy-done.1), kind=kOutput, calls=%fused_computation.31 | convolution fusion | flops 6291456 | bytes 625664 | tf_op jit(solution)/shard_map/dot_general | solution.py:67
  (16 shorter events, 0.2 us)
Async XLA Ops:
  0.0 1.7 %copy-start = (bf16[128,7168]{1,0:T(8,128)(2,1)S(1)}, bf16[128,7168]{1,0:T(8,128)(2,1)}, u32[]{:S(2)}) copy-start(bf16[128,7168]{1,0:T(8,128)(2,1)} %param.8) | copy-start | bytes 5505028
  3.7 40.0 %copy-start.1 = (bf16[64,4096]{1,0:T(8,128)(2,1)S(1)}, bf16[64,4096]{1,0:T(8,128)(2,1)}, u32[]{:S(2)}) copy-start(bf16[64,4096]{1,0:T(8,128)(2,1)} %param.13) | copy-start | bytes 1572868
  3.7 2.5 %collective-permute-start = (f32[128,128]{0,1:T(8,128)S(1)}, f32[128,128]{0,1:T(8,128)S(1)}, u32[]{:S(2)}, u32[]{:S(2)}) collective-permute-start(f32[128,128]{0,1:T(8,128)S(1)} %pad_maximum_fusion), channel_id=1, source_target_pairs={{0,1},{1,0},{2,3},{3,2},{4,5},{5,4},{6,7},{7,6},{8,9},{9,8},{10,11... | collective-permute-start | bytes 196616 | tf_op jit(solution)/shard_map/ppermute | solution.py:9
  6.6 4.6 %collective-permute-start.1 = (f32[1,4,2048]{2,0,1:T(1,128)S(1)}, f32[1,4,2048]{2,0,1:T(1,128)S(1)}, u32[]{:S(2)}, u32[]{:S(2)}) collective-permute-start(f32[1,4,2048]{2,0,1:T(1,128)S(1)} %copy.12), channel_id=1, source_target_pairs={{0,2},{2,0},{4,6},{6,4},{8,10},{10,8},{12,14},{14,12},{1,3},{3,1},... | collective-permute-start | bytes 98312 | tf_op jit(solution)/shard_map/ppermute | solution.py:9
  11.4 4.3 %collective-permute-start.2 = (f32[2,4,2048]{2,0,1:T(2,128)S(1)}, f32[2,4,2048]{2,0,1:T(2,128)S(1)}, u32[]{:S(2)}, u32[]{:S(2)}) collective-permute-start(f32[2,4,2048]{2,0,1:T(2,128)S(1)} %maximum_select_fusion.3), channel_id=1, source_target_pairs={{0,4},{2,6},{4,0},{6,2},{8,12},{10,14},{12,8},{14,10},{1,5},{3,7},... | collective-permute-start | bytes 196616 | tf_op jit(solution)/shard_map/ppermute | solution.py:9
  15.8 7.9 %collective-permute-start.3 = (f32[4,4,2048]{2,0,1:T(4,128)S(1)}, f32[4,4,2048]{2,0,1:T(4,128)S(1)}, u32[]{:S(2)}, u32[]{:S(2)}) collective-permute-start(f32[4,4,2048]{2,0,1:T(4,128)S(1)} %maximum_select_fusion.1), channel_id=1, source_target_pairs={{0,8},{2,10},{4,12},{6,14},{8,0},{10,2},{12,4},{14,6},{1,9},{3,11}... | collective-permute-start | bytes 393224 | tf_op jit(solution)/shard_map/ppermute | solution.py:9
  28.6 1.2 %collective-permute-start.4 = (f32[12,512]{1,0:T(8,128)S(1)}, f32[12,512]{1,0:T(8,128)S(1)}, u32[]{:S(2)}, u32[]{:S(2)}) collective-permute-start(f32[12,512]{1,0:T(8,128)S(1)} %fusion.12), channel_id=1, source_target_pairs={{0,1},{1,0},{2,3},{3,2},{4,5},{5,4},{6,7},{7,6},{8,9},{9,8},{10,11... | collective-permute-start | bytes 73736 | tf_op jit(solution)/shard_map/ppermute | solution.py:9
  29.8 3.7 %collective-permute-start.5 = (bf16[1,12,512]{2,1,0:T(8,128)(2,1)S(1)}, bf16[1,12,512]{2,1,0:T(8,128)(2,1)S(1)}, u32[]{:S(2)}, u32[]{:S(2)}) collective-permute-start(bf16[1,12,512]{2,1,0:T(8,128)(2,1)S(1)} %fusion.4), channel_id=1, source_target_pairs={{0,2},{2,0},{4,6},{6,4},{8,10},{10,8},{12,14},{14,12},{1,3},{3,1},... | collective-permute-start | bytes 36872 | tf_op jit(solution)/shard_map/ppermute | solution.py:9
  33.6 4.0 %collective-permute-start.6 = (bf16[2,12,512]{2,1,0:T(8,128)(2,1)S(1)}, bf16[2,12,512]{2,1,0:T(8,128)(2,1)S(1)}, u32[]{:S(2)}, u32[]{:S(2)}) collective-permute-start(bf16[2,12,512]{2,1,0:T(8,128)(2,1)S(1)} %maximum_select_fusion.5), channel_id=1, source_target_pairs={{0,4},{2,6},{4,0},{6,2},{8,12},{10,14},{12,8},{14,10},{1,5},{3,7},... | collective-permute-start | bytes 73736 | tf_op jit(solution)/shard_map/ppermute | solution.py:9
  37.6 5.9 %collective-permute-start.7 = (bf16[4,12,512]{2,1,0:T(8,128)(2,1)S(1)}, bf16[4,12,512]{2,1,0:T(8,128)(2,1)S(1)}, u32[]{:S(2)}, u32[]{:S(2)}) collective-permute-start(bf16[4,12,512]{2,1,0:T(8,128)(2,1)S(1)} %maximum_select_fusion.4), channel_id=1, source_target_pairs={{0,8},{2,10},{4,12},{6,14},{8,0},{10,2},{12,4},{14,6},{1,9},{3,11}... | collective-permute-start | bytes 147464 | tf_op jit(solution)/shard_map/ppermute | solution.py:9

commit v2 on v0

v2 whole, which is shorter than its diff:
```python
import functools

import jax
import jax.numpy as jnp
from jax import lax
from jax.experimental import pallas as pl
from jax.experimental.pallas import tpu as pltpu
from jax.sharding import PartitionSpec as P

SLOTS = 3
LANES = 128


def distances(axis):
    size = lax.axis_size(axis)
    return [size >> step for step in range(1, size.bit_length())]


def swap(block, distance, cross):
    ctx, col = lax.axis_size("ctx"), lax.axis_size("col")
    route = [
        (c * col + p, (c ^ distance) * col + (p ^ cross)) for c in range(ctx) for p in range(col)
    ]
    return lax.ppermute(block, ("ctx", "col"), route)


def ordered(own, other, distance):
    upper = (lax.axis_index("ctx") & distance) != 0
    return jnp.where(upper, jnp.concatenate([other, own]), jnp.concatenate([own, other]))


def position():
    index, place = lax.axis_index("ctx"), 0
    for step, distance in enumerate(distances("ctx")):
        place = place + jnp.where((index & distance) != 0, 1 << step, 0)
    return place


def project_kernel(chunks, ids_hbm, act_hbm, pin_hbm, grad_hbm, pout_hbm, out, mask, ids, act, pin, grad, pout, sems):
    depth = grad.shape[1] // chunks
    copies = [
        pltpu.make_async_copy(act_hbm, act, sems.at[0]),
        pltpu.make_async_copy(pin_hbm, pin, sems.at[1]),
    ]
    for n in range(chunks):
        part = pl.ds(n * depth, depth)
        copies.append(pltpu.make_async_copy(pout_hbm.at[:, part], pout.at[:, part], sems.at[2 + 2 * n]))
        copies.append(pltpu.make_async_copy(grad_hbm.at[:, part], grad.at[:, part], sems.at[3 + 2 * n]))
    copies.append(pltpu.make_async_copy(ids_hbm, ids, sems.at[2 + 2 * chunks]))
    for copy in copies:
        copy.start()
    rank = pin.shape[0]
    dims = (((1,), (1,)), ((), ()))
    copies[0].wait()
    copies[1].wait()
    out[:rank, :] = lax.dot_general(pin[...], act[...], dims, preferred_element_type=jnp.float32)
    total = None
    for n in range(chunks):
        copies[2 + 2 * n].wait()
        copies[3 + 2 * n].wait()
        part = pl.ds(n * depth, depth)
        term = lax.dot_general(pout[:, part], grad[:, part], dims, preferred_element_type=jnp.float32)
        total = term if total is None else total + term
    out[rank:, :] = total
    copies[-1].wait()
    first = ids[:, :1]
    rows = lax.broadcasted_iota(jnp.int32, mask.shape, 0)
    tokens = jnp.broadcast_to(ids[...], mask.shape)
    heads = jnp.broadcast_to(first, mask.shape)
    hit = (tokens - heads == rows).astype(jnp.float32)
    mask[...] = jnp.where(rows == mask.shape[0] - 1, heads.astype(jnp.float32), hit)


def project(activations, gradients, proj_in, proj_out, doc_ids):
    tokens, depth = gradients.shape
    rank = proj_in.shape[1]
    chunks = max(n for n in (4, 2, 1) if depth % (n * LANES) == 0)
    anywhere = pl.BlockSpec(memory_space=pl.ANY)
    vmem = pl.BlockSpec(memory_space=pltpu.VMEM)
    return pl.pallas_call(
        functools.partial(project_kernel, chunks),
        out_shape=(
            jax.ShapeDtypeStruct((2 * rank, tokens), jnp.float32),
            jax.ShapeDtypeStruct((8, tokens), jnp.float32),
        ),
        in_specs=[anywhere] * 5,
        out_specs=(vmem, vmem),
        scratch_shapes=[
            pltpu.VMEM((1, tokens), jnp.int32),
            pltpu.VMEM(activations.shape, jnp.bfloat16),
            pltpu.VMEM(proj_in.shape[::-1], jnp.bfloat16),
            pltpu.VMEM(gradients.shape, jnp.bfloat16),
            pltpu.VMEM(proj_out.shape[::-1], jnp.bfloat16),
            pltpu.SemaphoreType.DMA((3 + 2 * chunks,)),
        ],
    )(doc_ids.reshape(1, tokens), activations, proj_in.T, gradients, proj_out.T)


def split(array):
    high = lax.reduce_precision(array, 8, 7)
    return high.astype(jnp.bfloat16), (array - high).astype(jnp.bfloat16)


def shards(activations, gradients, doc_ids, proj_in, proj_out, inverse, store_rows):
    ctx = lax.axis_size("ctx")
    rank = proj_in.shape[1]
    half = rank // lax.axis_size("col")
    doc_count = SLOTS * ctx // 2
    inverse_high, inverse_low = split(inverse)

    part, mask = project(activations, gradients, proj_in, proj_out, doc_ids)
    both = part + swap(part, 0, 1)
    own_half = lax.dynamic_slice_in_dim(both, lax.axis_index("col") * half, half, 0)
    weighted = (mask[:SLOTS, None, :] * own_half[None]).reshape(SLOTS * half, -1)
    local = lax.dot_general(
        weighted,
        both[rank:],
        (((1,), (1,)), ((), ())),
        precision=lax.Precision.HIGHEST,
        preferred_element_type=jnp.float32,
    )
    blocks = local.reshape(-1, LANES)
    places = 8 * LANES
    place = jnp.arange(places, dtype=jnp.int32) - SLOTS * position()
    first = mask[-1, 0]
    numbers = jnp.where((place >= 0) & (place < SLOTS), first + place.astype(jnp.float32), 0.0)
    numbers = numbers.reshape(8, LANES)
    for distance in distances("ctx"):
        size = blocks.shape[0]
        other = swap(jnp.concatenate([blocks, numbers]), distance, 0)
        blocks = ordered(blocks, other[:size], distance)
        numbers = numbers + other[size:]
    if SLOTS * ctx <= LANES:
        numbers = numbers[0]
    numbers = numbers.reshape(-1)[: SLOTS * ctx]
    docs = jnp.arange(doc_count, dtype=jnp.int32).astype(jnp.float32)
    pick = (numbers[None, :] == docs[:, None]).astype(jnp.float32)
    pieces = blocks.reshape(SLOTS * ctx, half * rank)
    pieces_high, pieces_low = split(pieces)
    terms = jnp.dot(
        jnp.concatenate([pieces_high, pieces_low]), inverse_high, preferred_element_type=jnp.float32
    )
    small = jnp.dot(pieces_high, inverse_low, preferred_element_type=jnp.float32)
    terms = terms[: SLOTS * ctx] + (terms[SLOTS * ctx :] + small)
    partial_q = jnp.dot(
        pick, terms, precision=lax.Precision.HIGHEST, preferred_element_type=jnp.float32
    )
    precond = (partial_q + swap(partial_q, 0, 1)).astype(jnp.bfloat16)
    width = precond.shape[1]
    whole = precond.reshape(-1, min(width, LANES))
    for distance in distances("ctx"):
        whole = ordered(whole, swap(whole, distance, 1), distance)
    bits = len(distances("ctx"))
    whole = whole.reshape((2,) * bits + (doc_count, width))
    whole = whole.transpose((bits,) + tuple(range(bits))[::-1] + (bits + 1,)).reshape(doc_count, -1)
    return lax.dot_general(
        whole, store_rows, (((1,), (1,)), ((), ())), preferred_element_type=jnp.float32
    )


def solution(mesh):
    in_specs = (
        P(("groups", "ctx"), "col"),
        P(("groups", "ctx"), "col"),
        P(("groups", "ctx")),
        P("col", None),
        P("col", None),
        P("col", "ctx"),
        P(("groups", "ctx", "col"), None),
    )
    out_specs = P(None, ("groups", "ctx", "col"))
    return jax.shard_map(shards, mesh=mesh, in_specs=in_specs, out_specs=out_specs, check_vma=False)
```

time: 130 us -> 41.7 us (0.32)
  blocking collectives: 83.5 us -> 0 us
  between operations: 18 us -> 0.18 us
  waiting for transfers between devices: 1.03 us -> 13.6 us
  matrix products: 10.7 us -> 4.54 us
  starting transfers between devices: 8.66 us -> 13.8 us
  Pallas kernels: 0 us -> 3.5 us
  local copies, waits for them, and re-layouts: 5.17 us -> 2.91 us
    all_gather x2 -> x0, blocking collectives: 61.2 us -> none  [the longest x1 30.7 us: shards(): lax.all_gather(owned_rows, 'ctx', axis=0, tiled=True)]
    unnamed x1 -> x0, blocking collectives: 18.9 us -> none
    ppermute x2 -> x8, waiting for transfers between devices: 0.99 us -> 13.6 us  [swap(): return lax.ppermute(block, ('ctx', 'col'), route)]
    dot_general x5, matrix products: 10.7 us -> 4.54 us  [the longest x1 2.82 us: shards(): jnp.dot(jnp.concatenate([pieces_high, pieces_low]), inverse_high, preferr...]
    ppermute x2 -> x8, starting transfers between devices: 8.66 us -> 13.8 us  [swap(): return lax.ppermute(block, ('ctx', 'col'), route)]
    pallas_call x0 -> x1, Pallas kernels: none -> 3.5 us  [project(): pl.pallas_call(functools.partial(project_kernel, chunks), out_shape=(jax....]
    psum x1 -> x0, blocking collectives: 3.4 us -> none  [shards(): precond = lax.psum(partial_q, 'col').astype(jnp.bfloat16)]
    add x1 -> x4, other arithmetic: 0.01 us -> 2.11 us  [the longest x3 1.26 us: shards(): numbers = numbers + other[size:]]
  transfers between devices with their start and end apart: 3 -> 8, of which waited for: 1 -> 7; matrix products, arithmetic and copies ran while one was open for 7% -> 6% of each run, Pallas kernels for 0% -> 0%
where the time goes in v2:
time: 41.7 us; the launch traced here: 41.5 us
  starting transfers between devices  13.8 us (33%)
  waiting for transfers between devices  13.6 us (33%)
  matrix products  4.54 us (11%)
  Pallas kernels  3.5 us (8%)
  local copies, waits for them, and re-layouts  2.91 us (7%)
  other arithmetic  2.89 us (7%)
    ppermute x8, starting transfers between devices, swap(): return lax.ppermute(block, ('ctx', 'col'), route)  13.8 us
    ppermute x8, waiting for transfers between devices, swap(): return lax.ppermute(block, ('ctx', 'col'), route)  13.6 us
    pallas_call x1, Pallas kernels, project(): pl.pallas_call(functools.partial(project_kernel, chunks), out_shape=(jax....  3.5 us
    dot_general x1, matrix products, shards(): jnp.dot(jnp.concatenate([pieces_high, pieces_low]), inverse_high, preferr...  2.82 us
    add x3, other arithmetic, shards(): numbers = numbers + other[size:]  1.26 us
    slice x1, local copies, waits for them, and re-layouts, shards(): first = mask[-1, 0]  1.26 us
    dot_general x1, matrix products, shards(): lax.dot_general(whole, store_rows, (((1,), (1,)), ((), ())), preferred_el...  0.85 us
    add x1, other arithmetic, shards(): both = part + swap(part, 0, 1)  0.85 us
  transfers between devices with their start and end apart: 8, of which 7 were waited for; matrix products, arithmetic and copies ran while one was open for 6% of the time, Pallas kernels for 0%

profile of v2, /device:TPU:0, one launch (start us, length us, event | category | flops | bytes accessed | tf_op | source)
XLA Modules:
  0.0 41.5 jit_solution(1136450038700310640)
XLA Ops:
  0.0 0.0 copy-start
  0.0 3.5 %shard_map.73 = (f32[128,128]{1,0:T(8,128)}, f32[8,128]{1,0:T(8,128)}) custom-call(s32[1,128]{1,0:T(1,128)} %bitcast.17, bf16[128,2048]{1,0:T(8,128)(2,1)} %act_hbm.1, bf16[64,2048]{1,0:T(8,128)(2,1)} %bitcast.15, bf16[128,7168]{1,0:T(8,128)(2,1)} %grad_hbm.1, bf16[64,7168]{1,0:T(8,128)(2,1)} %bitcast.13), custom_call_target="tpu_custom_call" | custom-call | tf_op jit(solution)/shard_map/pallas_call | solution.py:80
  3.5 0.6 %collective-permute-start = (f32[128,128]{1,0:T(8,128)}, f32[128,128]{1,0:T(8,128)S(1)}, u32[]{:S(2)}, u32[]{:S(2)}) collective-permute-start(f32[128,128]{1,0:T(8,128)} %get-tuple-element.8), channel_id=1, source_target_pairs={{0,1},{1,0},{2,3},{3,2},{4,5},{5,4},{6,7},{7,6},{8,9},{9,8},{10,11... | collective-permute-start | bytes 196616 | tf_op jit(solution)/shard_map/ppermute | solution.py:24
  4.1 1.3 %slice.39 = f32[1,1]{1,0:T(1,128)} slice(f32[8,128]{1,0:T(8,128)} %get-tuple-element.7), slice={[7:8], [0:1]} | slice | bytes 8 | tf_op jit(solution)/shard_map/slice | solution.py:125
  5.3 0.7 %slice.40 = f32[3,128]{1,0:T(4,128)S(1)} slice(f32[8,128]{1,0:T(8,128)} %get-tuple-element.7), slice={[0:3], [0:128]} | slice | bytes 3072 | tf_op jit(solution)/shard_map/slice | solution.py:114
  6.0 0.6 %add_select_fusion = f32[8,128]{1,0:T(8,128)S(1)} fusion(f32[]{:T(128)} %bitcast.3, s32[]{:T(128)S(6)} %mul.23), kind=kLoop, calls=%fused_computation.32 | loop fusion | flops 9216 | bytes 4104 | tf_op jit(solution)/shard_map/jit(_where)/select_n | solution.py:126
  6.7 0.0 collective-permute-done
  6.7 0.8 %add.42 = f32[128,128]{1,0:T(8,128)S(1)} add(f32[128,128]{1,0:T(8,128)} %get-tuple-element.8, f32[128,128]{1,0:T(8,128)S(1)} %collective-permute-done) | non-fusion elementwise | flops 16384 | bytes 196608 | tf_op jit(solution)/shard_map/add | solution.py:112
  7.5 0.2 fusion.14
  7.7 0.1 reshape.37
  7.8 3.6 %collective-permute-start.1 = (f32[56,128]{1,0:T(8,128)S(1)}, f32[56,128]{1,0:T(8,128)S(1)}, u32[]{:S(2)}, u32[]{:S(2)}) collective-permute-start(f32[56,128]{1,0:T(8,128)S(1)} %pad_maximum_fusion.2), channel_id=1, source_target_pairs={{0,8},{1,9},{2,10},{3,11},{4,12},{5,13},{6,14},{7,15},{8,0},{9,1},... | collective-permute-start | bytes 86024 | tf_op jit(solution)/shard_map/ppermute | solution.py:24
  11.4 2.0 %collective-permute-done.1 = f32[56,128]{1,0:T(8,128)S(1)} collective-permute-done((f32[56,128]{1,0:T(8,128)S(1)}, f32[56,128]{1,0:T(8,128)S(1)}, u32[]{:S(2)}, u32[]{:S(2)}) %collective-permute-start.1) | collective-permute-done | bytes 28704 | tf_op jit(solution)/shard_map/ppermute | solution.py:24
  13.4 0.6 %slice_add_fusion.2 = f32[8,128]{1,0:T(8,128)S(1)} fusion(f32[56,128]{1,0:T(8,128)S(1)} %collective-permute-done.1, f32[]{:T(128)} %bitcast.3, s32[]{:T(128)S(6)} %mul.23), kind=kLoop, calls=%fused_computation.30 | loop fusion | flops 10240 | bytes 8200 | tf_op jit(solution)/shard_map/add | solution.py:132
  14.1 1.9 %collective-permute-start.2 = (f32[104,128]{1,0:T(8,128)S(1)}, f32[104,128]{1,0:T(8,128)S(1)}, u32[]{:S(2)}, u32[]{:S(2)}) collective-permute-start(f32[104,128]{1,0:T(8,128)S(1)} %pad_maximum_fusion.1), channel_id=1, source_target_pairs={{0,4},{1,5},{2,6},{3,7},{4,0},{5,1},{6,2},{7,3},{8,12},{9,13},{10,... | collective-permute-start | bytes 159752 | tf_op jit(solution)/shard_map/ppermute | solution.py:24
  15.9 2.3 %collective-permute-done.2 = f32[104,128]{1,0:T(8,128)S(1)} collective-permute-done((f32[104,128]{1,0:T(8,128)S(1)}, f32[104,128]{1,0:T(8,128)S(1)}, u32[]{:S(2)}, u32[]{:S(2)}) %collective-permute-start.2) | collective-permute-done | bytes 53280 | tf_op jit(solution)/shard_map/ppermute | solution.py:24
  18.3 0.6 %slice_add_fusion.1 = f32[8,128]{1,0:T(8,128)S(1)} fusion(f32[104,128]{1,0:T(8,128)S(1)} %collective-permute-done.2, f32[56,128]{1,0:T(8,128)S(1)} %collective-permute-done.1, f32[]{:T(128)} %bitcast.3, s32[]{:T(128)S(6)} %mul.23), kind=kLoop, calls=%fused_computation.29 | loop fusion | flops 11264 | bytes 12296 | tf_op jit(solution)/shard_map/add | solution.py:132
  18.9 1.8 %collective-permute-start.3 = (f32[200,128]{1,0:T(8,128)S(1)}, f32[200,128]{1,0:T(8,128)S(1)}, u32[]{:S(2)}, u32[]{:S(2)}) collective-permute-start(f32[200,128]{1,0:T(8,128)S(1)} %pad_maximum_fusion), channel_id=1, source_target_pairs={{0,2},{1,3},{2,0},{3,1},{4,6},{5,7},{6,4},{7,5},{8,10},{9,11},{10,... | collective-permute-start | bytes 307208 | tf_op jit(solution)/shard_map/ppermute | solution.py:24
  20.7 2.9 %collective-permute-done.3 = f32[200,128]{1,0:T(8,128)S(1)} collective-permute-done((f32[200,128]{1,0:T(8,128)S(1)}, f32[200,128]{1,0:T(8,128)S(1)}, u32[]{:S(2)}, u32[]{:S(2)}) %collective-permute-start.3) | collective-permute-done | bytes 102432 | tf_op jit(solution)/shard_map/ppermute | solution.py:24
  23.7 0.0 copy-start.1
  23.8 2.8 %fusion.3 = f32[48,512]{1,0:T(8,128)S(1)} fusion(f32[2048,512]{1,0:T(8,128)} %param.12, bf16[24,2048]{1,0:T(8,128)(2,1)S(1)} %get-tuple-element.9, bf16[24,2048]{1,0:T(8,128)(2,1)S(1)} %get-tuple-element.10), kind=kOutput, calls=%fused_computation.4 | convolution fusion | flops 103153664 | bytes 4489216 | tf_op jit(solution)/shard_map/dot_general | solution.py:140
  26.6 0.6 %copy-done.1 = f32[2048,512]{1,0:T(8,128)S(1)} copy-done((f32[2048,512]{1,0:T(8,128)S(1)}, f32[2048,512]{1,0:T(8,128)}, u32[]{:S(2)}) %copy-start.1) | copy-done | bytes 4194328
  27.2 0.5 %fusion.7 = f32[24,512]{1,0:T(8,128)S(1)} fusion(bf16[24,2048]{1,0:T(8,128)(2,1)S(1)} %get-tuple-element.10, f32[2048,512]{1,0:T(8,128)S(1)} %copy-done.1, f32[48,512]{1,0:T(8,128)S(1)} %fusion.3), kind=kOutput, calls=%fused_computation.6 | convolution fusion | flops 53501952 | bytes 4440064 | tf_op jit(solution)/shard_map/dot_general | solution.py:143
  27.7 0.2 fusion.16
  27.9 0.0 collective-permute-start.4
  27.9 1.2 %collective-permute-done.4 = f32[12,512]{1,0:T(8,128)S(1)} collective-permute-done((f32[12,512]{1,0:T(8,128)S(1)}, f32[12,512]{1,0:T(8,128)S(1)}, u32[]{:S(2)}, u32[]{:S(2)}) %collective-permute-start.4) | collective-permute-done | bytes 24608 | tf_op jit(solution)/shard_map/ppermute | solution.py:24
  29.1 2.6 %collective-permute-start.5 = (bf16[48,128]{1,0:T(8,128)(2,1)S(1)}, bf16[48,128]{1,0:T(8,128)(2,1)S(1)}, u32[]{:S(2)}, u32[]{:S(2)}) collective-permute-start(bf16[48,128]{1,0:T(8,128)(2,1)S(1)} %reshape.38), channel_id=1, source_target_pairs={{0,9},{1,8},{2,11},{3,10},{4,13},{5,12},{6,15},{7,14},{8,1},{9,0},... | collective-permute-start | bytes 36872 | tf_op jit(solution)/shard_map/ppermute | solution.py:24
  31.8 1.4 %collective-permute-done.5 = bf16[48,128]{1,0:T(8,128)(2,1)S(1)} collective-permute-done((bf16[48,128]{1,0:T(8,128)(2,1)S(1)}, bf16[48,128]{1,0:T(8,128)(2,1)S(1)}, u32[]{:S(2)}, u32[]{:S(2)}) %collective-permute-start.5) | collective-permute-done | bytes 12320 | tf_op jit(solution)/shard_map/ppermute | solution.py:24
  33.2 1.9 %collective-permute-start.6 = (bf16[96,128]{1,0:T(8,128)(2,1)S(1)}, bf16[96,128]{1,0:T(8,128)(2,1)S(1)}, u32[]{:S(2)}, u32[]{:S(2)}) collective-permute-start(bf16[96,128]{1,0:T(8,128)(2,1)S(1)} %maximum_select_fusion.5), channel_id=1, source_target_pairs={{0,5},{1,4},{2,7},{3,6},{4,1},{5,0},{6,3},{7,2},{8,13},{9,12},{10,... | collective-permute-start | bytes 73736 | tf_op jit(solution)/shard_map/ppermute | solution.py:24
  35.1 1.5 %collective-permute-done.6 = bf16[96,128]{1,0:T(8,128)(2,1)S(1)} collective-permute-done((bf16[96,128]{1,0:T(8,128)(2,1)S(1)}, bf16[96,128]{1,0:T(8,128)(2,1)S(1)}, u32[]{:S(2)}, u32[]{:S(2)}) %collective-permute-start.6) | collective-permute-done | bytes 24608 | tf_op jit(solution)/shard_map/ppermute | solution.py:24
  36.6 1.5 %collective-permute-start.7 = (bf16[192,128]{1,0:T(8,128)(2,1)S(1)}, bf16[192,128]{1,0:T(8,128)(2,1)S(1)}, u32[]{:S(2)}, u32[]{:S(2)}) collective-permute-start(bf16[192,128]{1,0:T(8,128)(2,1)S(1)} %maximum_select_fusion.4), channel_id=1, source_target_pairs={{0,3},{1,2},{2,1},{3,0},{4,7},{5,6},{6,5},{7,4},{8,11},{9,10},{10,... | collective-permute-start | bytes 147464 | tf_op jit(solution)/shard_map/ppermute | solution.py:24
  38.1 2.2 %collective-permute-done.7 = bf16[192,128]{1,0:T(8,128)(2,1)S(1)} collective-permute-done((bf16[192,128]{1,0:T(8,128)(2,1)S(1)}, bf16[192,128]{1,0:T(8,128)(2,1)S(1)}, u32[]{:S(2)}, u32[]{:S(2)}) %collective-permute-start.7) | collective-permute-done | bytes 49184 | tf_op jit(solution)/shard_map/ppermute | solution.py:24
  40.4 0.1 select_n.83
  40.4 0.1 copy.9
  40.6 0.1 reshape.39
  40.6 0.0 copy-done
  40.6 0.9 %fusion.24 = f32[12,64]{1,0:T(8,128)} fusion(bf16[12,4096]{1,0:T(8,128)(2,1)S(1)} %reshape.39, bf16[64,4096]{1,0:T(8,128)(2,1)S(1)} %copy-done), kind=kOutput, calls=%fused_computation.42 | convolution fusion | flops 6291456 | bytes 625664 | tf_op jit(solution)/shard_map/dot_general | solution.py:156
  (21 shorter events, 0.2 us)
Async XLA Ops:
  0.0 40.6 %copy-start = (bf16[64,4096]{1,0:T(8,128)(2,1)S(1)}, bf16[64,4096]{1,0:T(8,128)(2,1)}, u32[]{:S(2)}) copy-start(bf16[64,4096]{1,0:T(8,128)(2,1)} %param.13) | copy-start | bytes 1572868
  3.5 3.1 %collective-permute-start = (f32[128,128]{1,0:T(8,128)}, f32[128,128]{1,0:T(8,128)S(1)}, u32[]{:S(2)}, u32[]{:S(2)}) collective-permute-start(f32[128,128]{1,0:T(8,128)} %get-tuple-element.8), channel_id=1, source_target_pairs={{0,1},{1,0},{2,3},{3,2},{4,5},{5,4},{6,7},{7,6},{8,9},{9,8},{10,11... | collective-permute-start | bytes 196616 | tf_op jit(solution)/shard_map/ppermute | solution.py:24
  7.8 5.6 %collective-permute-start.1 = (f32[56,128]{1,0:T(8,128)S(1)}, f32[56,128]{1,0:T(8,128)S(1)}, u32[]{:S(2)}, u32[]{:S(2)}) collective-permute-start(f32[56,128]{1,0:T(8,128)S(1)} %pad_maximum_fusion.2), channel_id=1, source_target_pairs={{0,8},{1,9},{2,10},{3,11},{4,12},{5,13},{6,14},{7,15},{8,0},{9,1},... | collective-permute-start | bytes 86024 | tf_op jit(solution)/shard_map/ppermute | solution.py:24
  14.1 4.2 %collective-permute-start.2 = (f32[104,128]{1,0:T(8,128)S(1)}, f32[104,128]{1,0:T(8,128)S(1)}, u32[]{:S(2)}, u32[]{:S(2)}) collective-permute-start(f32[104,128]{1,0:T(8,128)S(1)} %pad_maximum_fusion.1), channel_id=1, source_target_pairs={{0,4},{1,5},{2,6},{3,7},{4,0},{5,1},{6,2},{7,3},{8,12},{9,13},{10,... | collective-permute-start | bytes 159752 | tf_op jit(solution)/shard_map/ppermute | solution.py:24
  18.9 4.7 %collective-permute-start.3 = (f32[200,128]{1,0:T(8,128)S(1)}, f32[200,128]{1,0:T(8,128)S(1)}, u32[]{:S(2)}, u32[]{:S(2)}) collective-permute-start(f32[200,128]{1,0:T(8,128)S(1)} %pad_maximum_fusion), channel_id=1, source_target_pairs={{0,2},{1,3},{2,0},{3,1},{4,6},{5,7},{6,4},{7,5},{8,10},{9,11},{10,... | collective-permute-start | bytes 307208 | tf_op jit(solution)/shard_map/ppermute | solution.py:24
  23.7 3.5 %copy-start.1 = (f32[2048,512]{1,0:T(8,128)S(1)}, f32[2048,512]{1,0:T(8,128)}, u32[]{:S(2)}) copy-start(f32[2048,512]{1,0:T(8,128)} %param.12) | copy-start | bytes 12582916
  27.9 1.3 %collective-permute-start.4 = (f32[12,512]{1,0:T(8,128)S(1)}, f32[12,512]{1,0:T(8,128)S(1)}, u32[]{:S(2)}, u32[]{:S(2)}) collective-permute-start(f32[12,512]{1,0:T(8,128)S(1)} %fusion.16), channel_id=1, source_target_pairs={{0,1},{1,0},{2,3},{3,2},{4,5},{5,4},{6,7},{7,6},{8,9},{9,8},{10,11... | collective-permute-start | bytes 73736 | tf_op jit(solution)/shard_map/ppermute | solution.py:24
  29.1 4.1 %collective-permute-start.5 = (bf16[48,128]{1,0:T(8,128)(2,1)S(1)}, bf16[48,128]{1,0:T(8,128)(2,1)S(1)}, u32[]{:S(2)}, u32[]{:S(2)}) collective-permute-start(bf16[48,128]{1,0:T(8,128)(2,1)S(1)} %reshape.38), channel_id=1, source_target_pairs={{0,9},{1,8},{2,11},{3,10},{4,13},{5,12},{6,15},{7,14},{8,1},{9,0},... | collective-permute-start | bytes 36872 | tf_op jit(solution)/shard_map/ppermute | solution.py:24
  33.2 3.4 %collective-permute-start.6 = (bf16[96,128]{1,0:T(8,128)(2,1)S(1)}, bf16[96,128]{1,0:T(8,128)(2,1)S(1)}, u32[]{:S(2)}, u32[]{:S(2)}) collective-permute-start(bf16[96,128]{1,0:T(8,128)(2,1)S(1)} %maximum_select_fusion.5), channel_id=1, source_target_pairs={{0,5},{1,4},{2,7},{3,6},{4,1},{5,0},{6,3},{7,2},{8,13},{9,12},{10,... | collective-permute-start | bytes 73736 | tf_op jit(solution)/shard_map/ppermute | solution.py:24
  36.6 3.7 %collective-permute-start.7 = (bf16[192,128]{1,0:T(8,128)(2,1)S(1)}, bf16[192,128]{1,0:T(8,128)(2,1)S(1)}, u32[]{:S(2)}, u32[]{:S(2)}) collective-permute-start(bf16[192,128]{1,0:T(8,128)(2,1)S(1)} %maximum_select_fusion.4), channel_id=1, source_target_pairs={{0,3},{1,2},{2,1},{3,0},{4,7},{5,6},{6,5},{7,4},{8,11},{9,10},{10,... | collective-permute-start | bytes 147464 | tf_op jit(solution)/shard_map/ppermute | solution.py:24

commit v3 on v2

--- a/solution.py
+++ b/solution.py
@@ -9,6 +9,7 @@
 
 SLOTS = 3
 LANES = 128
+VMEM_LIMIT = 16 << 20
 
 
 def distances(axis):
@@ -31,12 +32,40 @@
 
 def position():
     index, place = lax.axis_index("ctx"), 0
-    for step, distance in enumerate(distances("ctx")):
+    for step, distance in enumerate(distances("ctx")[:-1]):
         place = place + jnp.where((index & distance) != 0, 1 << step, 0)
     return place
 
 
-def project_kernel(chunks, ids_hbm, act_hbm, pin_hbm, grad_hbm, pout_hbm, out, mask, ids, act, pin, grad, pout, sems):
+def kept(space, *arrays):
+    return [pltpu.with_memory_space_constraint(array, space) for array in arrays]
+
+
+def fetch_kernel(pieces, array, after, out, sems):
+    rows = out.shape[0] // pieces
+    copies = [
+        pltpu.make_async_copy(array.at[pl.ds(n * rows, rows), :], out.at[pl.ds(n * rows, rows), :], sems.at[n])
+        for n in range(pieces)
+    ]
+    for copy in copies:
+        copy.start()
+    for copy in copies:
+        copy.wait()
+
+
+def fetch(array, after):
+    pieces = 4
+    return pl.pallas_call(
+        functools.partial(fetch_kernel, pieces),
+        out_shape=pltpu.VMEM(array.shape, array.dtype),
+        in_specs=[pl.BlockSpec(memory_space=pltpu.HBM), pl.BlockSpec(memory_space=pltpu.VMEM)],
+        out_specs=pl.BlockSpec(memory_space=pltpu.VMEM),
+        scratch_shapes=[pltpu.SemaphoreType.DMA((pieces,))],
+        compiler_params=pltpu.CompilerParams(vmem_limit_bytes=VMEM_LIMIT),
+    )(*kept(pltpu.HBM, array), *kept(pltpu.VMEM, after))
+
+
+def project_kernel(chunks, ids_hbm, act_hbm, pin_hbm, grad_hbm, pout_hbm, out, mask, numbers, ids, act, pin, grad, pout, sems):
     depth = grad.shape[1] // chunks
     copies = [
         pltpu.make_async_copy(act_hbm, act, sems.at[0]),
@@ -63,28 +92,32 @@
         total = term if total is None else total + term
     out[rank:, :] = total
     copies[-1].wait()
-    first = ids[:, :1]
     rows = lax.broadcasted_iota(jnp.int32, mask.shape, 0)
-    tokens = jnp.broadcast_to(ids[...], mask.shape)
-    heads = jnp.broadcast_to(first, mask.shape)
-    hit = (tokens - heads == rows).astype(jnp.float32)
-    mask[...] = jnp.where(rows == mask.shape[0] - 1, heads.astype(jnp.float32), hit)
+    first = jnp.broadcast_to(ids[:, :1], mask.shape)
+    mask[...] = (jnp.broadcast_to(ids[...], mask.shape) - first == rows).astype(jnp.float32)
+    shape = numbers.shape
+    place = lax.broadcasted_iota(jnp.int32, shape, 0) * LANES + lax.broadcasted_iota(jnp.int32, shape, 1)
+    place = place - SLOTS * position()
+    owned = (place >= 0) & (place < SLOTS)
+    first = jnp.broadcast_to(ids[:, :1], shape)
+    numbers[...] = jnp.where(owned, first + place, 0).astype(jnp.float32)
 
 
 def project(activations, gradients, proj_in, proj_out, doc_ids):
     tokens, depth = gradients.shape
     rank = proj_in.shape[1]
     chunks = max(n for n in (4, 2, 1) if depth % (n * LANES) == 0)
-    anywhere = pl.BlockSpec(memory_space=pl.ANY)
+    hbm = pl.BlockSpec(memory_space=pltpu.HBM)
     vmem = pl.BlockSpec(memory_space=pltpu.VMEM)
     return pl.pallas_call(
         functools.partial(project_kernel, chunks),
         out_shape=(
-            jax.ShapeDtypeStruct((2 * rank, tokens), jnp.float32),
-            jax.ShapeDtypeStruct((8, tokens), jnp.float32),
+            pltpu.VMEM((2 * rank, tokens), jnp.float32),
+            pltpu.VMEM((8, tokens), jnp.float32),
+            pltpu.VMEM((8, LANES), jnp.float32),
         ),
-        in_specs=[anywhere] * 5,
-        out_specs=(vmem, vmem),
+        in_specs=[hbm] * 5,
+        out_specs=(vmem, vmem, vmem),
         scratch_shapes=[
             pltpu.VMEM((1, tokens), jnp.int32),
             pltpu.VMEM(activations.shape, jnp.bfloat16),
@@ -93,12 +126,66 @@
             pltpu.VMEM(proj_out.shape[::-1], jnp.bfloat16),
             pltpu.SemaphoreType.DMA((3 + 2 * chunks,)),
         ],
-    )(doc_ids.reshape(1, tokens), activations, proj_in.T, gradients, proj_out.T)
+        compiler_params=pltpu.CompilerParams(vmem_limit_bytes=VMEM_LIMIT),
+    )(*kept(pltpu.HBM, doc_ids.reshape(1, tokens), activations, proj_in.T, gradients, proj_out.T))
 
 
 def split(array):
-    high = lax.reduce_precision(array, 8, 7)
-    return high.astype(jnp.bfloat16), (array - high).astype(jnp.bfloat16)
+    high = array.astype(jnp.bfloat16)
+    return high, (array - high.astype(jnp.float32)).astype(jnp.bfloat16)
+
+
+def precondition_kernel(own, other, inverse, out, pieces):
+    depth = inverse.shape[0]
+    size = own.shape[0] - 8
+    count = size * LANES // depth
+    room = pieces.shape[0] // 2
+    pieces[...] = jnp.zeros_like(pieces)
+    for k in range(depth // LANES):
+        for n, part in enumerate((own, other)):
+            pieces[pl.ds(n * room, count), pl.ds(k * LANES, LANES)] = part[
+                pl.ds(k, count, stride=depth // LANES), :
+            ]
+    step = 2 * LANES if depth % (2 * LANES) == 0 else LANES
+    total = None
+    for n in range(depth // step):
+        at = pl.ds(n * step, step)
+        high, low = split(pieces[:, at])
+        weights_high, weights_low = split(inverse[at, :])
+        first = jnp.dot(
+            jnp.concatenate([high, low]), weights_high, preferred_element_type=jnp.float32
+        )
+        second = jnp.dot(high, weights_low, preferred_element_type=jnp.float32)
+        term = first[: 2 * room] + (first[2 * room :] + second)
+        total = term if total is None else total + term
+    docs = lax.broadcasted_iota(jnp.int32, (out.shape[0], count), 0).astype(jnp.float32)
+    result = None
+    for n, part in enumerate((own, other)):
+        lanes = jnp.concatenate(
+            [part[size + r : size + r + 1, :] for r in range(pl.cdiv(count, LANES))], 1
+        )[:, :count]
+        pick = (jnp.broadcast_to(lanes, docs.shape) == docs).astype(jnp.float32)
+        term = jnp.dot(
+            pick,
+            total[n * room : n * room + count],
+            precision=lax.Precision.HIGHEST,
+            preferred_element_type=jnp.float32,
+        )
+        result = term if result is None else result + term
+    out[...] = result
+
+
+def precondition(own, other, inverse, doc_count):
+    vmem = pl.BlockSpec(memory_space=pltpu.VMEM)
+    count = (own.shape[0] - 8) * LANES // inverse.shape[0]
+    return pl.pallas_call(
+        precondition_kernel,
+        out_shape=pltpu.VMEM((doc_count, inverse.shape[1]), jnp.float32),
+        in_specs=[vmem] * 3,
+        out_specs=vmem,
+        scratch_shapes=[pltpu.VMEM((2 * pl.cdiv(count, 8) * 8, inverse.shape[0]), jnp.float32)],
+        compiler_params=pltpu.CompilerParams(vmem_limit_bytes=VMEM_LIMIT),
+    )(*kept(pltpu.VMEM, own, other, inverse))
 
 
 def shards(activations, gradients, doc_ids, proj_in, proj_out, inverse, store_rows):
@@ -106,9 +193,7 @@
     rank = proj_in.shape[1]
     half = rank // lax.axis_size("col")
     doc_count = SLOTS * ctx // 2
-    inverse_high, inverse_low = split(inverse)
-
-    part, mask = project(activations, gradients, proj_in, proj_out, doc_ids)
+    part, mask, numbers = project(activations, gradients, proj_in, proj_out, doc_ids)
     both = part + swap(part, 0, 1)
     own_half = lax.dynamic_slice_in_dim(both, lax.axis_index("col") * half, half, 0)
     weighted = (mask[:SLOTS, None, :] * own_half[None]).reshape(SLOTS * half, -1)
@@ -120,31 +205,16 @@
         preferred_element_type=jnp.float32,
     )
     blocks = local.reshape(-1, LANES)
-    places = 8 * LANES
-    place = jnp.arange(places, dtype=jnp.int32) - SLOTS * position()
-    first = mask[-1, 0]
-    numbers = jnp.where((place >= 0) & (place < SLOTS), first + place.astype(jnp.float32), 0.0)
-    numbers = numbers.reshape(8, LANES)
-    for distance in distances("ctx"):
-        size = blocks.shape[0]
-        other = swap(jnp.concatenate([blocks, numbers]), distance, 0)
-        blocks = ordered(blocks, other[:size], distance)
-        numbers = numbers + other[size:]
-    if SLOTS * ctx <= LANES:
-        numbers = numbers[0]
-    numbers = numbers.reshape(-1)[: SLOTS * ctx]
-    docs = jnp.arange(doc_count, dtype=jnp.int32).astype(jnp.float32)
-    pick = (numbers[None, :] == docs[:, None]).astype(jnp.float32)
-    pieces = blocks.reshape(SLOTS * ctx, half * rank)
-    pieces_high, pieces_low = split(pieces)
-    terms = jnp.dot(
-        jnp.concatenate([pieces_high, pieces_low]), inverse_high, preferred_element_type=jnp.float32
-    )
-    small = jnp.dot(pieces_high, inverse_low, preferred_element_type=jnp.float32)
-    terms = terms[: SLOTS * ctx] + (terms[SLOTS * ctx :] + small)
-    partial_q = jnp.dot(
-        pick, terms, precision=lax.Precision.HIGHEST, preferred_element_type=jnp.float32
-    )
+    payload = jnp.concatenate([blocks, numbers])
+    for distance in distances("ctx")[:-1]:
+        size = payload.shape[0] - 8
+        other = swap(payload, distance, 0)
+        blocks = ordered(payload[:size], other[:size], distance)
+        payload = jnp.concatenate([blocks, payload[size:] + other[size:]])
+    other = swap(payload, distances("ctx")[-1], 0)
+    inside = fetch(inverse, payload)
+    other, inside = lax.optimization_barrier((other, inside))
+    partial_q = precondition(payload, other, inside, doc_count)
     precond = (partial_q + swap(partial_q, 0, 1)).astype(jnp.bfloat16)
     width = precond.shape[1]
     whole = precond.reshape(-1, min(width, LANES))

time: 41.7 us -> 34.4 us (0.82)
  matrix products: 4.54 us -> 1.05 us
  Pallas kernels: 3.5 us -> 6.3 us
  other arithmetic: 2.89 us -> 0.12 us
  local copies, waits for them, and re-layouts: 2.91 us -> 0.34 us
  waiting for transfers between devices: 13.6 us -> 11.4 us
  starting transfers between devices: 13.8 us -> 14.9 us
    dot_general x3 -> x0, matrix products: 3.5 us -> none  [the longest x1 2.82 us: shards(): jnp.dot(jnp.concatenate([pieces_high, pieces_low]), inverse_high, preferr...]
    pallas_call x1 -> x3, Pallas kernels: 3.5 us -> 6.3 us  [the longest x1 2.91 us: project(): pl.pallas_call(functools.partial(project_kernel, chunks), out_shape=(pltp...]
    ppermute x8, waiting for transfers between devices: 13.6 us -> 11.4 us  [swap(): return lax.ppermute(block, ('ctx', 'col'), route)]
    slice x4 -> x2, local copies, waits for them, and re-layouts: 1.27 us -> 0.01 us  [shards(): blocks = ordered(payload[:size], other[:size], distance)]
    add x3 -> x2, other arithmetic: 1.26 us -> 0.01 us  [shards(): payload = jnp.concatenate([blocks, payload[size:] + other[size:]])]
    ppermute x8, starting transfers between devices: 13.8 us -> 14.9 us  [swap(): return lax.ppermute(block, ('ctx', 'col'), route)]
    add x1, other arithmetic: 0.85 us -> 0.01 us  [shards(): both = part + swap(part, 0, 1)]
    slice x1, local copies, waits for them, and re-layouts: 0.69 us -> 0.01 us  [shards(): mask[:SLOTS, None, :] * own_half[None]]
  transfers between devices with their start and end apart: 8 -> 8, of which waited for: 7 -> 8; matrix products, arithmetic and copies ran while one was open for 6% -> 0% of each run, Pallas kernels for 0% -> 6%
where the time goes in v3:
time: 34.4 us; the launch traced here: 34.3 us
  starting transfers between devices  14.9 us (43%)
  waiting for transfers between devices  11.4 us (33%)
  Pallas kernels  6.3 us (18%)
  matrix products  1.05 us (3%)
    ppermute x8, starting transfers between devices, swap(): return lax.ppermute(block, ('ctx', 'col'), route)  14.9 us
    ppermute x8, waiting for transfers between devices, swap(): return lax.ppermute(block, ('ctx', 'col'), route)  11.4 us
    pallas_call x1, Pallas kernels, project(): pl.pallas_call(functools.partial(project_kernel, chunks), out_shape=(pltp...  2.91 us
    pallas_call x1, Pallas kernels, fetch(): pl.pallas_call(functools.partial(fetch_kernel, pieces), out_shape=pltpu.V...  2.2 us
    pallas_call x1, Pallas kernels, precondition(): pl.pallas_call(precondition_kernel, out_shape=pltpu.VMEM((doc_count, inve...  1.19 us
    dot_general x1, matrix products, shards(): lax.dot_general(whole, store_rows, (((1,), (1,)), ((), ())), preferred_el...  0.85 us
  transfers between devices with their start and end apart: 8, of which 8 were waited for; matrix products, arithmetic and copies ran while one was open for 0% of the time, Pallas kernels for 6%

profile of v3, /device:TPU:0, one launch (start us, length us, event | category | flops | bytes accessed | tf_op | source)
XLA Modules:
  0.0 34.3 jit_solution(6921765337278793421)
XLA Ops:
  0.0 0.0 copy-start
  0.0 2.9 %shard_map.73 = (f32[128,128]{1,0:T(8,128)S(1)}, f32[8,128]{1,0:T(8,128)S(1)}, f32[8,128]{1,0:T(8,128)S(1)}) custom-call(s32[1,128]{1,0:T(1,128)} %bitcast.12, bf16[128,2048]{1,0:T(8,128)(2,1)} %act_hbm.1, bf16[64,2048]{1,0:T(8,128)(2,1)} %bitcast.10, bf16[128,7168]{1,0:T(8,128)(2,1)} %grad_hbm.1, bf16[64,7168]{1,0:T(8,128)(2,1)} %bitcast.8), custom_call_target="tpu_custom_call" | custom-call | tf_op jit(solution)/shard_map/pallas_call | solution.py:112
  2.9 0.6 %collective-permute-start = (f32[128,128]{1,0:T(8,128)S(1)}, f32[128,128]{1,0:T(8,128)S(1)}, u32[]{:S(2)}, u32[]{:S(2)}) collective-permute-start(f32[128,128]{1,0:T(8,128)S(1)} %get-tuple-element.11), channel_id=1, source_target_pairs={{0,1},{1,0},{2,3},{3,2},{4,5},{5,4},{6,7},{7,6},{8,9},{9,8},{10,11... | collective-permute-start | bytes 196616 | tf_op jit(solution)/shard_map/ppermute | solution.py:25
  3.5 0.9 %collective-permute-done = f32[128,128]{1,0:T(8,128)S(1)} collective-permute-done((f32[128,128]{1,0:T(8,128)S(1)}, f32[128,128]{1,0:T(8,128)S(1)}, u32[]{:S(2)}, u32[]{:S(2)}) %collective-permute-start) | collective-permute-done | bytes 65568 | tf_op jit(solution)/shard_map/ppermute | solution.py:25
  4.4 0.2 fusion
  4.6 0.1 reshape.24
  4.7 3.9 %collective-permute-start.1 = (f32[56,128]{1,0:T(8,128)S(1)}, f32[56,128]{1,0:T(8,128)S(1)}, u32[]{:S(2)}, u32[]{:S(2)}) collective-permute-start(f32[56,128]{1,0:T(8,128)S(1)} %pad_maximum_fusion.2), channel_id=1, source_target_pairs={{0,8},{1,9},{2,10},{3,11},{4,12},{5,13},{6,14},{7,15},{8,0},{9,1},... | collective-permute-start | bytes 86024 | tf_op jit(solution)/shard_map/ppermute | solution.py:25
  8.7 1.9 %collective-permute-done.1 = f32[56,128]{1,0:T(8,128)S(1)} collective-permute-done((f32[56,128]{1,0:T(8,128)S(1)}, f32[56,128]{1,0:T(8,128)S(1)}, u32[]{:S(2)}, u32[]{:S(2)}) %collective-permute-start.1) | collective-permute-done | bytes 28704 | tf_op jit(solution)/shard_map/ppermute | solution.py:25
  10.5 2.0 %collective-permute-start.2 = (f32[104,128]{1,0:T(8,128)S(1)}, f32[104,128]{1,0:T(8,128)S(1)}, u32[]{:S(2)}, u32[]{:S(2)}) collective-permute-start(f32[104,128]{1,0:T(8,128)S(1)} %pad_maximum_fusion.1), channel_id=1, source_target_pairs={{0,4},{1,5},{2,6},{3,7},{4,0},{5,1},{6,2},{7,3},{8,12},{9,13},{10,... | collective-permute-start | bytes 159752 | tf_op jit(solution)/shard_map/ppermute | solution.py:25
  12.5 2.2 %collective-permute-done.2 = f32[104,128]{1,0:T(8,128)S(1)} collective-permute-done((f32[104,128]{1,0:T(8,128)S(1)}, f32[104,128]{1,0:T(8,128)S(1)}, u32[]{:S(2)}, u32[]{:S(2)}) %collective-permute-start.2) | collective-permute-done | bytes 53280 | tf_op jit(solution)/shard_map/ppermute | solution.py:25
  14.8 2.2 %collective-permute-start.3 = (f32[200,128]{1,0:T(8,128)S(1)}, f32[200,128]{1,0:T(8,128)S(1)}, u32[]{:S(2)}, u32[]{:S(2)}) collective-permute-start(f32[200,128]{1,0:T(8,128)S(1)} %pad_maximum_fusion.after.own), channel_id=1, source_target_pairs={{0,2},{1,3},{2,0},{3,1},{4,6},{5,7},{6,4},{7,5},{8,10},{9,11},{10,... | collective-permute-start | bytes 307208 | tf_op jit(solution)/shard_map/ppermute | solution.py:25
  17.0 2.2 %shard_map.74.inverse = f32[2048,512]{1,0:T(8,128)S(1)} custom-call(f32[2048,512]{1,0:T(8,128)} %array.1, f32[200,128]{1,0:T(8,128)S(1)} %pad_maximum_fusion.after.own), custom_call_target="tpu_custom_call" | custom-call | tf_op jit(solution)/shard_map/pallas_call | solution.py:58
  19.2 0.4 %collective-permute-done.3.other = f32[200,128]{1,0:T(8,128)S(1)} collective-permute-done((f32[200,128]{1,0:T(8,128)S(1)}, f32[200,128]{1,0:T(8,128)S(1)}, u32[]{:S(2)}, u32[]{:S(2)}) %collective-permute-start.3) | collective-permute-done | bytes 102432 | tf_op jit(solution)/shard_map/ppermute | solution.py:25
  19.6 1.2 %shard_map.75 = f32[12,512]{1,0:T(8,128)S(1)} custom-call(f32[200,128]{1,0:T(8,128)S(1)} %pad_maximum_fusion.after.own, f32[200,128]{1,0:T(8,128)S(1)} %collective-permute-done.3.other, f32[2048,512]{1,0:T(8,128)S(1)} %shard_map.74.inverse), custom_call_target="tpu_custom_call" | custom-call | tf_op jit(solution)/shard_map/pallas_call | solution.py:181
  20.8 0.0 collective-permute-start.4
  20.8 1.2 %collective-permute-done.4 = f32[12,512]{1,0:T(8,128)S(1)} collective-permute-done((f32[12,512]{1,0:T(8,128)S(1)}, f32[12,512]{1,0:T(8,128)S(1)}, u32[]{:S(2)}, u32[]{:S(2)}) %collective-permute-start.4) | collective-permute-done | bytes 24608 | tf_op jit(solution)/shard_map/ppermute | solution.py:25
  22.1 2.7 %collective-permute-start.5 = (bf16[48,128]{1,0:T(8,128)(2,1)S(1)}, bf16[48,128]{1,0:T(8,128)(2,1)S(1)}, u32[]{:S(2)}, u32[]{:S(2)}) collective-permute-start(bf16[48,128]{1,0:T(8,128)(2,1)S(1)} %reshape.25), channel_id=1, source_target_pairs={{0,9},{1,8},{2,11},{3,10},{4,13},{5,12},{6,15},{7,14},{8,1},{9,0},... | collective-permute-start | bytes 36872 | tf_op jit(solution)/shard_map/ppermute | solution.py:25
  24.7 1.4 %collective-permute-done.5 = bf16[48,128]{1,0:T(8,128)(2,1)S(1)} collective-permute-done((bf16[48,128]{1,0:T(8,128)(2,1)S(1)}, bf16[48,128]{1,0:T(8,128)(2,1)S(1)}, u32[]{:S(2)}, u32[]{:S(2)}) %collective-permute-start.5) | collective-permute-done | bytes 12320 | tf_op jit(solution)/shard_map/ppermute | solution.py:25
  26.2 1.7 %collective-permute-start.6 = (bf16[96,128]{1,0:T(8,128)(2,1)S(1)}, bf16[96,128]{1,0:T(8,128)(2,1)S(1)}, u32[]{:S(2)}, u32[]{:S(2)}) collective-permute-start(bf16[96,128]{1,0:T(8,128)(2,1)S(1)} %maximum_select_fusion.4), channel_id=1, source_target_pairs={{0,5},{1,4},{2,7},{3,6},{4,1},{5,0},{6,3},{7,2},{8,13},{9,12},{10,... | collective-permute-start | bytes 73736 | tf_op jit(solution)/shard_map/ppermute | solution.py:25
  27.9 1.6 %collective-permute-done.6 = bf16[96,128]{1,0:T(8,128)(2,1)S(1)} collective-permute-done((bf16[96,128]{1,0:T(8,128)(2,1)S(1)}, bf16[96,128]{1,0:T(8,128)(2,1)S(1)}, u32[]{:S(2)}, u32[]{:S(2)}) %collective-permute-start.6) | collective-permute-done | bytes 24608 | tf_op jit(solution)/shard_map/ppermute | solution.py:25
  29.5 1.9 %collective-permute-start.7 = (bf16[192,128]{1,0:T(8,128)(2,1)S(1)}, bf16[192,128]{1,0:T(8,128)(2,1)S(1)}, u32[]{:S(2)}, u32[]{:S(2)}) collective-permute-start(bf16[192,128]{1,0:T(8,128)(2,1)S(1)} %maximum_select_fusion.3), channel_id=1, source_target_pairs={{0,3},{1,2},{2,1},{3,0},{4,7},{5,6},{6,5},{7,4},{8,11},{9,10},{10,... | collective-permute-start | bytes 147464 | tf_op jit(solution)/shard_map/ppermute | solution.py:25
  31.4 1.8 %collective-permute-done.7 = bf16[192,128]{1,0:T(8,128)(2,1)S(1)} collective-permute-done((bf16[192,128]{1,0:T(8,128)(2,1)S(1)}, bf16[192,128]{1,0:T(8,128)(2,1)S(1)}, u32[]{:S(2)}, u32[]{:S(2)}) %collective-permute-start.7) | collective-permute-done | bytes 49184 | tf_op jit(solution)/shard_map/ppermute | solution.py:25
  33.2 0.1 select_n.52
  33.3 0.1 copy.10
  33.4 0.1 reshape.26
  33.4 0.0 copy-done
  33.4 0.9 %fusion.2 = f32[12,64]{1,0:T(8,128)} fusion(bf16[12,4096]{1,0:T(8,128)(2,1)S(1)} %reshape.26, bf16[64,4096]{1,0:T(8,128)(2,1)S(1)} %copy-done), kind=kOutput, calls=%fused_computation.15 | convolution fusion | flops 6291456 | bytes 625664 | tf_op jit(solution)/shard_map/dot_general | solution.py:226
  (18 shorter events, 0.2 us)
Async XLA Ops:
  0.0 33.4 %copy-start = (bf16[64,4096]{1,0:T(8,128)(2,1)S(1)}, bf16[64,4096]{1,0:T(8,128)(2,1)}, u32[]{:S(2)}) copy-start(bf16[64,4096]{1,0:T(8,128)(2,1)} %param.13) | copy-start | bytes 1572868
  2.9 1.5 %collective-permute-start = (f32[128,128]{1,0:T(8,128)S(1)}, f32[128,128]{1,0:T(8,128)S(1)}, u32[]{:S(2)}, u32[]{:S(2)}) collective-permute-start(f32[128,128]{1,0:T(8,128)S(1)} %get-tuple-element.11), channel_id=1, source_target_pairs={{0,1},{1,0},{2,3},{3,2},{4,5},{5,4},{6,7},{7,6},{8,9},{9,8},{10,11... | collective-permute-start | bytes 196616 | tf_op jit(solution)/shard_map/ppermute | solution.py:25
  4.7 5.8 %collective-permute-start.1 = (f32[56,128]{1,0:T(8,128)S(1)}, f32[56,128]{1,0:T(8,128)S(1)}, u32[]{:S(2)}, u32[]{:S(2)}) collective-permute-start(f32[56,128]{1,0:T(8,128)S(1)} %pad_maximum_fusion.2), channel_id=1, source_target_pairs={{0,8},{1,9},{2,10},{3,11},{4,12},{5,13},{6,14},{7,15},{8,0},{9,1},... | collective-permute-start | bytes 86024 | tf_op jit(solution)/shard_map/ppermute | solution.py:25
  10.5 4.2 %collective-permute-start.2 = (f32[104,128]{1,0:T(8,128)S(1)}, f32[104,128]{1,0:T(8,128)S(1)}, u32[]{:S(2)}, u32[]{:S(2)}) collective-permute-start(f32[104,128]{1,0:T(8,128)S(1)} %pad_maximum_fusion.1), channel_id=1, source_target_pairs={{0,4},{1,5},{2,6},{3,7},{4,0},{5,1},{6,2},{7,3},{8,12},{9,13},{10,... | collective-permute-start | bytes 159752 | tf_op jit(solution)/shard_map/ppermute | solution.py:25
  14.8 4.8 %collective-permute-start.3 = (f32[200,128]{1,0:T(8,128)S(1)}, f32[200,128]{1,0:T(8,128)S(1)}, u32[]{:S(2)}, u32[]{:S(2)}) collective-permute-start(f32[200,128]{1,0:T(8,128)S(1)} %pad_maximum_fusion.after.own), channel_id=1, source_target_pairs={{0,2},{1,3},{2,0},{3,1},{4,6},{5,7},{6,4},{7,5},{8,10},{9,11},{10,... | collective-permute-start | bytes 307208 | tf_op jit(solution)/shard_map/ppermute | solution.py:25
  20.8 1.2 %collective-permute-start.4 = (f32[12,512]{1,0:T(8,128)S(1)}, f32[12,512]{1,0:T(8,128)S(1)}, u32[]{:S(2)}, u32[]{:S(2)}) collective-permute-start(f32[12,512]{1,0:T(8,128)S(1)} %shard_map.75), channel_id=1, source_target_pairs={{0,1},{1,0},{2,3},{3,2},{4,5},{5,4},{6,7},{7,6},{8,9},{9,8},{10,11... | collective-permute-start | bytes 73736 | tf_op jit(solution)/shard_map/ppermute | solution.py:25
  22.1 4.1 %collective-permute-start.5 = (bf16[48,128]{1,0:T(8,128)(2,1)S(1)}, bf16[48,128]{1,0:T(8,128)(2,1)S(1)}, u32[]{:S(2)}, u32[]{:S(2)}) collective-permute-start(bf16[48,128]{1,0:T(8,128)(2,1)S(1)} %reshape.25), channel_id=1, source_target_pairs={{0,9},{1,8},{2,11},{3,10},{4,13},{5,12},{6,15},{7,14},{8,1},{9,0},... | collective-permute-start | bytes 36872 | tf_op jit(solution)/shard_map/ppermute | solution.py:25
  26.2 3.3 %collective-permute-start.6 = (bf16[96,128]{1,0:T(8,128)(2,1)S(1)}, bf16[96,128]{1,0:T(8,128)(2,1)S(1)}, u32[]{:S(2)}, u32[]{:S(2)}) collective-permute-start(bf16[96,128]{1,0:T(8,128)(2,1)S(1)} %maximum_select_fusion.4), channel_id=1, source_target_pairs={{0,5},{1,4},{2,7},{3,6},{4,1},{5,0},{6,3},{7,2},{8,13},{9,12},{10,... | collective-permute-start | bytes 73736 | tf_op jit(solution)/shard_map/ppermute | solution.py:25
  29.5 3.7 %collective-permute-start.7 = (bf16[192,128]{1,0:T(8,128)(2,1)S(1)}, bf16[192,128]{1,0:T(8,128)(2,1)S(1)}, u32[]{:S(2)}, u32[]{:S(2)}) collective-permute-start(bf16[192,128]{1,0:T(8,128)(2,1)S(1)} %maximum_select_fusion.3), channel_id=1, source_target_pairs={{0,3},{1,2},{2,1},{3,0},{4,7},{5,6},{6,5},{7,4},{8,11},{9,10},{10,... | collective-permute-start | bytes 147464 | tf_op jit(solution)/shard_map/ppermute | solution.py:25

commit v4 on v3

--- a/solution.py
+++ b/solution.py
@@ -9,6 +9,7 @@
 
 SLOTS = 3
 LANES = 128
+TOP = 13.0
 VMEM_LIMIT = 16 << 20
 
 
@@ -41,10 +42,12 @@
     return [pltpu.with_memory_space_constraint(array, space) for array in arrays]
 
 
-def fetch_kernel(pieces, array, after, out, sems):
+def fetch_kernel(start, pieces, array, after, out, sems):
     rows = out.shape[0] // pieces
     copies = [
-        pltpu.make_async_copy(array.at[pl.ds(n * rows, rows), :], out.at[pl.ds(n * rows, rows), :], sems.at[n])
+        pltpu.make_async_copy(
+            array.at[pl.ds(start + n * rows, rows), :], out.at[pl.ds(n * rows, rows), :], sems.at[n]
+        )
         for n in range(pieces)
     ]
     for copy in copies:
@@ -53,11 +56,11 @@
         copy.wait()
 
 
-def fetch(array, after):
-    pieces = 4
-    return pl.pallas_call(
-        functools.partial(fetch_kernel, pieces),
-        out_shape=pltpu.VMEM(array.shape, array.dtype),
+def fetch(array, start, rows, after):
+    pieces = 2
+    return pl.pallas_call(
+        functools.partial(fetch_kernel, start, pieces),
+        out_shape=pltpu.VMEM((rows, array.shape[1]), array.dtype),
         in_specs=[pl.BlockSpec(memory_space=pltpu.HBM), pl.BlockSpec(memory_space=pltpu.VMEM)],
         out_specs=pl.BlockSpec(memory_space=pltpu.VMEM),
         scratch_shapes=[pltpu.SemaphoreType.DMA((pieces,))],
@@ -96,11 +99,11 @@
     first = jnp.broadcast_to(ids[:, :1], mask.shape)
     mask[...] = (jnp.broadcast_to(ids[...], mask.shape) - first == rows).astype(jnp.float32)
     shape = numbers.shape
-    place = lax.broadcasted_iota(jnp.int32, shape, 0) * LANES + lax.broadcasted_iota(jnp.int32, shape, 1)
-    place = place - SLOTS * position()
-    owned = (place >= 0) & (place < SLOTS)
+    row = lax.broadcasted_iota(jnp.int32, shape, 0)
+    place = row % 4 * LANES + lax.broadcasted_iota(jnp.int32, shape, 1) - SLOTS * position()
     first = jnp.broadcast_to(ids[:, :1], shape)
-    numbers[...] = jnp.where(owned, first + place, 0).astype(jnp.float32)
+    value = jnp.where(row < 4, first + place, 1)
+    numbers[...] = jnp.where((place >= 0) & (place < SLOTS), value, 0).astype(jnp.float32)
 
 
 def project(activations, gradients, proj_in, proj_out, doc_ids):
@@ -130,13 +133,55 @@
     )(*kept(pltpu.HBM, doc_ids.reshape(1, tokens), activations, proj_in.T, gradients, proj_out.T))
 
 
+def outer_kernel(part, other, mask, numbers, sums, tags, left):
+    rank, tokens = left.shape
+    left[...] = part[:rank, :] + other[:rank, :]
+    right = part[rank:, :] + other[rank:, :]
+    columns = [left[pl.ds(k, rank // 2, stride=2), :] for k in range(2)]
+    weighted = jnp.concatenate(
+        [jnp.concatenate([half * mask[s : s + 1, :] for half in columns], 1) for s in range(SLOTS)]
+    )
+    none = jnp.zeros_like(right)
+    paired = jnp.concatenate(
+        [jnp.concatenate([right, none], 1), jnp.concatenate([none, right], 1)]
+    )
+    found = lax.dot_general(
+        weighted,
+        paired,
+        (((1,), (1,)), ((), ())),
+        precision=lax.Precision.HIGHEST,
+        preferred_element_type=jnp.float32,
+    )
+    largest = jnp.max(jnp.max(jnp.abs(found), 0, keepdims=True), 1, keepdims=True)
+    power = jnp.floor(jnp.log2(jnp.maximum(largest, 1e-30)))
+    sums[...] = found * jnp.exp2(TOP - power)
+    rows = lax.broadcasted_iota(jnp.int32, numbers.shape, 0)
+    tags[...] = numbers[...] * jnp.where(rows < 4, 1.0, jnp.broadcast_to(power, rows.shape))
+
+
+def outer(part, other, mask, numbers):
+    rank, tokens = part.shape[0] // 2, part.shape[1]
+    vmem = pl.BlockSpec(memory_space=pltpu.VMEM)
+    return pl.pallas_call(
+        outer_kernel,
+        out_shape=(
+            pltpu.VMEM((SLOTS * rank // 2, 2 * rank), jnp.float32),
+            pltpu.VMEM(numbers.shape, jnp.float32),
+        ),
+        in_specs=[vmem] * 4,
+        out_specs=(vmem, vmem),
+        scratch_shapes=[pltpu.VMEM((rank, tokens), jnp.float32)],
+        compiler_params=pltpu.CompilerParams(vmem_limit_bytes=VMEM_LIMIT),
+    )(*kept(pltpu.VMEM, part, other, mask, numbers))
+
+
 def split(array):
     high = array.astype(jnp.bfloat16)
     return high, (array - high.astype(jnp.float32)).astype(jnp.bfloat16)
 
 
-def precondition_kernel(own, other, inverse, out, pieces):
-    depth = inverse.shape[0]
+def precondition_kernel(own, other, upper, lower, out, pieces):
+    depth = 2 * upper.shape[0]
     size = own.shape[0] - 8
     count = size * LANES // depth
     room = pieces.shape[0] // 2
@@ -146,12 +191,12 @@
             pieces[pl.ds(n * room, count), pl.ds(k * LANES, LANES)] = part[
                 pl.ds(k, count, stride=depth // LANES), :
             ]
-    step = 2 * LANES if depth % (2 * LANES) == 0 else LANES
+    step = 2 * LANES if depth % (4 * LANES) == 0 else LANES
     total = None
     for n in range(depth // step):
-        at = pl.ds(n * step, step)
-        high, low = split(pieces[:, at])
-        weights_high, weights_low = split(inverse[at, :])
+        high, low = split(pieces[:, pl.ds(n * step, step)])
+        half, row = divmod(n * step, depth // 2)
+        weights_high, weights_low = split((upper, lower)[half][pl.ds(row, step), :])
         first = jnp.dot(
             jnp.concatenate([high, low]), weights_high, preferred_element_type=jnp.float32
         )
@@ -161,10 +206,14 @@
     docs = lax.broadcasted_iota(jnp.int32, (out.shape[0], count), 0).astype(jnp.float32)
     result = None
     for n, part in enumerate((own, other)):
-        lanes = jnp.concatenate(
-            [part[size + r : size + r + 1, :] for r in range(pl.cdiv(count, LANES))], 1
-        )[:, :count]
-        pick = (jnp.broadcast_to(lanes, docs.shape) == docs).astype(jnp.float32)
+        rows = [
+            [part[size + r : size + r + 1, :] for r in range(at, at + pl.cdiv(count, LANES))]
+            for at in (0, 4)
+        ]
+        lanes, powers = (
+            jnp.broadcast_to(jnp.concatenate(row, 1)[:, :count], docs.shape) for row in rows
+        )
+        pick = jnp.where(lanes == docs, jnp.exp2(powers - TOP), 0.0)
         term = jnp.dot(
             pick,
             total[n * room : n * room + count],
@@ -175,17 +224,18 @@
     out[...] = result
 
 
-def precondition(own, other, inverse, doc_count):
+def precondition(own, other, upper, lower, doc_count):
     vmem = pl.BlockSpec(memory_space=pltpu.VMEM)
-    count = (own.shape[0] - 8) * LANES // inverse.shape[0]
+    depth, width = 2 * upper.shape[0], upper.shape[1]
+    count = (own.shape[0] - 8) * LANES // depth
     return pl.pallas_call(
         precondition_kernel,
-        out_shape=pltpu.VMEM((doc_count, inverse.shape[1]), jnp.float32),
-        in_specs=[vmem] * 3,
+        out_shape=pltpu.VMEM((doc_count, width), jnp.float32),
+        in_specs=[vmem] * 4,
         out_specs=vmem,
-        scratch_shapes=[pltpu.VMEM((2 * pl.cdiv(count, 8) * 8, inverse.shape[0]), jnp.float32)],
-        compiler_params=pltpu.CompilerParams(vmem_limit_bytes=VMEM_LIMIT),
-    )(*kept(pltpu.VMEM, own, other, inverse))
+        scratch_shapes=[pltpu.VMEM((2 * pl.cdiv(count, 8) * 8, depth), jnp.float32)],
+        compiler_params=pltpu.CompilerParams(vmem_limit_bytes=VMEM_LIMIT),
+    )(*kept(pltpu.VMEM, own, other, upper, lower))
 
 
 def shards(activations, gradients, doc_ids, proj_in, proj_out, inverse, store_rows):
@@ -194,27 +244,27 @@
     half = rank // lax.axis_size("col")
     doc_count = SLOTS * ctx // 2
     part, mask, numbers = project(activations, gradients, proj_in, proj_out, doc_ids)
-    both = part + swap(part, 0, 1)
-    own_half = lax.dynamic_slice_in_dim(both, lax.axis_index("col") * half, half, 0)
-    weighted = (mask[:SLOTS, None, :] * own_half[None]).reshape(SLOTS * half, -1)
-    local = lax.dot_general(
-        weighted,
-        both[rank:],
-        (((1,), (1,)), ((), ())),
-        precision=lax.Precision.HIGHEST,
-        preferred_element_type=jnp.float32,
-    )
-    blocks = local.reshape(-1, LANES)
-    payload = jnp.concatenate([blocks, numbers])
+    sums, tags = outer(part, swap(part, 0, 1), mask, numbers)
+    blocks, numbers = sums.astype(jnp.float16), tags.astype(jnp.float16)
+    rows = inverse.shape[0] // 2
     for distance in distances("ctx")[:-1]:
-        size = payload.shape[0] - 8
-        other = swap(payload, distance, 0)
-        blocks = ordered(payload[:size], other[:size], distance)
-        payload = jnp.concatenate([blocks, payload[size:] + other[size:]])
-    other = swap(payload, distances("ctx")[-1], 0)
-    inside = fetch(inverse, payload)
-    other, inside = lax.optimization_barrier((other, inside))
-    partial_q = precondition(payload, other, inside, doc_count)
+        size = blocks.shape[0]
+        payload = jnp.concatenate([blocks, numbers])
+        other = swap(payload, distance, 1)
+        if distance == distances("ctx")[-2]:
+            upper = fetch(inverse, 0, rows, numbers.astype(jnp.float32))
+            other, upper = lax.optimization_barrier((other, upper))
+        blocks = ordered(blocks, other[:size], distance)
+        numbers = numbers + other[size:]
+    halves = blocks.reshape(-1, 2, half * rank // LANES, LANES)
+    first = lax.axis_index("col") == 0
+    own = jnp.where(first, halves[:, 0], halves[:, 1]).reshape(-1, LANES)
+    others = jnp.where(first, halves[:, 1], halves[:, 0]).reshape(-1, LANES)
+    payload = jnp.concatenate([own, numbers]).astype(jnp.float32)
+    other = swap(jnp.concatenate([others, numbers]), distances("ctx")[-1], 1)
+    lower = fetch(inverse, rows, rows, payload)
+    other, lower = lax.optimization_barrier((other, lower))
+    partial_q = precondition(payload, other.astype(jnp.float32), upper, lower, doc_count)
     precond = (partial_q + swap(partial_q, 0, 1)).astype(jnp.bfloat16)
     width = precond.shape[1]
     whole = precond.reshape(-1, min(width, LANES))

time: 34.4 us -> 33.5 us (0.974)
  waiting for transfers between devices: 11.4 us -> 9.29 us
  Pallas kernels: 6.3 us -> 7.59 us
    ppermute x8, waiting for transfers between devices: 11.4 us -> 9.29 us  [swap(): return lax.ppermute(block, ('ctx', 'col'), route)]
    pallas_call x2 -> x4, Pallas kernels: 3.39 us -> 4.68 us  [the longest x2 3.11 us: fetch(): pl.pallas_call(functools.partial(fetch_kernel, start, pieces), out_shape=...]
  transfers between devices with their start and end apart: 8 -> 8, of which waited for: 8 -> 8; matrix products, arithmetic and copies ran while one was open for 0% -> 0% of each run, Pallas kernels for 6% -> 9%
where the time goes in v4:
time: 33.5 us; the launch traced here: 33.3 us
  starting transfers between devices  14.9 us (44%)
  waiting for transfers between devices  9.29 us (28%)
  Pallas kernels  7.59 us (23%)
  matrix products  0.85 us (3%)
    ppermute x8, starting transfers between devices, swap(): return lax.ppermute(block, ('ctx', 'col'), route)  14.9 us
    ppermute x8, waiting for transfers between devices, swap(): return lax.ppermute(block, ('ctx', 'col'), route)  9.29 us
    pallas_call x2, Pallas kernels, fetch(): pl.pallas_call(functools.partial(fetch_kernel, start, pieces), out_shape=...  3.11 us
    pallas_call x1, Pallas kernels, project(): pl.pallas_call(functools.partial(project_kernel, chunks), out_shape=(pltp...  2.91 us
    pallas_call x1, Pallas kernels, precondition(): pl.pallas_call(precondition_kernel, out_shape=pltpu.VMEM((doc_count, widt...  1.2 us
    dot_general x1, matrix products, shards(): lax.dot_general(whole, store_rows, (((1,), (1,)), ((), ())), preferred_el...  0.85 us
  transfers between devices with their start and end apart: 8, of which 8 were waited for; matrix products, arithmetic and copies ran while one was open for 0% of the time, Pallas kernels for 9%

profile of v4, /device:TPU:0, one launch (start us, length us, event | category | flops | bytes accessed | tf_op | source)
XLA Modules:
  0.0 33.3 jit_solution(4171840216365058985)
XLA Ops:
  0.0 0.0 copy-start
  0.0 2.9 %shard_map.73 = (f32[128,128]{1,0:T(8,128)S(1)}, f32[8,128]{1,0:T(8,128)S(1)}, f32[8,128]{1,0:T(8,128)S(1)}) custom-call(s32[1,128]{1,0:T(1,128)} %bitcast.15, bf16[128,2048]{1,0:T(8,128)(2,1)} %act_hbm.1, bf16[64,2048]{1,0:T(8,128)(2,1)} %bitcast.12, bf16[128,7168]{1,0:T(8,128)(2,1)} %grad_hbm.1, bf16[64,7168]{1,0:T(8,128)(2,1)} %bitcast.9), custom_call_target="tpu_custom_call" | custom-call | tf_op jit(solution)/shard_map/pallas_call | solution.py:115
  2.9 0.6 %collective-permute-start = (f32[128,128]{1,0:T(8,128)S(1)}, f32[128,128]{1,0:T(8,128)S(1)}, u32[]{:S(2)}, u32[]{:S(2)}) collective-permute-start(f32[128,128]{1,0:T(8,128)S(1)} %get-tuple-element.14.part), channel_id=1, source_target_pairs={{0,1},{1,0},{2,3},{3,2},{4,5},{5,4},{6,7},{7,6},{8,9},{9,8},{10,11... | collective-permute-start | bytes 196616 | tf_op jit(solution)/shard_map/ppermute | solution.py:26
  3.5 0.9 %collective-permute-done.other = f32[128,128]{1,0:T(8,128)S(1)} collective-permute-done((f32[128,128]{1,0:T(8,128)S(1)}, f32[128,128]{1,0:T(8,128)S(1)}, u32[]{:S(2)}, u32[]{:S(2)}) %collective-permute-start) | collective-permute-done | bytes 65568 | tf_op jit(solution)/shard_map/ppermute | solution.py:26
  4.4 0.4 %shard_map.74 = (f32[96,128]{1,0:T(8,128)S(1)}, f32[8,128]{1,0:T(8,128)S(1)}) custom-call(f32[128,128]{1,0:T(8,128)S(1)} %get-tuple-element.14.part, f32[128,128]{1,0:T(8,128)S(1)} %collective-permute-done.other, f32[8,128]{1,0:T(8,128)S(1)} %get-tuple-element.15.mask, f32[8,128]{1,0:T(8,128)S(1)} %get-tuple-element.16.numbers), custom_call_target="tpu_custom_call" | custom-call | tf_op jit(solution)/shard_map/pallas_call | solution.py:165
  4.8 3.8 %collective-permute-start.1 = (f16[104,128]{1,0:T(8,128)(2,1)S(1)}, f16[104,128]{1,0:T(8,128)(2,1)S(1)}, u32[]{:S(2)}, u32[]{:S(2)}) collective-permute-start(f16[104,128]{1,0:T(8,128)(2,1)S(1)} %pad_maximum_fusion.3), channel_id=1, source_target_pairs={{0,9},{1,8},{2,11},{3,10},{4,13},{5,12},{6,15},{7,14},{8,1},{9,0},... | collective-permute-start | bytes 79880 | tf_op jit(solution)/shard_map/ppermute | solution.py:26
  8.6 1.5 %collective-permute-done.1 = f16[104,128]{1,0:T(8,128)(2,1)S(1)} collective-permute-done((f16[104,128]{1,0:T(8,128)(2,1)S(1)}, f16[104,128]{1,0:T(8,128)(2,1)S(1)}, u32[]{:S(2)}, u32[]{:S(2)}) %collective-permute-start.1) | collective-permute-done | bytes 26656 | tf_op jit(solution)/shard_map/ppermute | solution.py:26
  10.2 1.7 %collective-permute-start.2 = (f16[200,128]{1,0:T(8,128)(2,1)S(1)}, f16[200,128]{1,0:T(8,128)(2,1)S(1)}, u32[]{:S(2)}, u32[]{:S(2)}) collective-permute-start(f16[200,128]{1,0:T(8,128)(2,1)S(1)} %pad_maximum_fusion.2), channel_id=1, source_target_pairs={{0,5},{1,4},{2,7},{3,6},{4,1},{5,0},{6,3},{7,2},{8,13},{9,12},{10,... | collective-permute-start | bytes 153608 | tf_op jit(solution)/shard_map/ppermute | solution.py:26
  11.9 1.6 %shard_map.75.upper = f32[1024,512]{1,0:T(8,128)S(1)} custom-call(f32[2048,512]{1,0:T(8,128)} %array.3, f32[8,128]{1,0:T(8,128)S(1)} %get-tuple-element.23.after), custom_call_target="tpu_custom_call" | custom-call | tf_op jit(solution)/shard_map/pallas_call | solution.py:61
  13.4 0.4 %collective-permute-done.2 = f16[200,128]{1,0:T(8,128)(2,1)S(1)} collective-permute-done((f16[200,128]{1,0:T(8,128)(2,1)S(1)}, f16[200,128]{1,0:T(8,128)(2,1)S(1)}, u32[]{:S(2)}, u32[]{:S(2)}) %collective-permute-start.2) | collective-permute-done | bytes 51232 | tf_op jit(solution)/shard_map/ppermute | solution.py:26
  13.8 0.1 maximum_select_fusion
  14.0 1.8 %collective-permute-start.3 = (f16[200,128]{1,0:T(8,128)(2,1)S(1)}, f16[200,128]{1,0:T(8,128)(2,1)S(1)}, u32[]{:S(2)}, u32[]{:S(2)}) collective-permute-start(f16[200,128]{1,0:T(8,128)(2,1)S(1)} %get-tuple-element.27), channel_id=1, source_target_pairs={{0,3},{1,2},{2,1},{3,0},{4,7},{5,6},{6,5},{7,4},{8,11},{9,10},{10,... | collective-permute-start | bytes 153608 | tf_op jit(solution)/shard_map/ppermute | solution.py:26
  15.8 1.6 %shard_map.76.lower = f32[1024,512]{1,0:T(8,128)S(1)} custom-call(f32[2048,512]{1,0:T(8,128)} %array.3, f32[200,128]{1,0:T(8,128)S(1)} %get-tuple-element.28.after.own), custom_call_target="tpu_custom_call" | custom-call | tf_op jit(solution)/shard_map/pallas_call | solution.py:61
  17.3 0.3 collective-permute-done.3
  17.6 1.2 %shard_map.77 = f32[12,512]{1,0:T(8,128)S(1)} custom-call(f32[200,128]{1,0:T(8,128)S(1)} %get-tuple-element.28.after.own, f32[200,128]{1,0:T(8,128)S(1)} %convert_element_type.22.other, f32[1024,512]{1,0:T(8,128)S(1)} %shard_map.75.upper, f32[1024,512]{1,0:T(8,128)S(1)} %shard_map.76.lower), custom_call_target="tpu_custom_call" | custom-call | tf_op jit(solution)/shard_map/pallas_call | solution.py:231
  18.8 0.3 %collective-permute-start.4 = (f32[12,512]{1,0:T(8,128)S(1)}, f32[12,512]{1,0:T(8,128)S(1)}, u32[]{:S(2)}, u32[]{:S(2)}) collective-permute-start(f32[12,512]{1,0:T(8,128)S(1)} %shard_map.77), channel_id=1, source_target_pairs={{0,1},{1,0},{2,3},{3,2},{4,5},{5,4},{6,7},{7,6},{8,9},{9,8},{10,11... | collective-permute-start | bytes 73736 | tf_op jit(solution)/shard_map/ppermute | solution.py:26
  19.2 0.9 %collective-permute-done.4 = f32[12,512]{1,0:T(8,128)S(1)} collective-permute-done((f32[12,512]{1,0:T(8,128)S(1)}, f32[12,512]{1,0:T(8,128)S(1)}, u32[]{:S(2)}, u32[]{:S(2)}) %collective-permute-start.4) | collective-permute-done | bytes 24608 | tf_op jit(solution)/shard_map/ppermute | solution.py:26
  20.1 3.2 %collective-permute-start.5 = (bf16[48,128]{1,0:T(8,128)(2,1)S(1)}, bf16[48,128]{1,0:T(8,128)(2,1)S(1)}, u32[]{:S(2)}, u32[]{:S(2)}) collective-permute-start(bf16[48,128]{1,0:T(8,128)(2,1)S(1)} %reshape.30), channel_id=1, source_target_pairs={{0,9},{1,8},{2,11},{3,10},{4,13},{5,12},{6,15},{7,14},{8,1},{9,0},... | collective-permute-start | bytes 36872 | tf_op jit(solution)/shard_map/ppermute | solution.py:26
  23.2 1.4 %collective-permute-done.5 = bf16[48,128]{1,0:T(8,128)(2,1)S(1)} collective-permute-done((bf16[48,128]{1,0:T(8,128)(2,1)S(1)}, bf16[48,128]{1,0:T(8,128)(2,1)S(1)}, u32[]{:S(2)}, u32[]{:S(2)}) %collective-permute-start.5) | collective-permute-done | bytes 12320 | tf_op jit(solution)/shard_map/ppermute | solution.py:26
  24.7 2.2 %collective-permute-start.6 = (bf16[96,128]{1,0:T(8,128)(2,1)S(1)}, bf16[96,128]{1,0:T(8,128)(2,1)S(1)}, u32[]{:S(2)}, u32[]{:S(2)}) collective-permute-start(bf16[96,128]{1,0:T(8,128)(2,1)S(1)} %maximum_select_fusion.4), channel_id=1, source_target_pairs={{0,5},{1,4},{2,7},{3,6},{4,1},{5,0},{6,3},{7,2},{8,13},{9,12},{10,... | collective-permute-start | bytes 73736 | tf_op jit(solution)/shard_map/ppermute | solution.py:26
  26.9 1.5 %collective-permute-done.6 = bf16[96,128]{1,0:T(8,128)(2,1)S(1)} collective-permute-done((bf16[96,128]{1,0:T(8,128)(2,1)S(1)}, bf16[96,128]{1,0:T(8,128)(2,1)S(1)}, u32[]{:S(2)}, u32[]{:S(2)}) %collective-permute-start.6) | collective-permute-done | bytes 24608 | tf_op jit(solution)/shard_map/ppermute | solution.py:26
  28.4 1.3 %collective-permute-start.7 = (bf16[192,128]{1,0:T(8,128)(2,1)S(1)}, bf16[192,128]{1,0:T(8,128)(2,1)S(1)}, u32[]{:S(2)}, u32[]{:S(2)}) collective-permute-start(bf16[192,128]{1,0:T(8,128)(2,1)S(1)} %maximum_select_fusion.3), channel_id=1, source_target_pairs={{0,3},{1,2},{2,1},{3,0},{4,7},{5,6},{6,5},{7,4},{8,11},{9,10},{10,... | collective-permute-start | bytes 147464 | tf_op jit(solution)/shard_map/ppermute | solution.py:26
  29.8 2.4 %collective-permute-done.7 = bf16[192,128]{1,0:T(8,128)(2,1)S(1)} collective-permute-done((bf16[192,128]{1,0:T(8,128)(2,1)S(1)}, bf16[192,128]{1,0:T(8,128)(2,1)S(1)}, u32[]{:S(2)}, u32[]{:S(2)}) %collective-permute-start.7) | collective-permute-done | bytes 49184 | tf_op jit(solution)/shard_map/ppermute | solution.py:26
  32.2 0.1 select_n.84
  32.3 0.1 copy.8
  32.4 0.1 reshape.31
  32.4 0.0 copy-done
  32.4 0.9 %fusion.2 = f32[12,64]{1,0:T(8,128)} fusion(bf16[12,4096]{1,0:T(8,128)(2,1)S(1)} %reshape.31, bf16[64,4096]{1,0:T(8,128)(2,1)S(1)} %copy-done), kind=kOutput, calls=%fused_computation.16 | convolution fusion | flops 6291456 | bytes 625664 | tf_op jit(solution)/shard_map/dot_general | solution.py:276
  (17 shorter events, 0.3 us)
Async XLA Ops:
  0.0 32.4 %copy-start = (bf16[64,4096]{1,0:T(8,128)(2,1)S(1)}, bf16[64,4096]{1,0:T(8,128)(2,1)}, u32[]{:S(2)}) copy-start(bf16[64,4096]{1,0:T(8,128)(2,1)} %param.13) | copy-start | bytes 1572868
  2.9 1.5 %collective-permute-start = (f32[128,128]{1,0:T(8,128)S(1)}, f32[128,128]{1,0:T(8,128)S(1)}, u32[]{:S(2)}, u32[]{:S(2)}) collective-permute-start(f32[128,128]{1,0:T(8,128)S(1)} %get-tuple-element.14.part), channel_id=1, source_target_pairs={{0,1},{1,0},{2,3},{3,2},{4,5},{5,4},{6,7},{7,6},{8,9},{9,8},{10,11... | collective-permute-start | bytes 196616 | tf_op jit(solution)/shard_map/ppermute | solution.py:26
  4.8 5.3 %collective-permute-start.1 = (f16[104,128]{1,0:T(8,128)(2,1)S(1)}, f16[104,128]{1,0:T(8,128)(2,1)S(1)}, u32[]{:S(2)}, u32[]{:S(2)}) collective-permute-start(f16[104,128]{1,0:T(8,128)(2,1)S(1)} %pad_maximum_fusion.3), channel_id=1, source_target_pairs={{0,9},{1,8},{2,11},{3,10},{4,13},{5,12},{6,15},{7,14},{8,1},{9,0},... | collective-permute-start | bytes 79880 | tf_op jit(solution)/shard_map/ppermute | solution.py:26
  10.2 3.6 %collective-permute-start.2 = (f16[200,128]{1,0:T(8,128)(2,1)S(1)}, f16[200,128]{1,0:T(8,128)(2,1)S(1)}, u32[]{:S(2)}, u32[]{:S(2)}) collective-permute-start(f16[200,128]{1,0:T(8,128)(2,1)S(1)} %pad_maximum_fusion.2), channel_id=1, source_target_pairs={{0,5},{1,4},{2,7},{3,6},{4,1},{5,0},{6,3},{7,2},{8,13},{9,12},{10,... | collective-permute-start | bytes 153608 | tf_op jit(solution)/shard_map/ppermute | solution.py:26
  14.0 3.6 %collective-permute-start.3 = (f16[200,128]{1,0:T(8,128)(2,1)S(1)}, f16[200,128]{1,0:T(8,128)(2,1)S(1)}, u32[]{:S(2)}, u32[]{:S(2)}) collective-permute-start(f16[200,128]{1,0:T(8,128)(2,1)S(1)} %get-tuple-element.27), channel_id=1, source_target_pairs={{0,3},{1,2},{2,1},{3,0},{4,7},{5,6},{6,5},{7,4},{8,11},{9,10},{10,... | collective-permute-start | bytes 153608 | tf_op jit(solution)/shard_map/ppermute | solution.py:26
  18.8 1.2 %collective-permute-start.4 = (f32[12,512]{1,0:T(8,128)S(1)}, f32[12,512]{1,0:T(8,128)S(1)}, u32[]{:S(2)}, u32[]{:S(2)}) collective-permute-start(f32[12,512]{1,0:T(8,128)S(1)} %shard_map.77), channel_id=1, source_target_pairs={{0,1},{1,0},{2,3},{3,2},{4,5},{5,4},{6,7},{7,6},{8,9},{9,8},{10,11... | collective-permute-start | bytes 73736 | tf_op jit(solution)/shard_map/ppermute | solution.py:26
  20.1 4.6 %collective-permute-start.5 = (bf16[48,128]{1,0:T(8,128)(2,1)S(1)}, bf16[48,128]{1,0:T(8,128)(2,1)S(1)}, u32[]{:S(2)}, u32[]{:S(2)}) collective-permute-start(bf16[48,128]{1,0:T(8,128)(2,1)S(1)} %reshape.30), channel_id=1, source_target_pairs={{0,9},{1,8},{2,11},{3,10},{4,13},{5,12},{6,15},{7,14},{8,1},{9,0},... | collective-permute-start | bytes 36872 | tf_op jit(solution)/shard_map/ppermute | solution.py:26
  24.7 3.7 %collective-permute-start.6 = (bf16[96,128]{1,0:T(8,128)(2,1)S(1)}, bf16[96,128]{1,0:T(8,128)(2,1)S(1)}, u32[]{:S(2)}, u32[]{:S(2)}) collective-permute-start(bf16[96,128]{1,0:T(8,128)(2,1)S(1)} %maximum_select_fusion.4), channel_id=1, source_target_pairs={{0,5},{1,4},{2,7},{3,6},{4,1},{5,0},{6,3},{7,2},{8,13},{9,12},{10,... | collective-permute-start | bytes 73736 | tf_op jit(solution)/shard_map/ppermute | solution.py:26
  28.4 3.7 %collective-permute-start.7 = (bf16[192,128]{1,0:T(8,128)(2,1)S(1)}, bf16[192,128]{1,0:T(8,128)(2,1)S(1)}, u32[]{:S(2)}, u32[]{:S(2)}) collective-permute-start(bf16[192,128]{1,0:T(8,128)(2,1)S(1)} %maximum_select_fusion.3), channel_id=1, source_target_pairs={{0,3},{1,2},{2,1},{3,0},{4,7},{5,6},{6,5},{7,4},{8,11},{9,10},{10,... | collective-permute-start | bytes 147464 | tf_op jit(solution)/shard_map/ppermute | solution.py:26

commit v5 on v4

--- a/solution.py
+++ b/solution.py
@@ -13,17 +13,36 @@
 VMEM_LIMIT = 16 << 20
 
 
-def distances(axis):
-    size = lax.axis_size(axis)
-    return [size >> step for step in range(1, size.bit_length())]
-
-
-def swap(block, distance, cross):
+def far_distances():
+    size = lax.axis_size("ctx")
+    return [size >> step for step in range(1, size.bit_length() - 2)]
+
+
+def near_distance(c, p, last):
+    even = (c ^ (c >> 1) ^ p ^ last) & 1
+    return 1 + even
+
+
+def swap(block, partner):
     ctx, col = lax.axis_size("ctx"), lax.axis_size("col")
-    route = [
-        (c * col + p, (c ^ distance) * col + (p ^ cross)) for c in range(ctx) for p in range(col)
-    ]
+    route = []
+    for c in range(ctx):
+        for p in range(col):
+            there, core = partner(c, p)
+            route.append((c * col + p, there * col + core))
     return lax.ppermute(block, ("ctx", "col"), route)
+
+
+def swap_cores(block):
+    return swap(block, lambda c, p: (c, p ^ 1))
+
+
+def swap_far(block, distance):
+    return swap(block, lambda c, p: (c ^ distance, p ^ 1))
+
+
+def swap_near(block, last):
+    return swap(block, lambda c, p: (c ^ near_distance(c, p, last), p ^ 1))
 
 
 def ordered(own, other, distance):
@@ -33,7 +52,7 @@
 
 def position():
     index, place = lax.axis_index("ctx"), 0
-    for step, distance in enumerate(distances("ctx")[:-1]):
+    for step, distance in enumerate(far_distances()):
         place = place + jnp.where((index & distance) != 0, 1 << step, 0)
     return place
 
@@ -100,10 +119,11 @@
     mask[...] = (jnp.broadcast_to(ids[...], mask.shape) - first == rows).astype(jnp.float32)
     shape = numbers.shape
     row = lax.broadcasted_iota(jnp.int32, shape, 0)
-    place = row % 4 * LANES + lax.broadcasted_iota(jnp.int32, shape, 1) - SLOTS * position()
+    place = row % 2 * LANES + lax.broadcasted_iota(jnp.int32, shape, 1) - SLOTS * position()
     first = jnp.broadcast_to(ids[:, :1], shape)
     value = jnp.where(row < 4, first + place, 1)
-    numbers[...] = jnp.where((place >= 0) & (place < SLOTS), value, 0).astype(jnp.float32)
+    owned = (place >= 0) & (place < SLOTS) & (row % 4 < 2)
+    numbers[...] = jnp.where(owned, value, 0).astype(jnp.float32)
 
 
 def project(activations, gradients, proj_in, proj_out, doc_ids):
@@ -206,13 +226,16 @@
     docs = lax.broadcasted_iota(jnp.int32, (out.shape[0], count), 0).astype(jnp.float32)
     result = None
     for n, part in enumerate((own, other)):
-        rows = [
-            [part[size + r : size + r + 1, :] for r in range(at, at + pl.cdiv(count, LANES))]
-            for at in (0, 4)
-        ]
-        lanes, powers = (
-            jnp.broadcast_to(jnp.concatenate(row, 1)[:, :count], docs.shape) for row in rows
-        )
+        rows = []
+        for at in (0, 4):
+            lanes = [
+                jnp.concatenate(
+                    [part[size + r : size + r + 1, :] for r in range(k, k + pl.cdiv(count // 2, LANES))], 1
+                )[:, : count // 2]
+                for k in (at, at + 2)
+            ]
+            rows.append(jnp.broadcast_to(jnp.concatenate(lanes, 1), docs.shape))
+        lanes, powers = rows
         pick = jnp.where(lanes == docs, jnp.exp2(powers - TOP), 0.0)
         term = jnp.dot(
             pick,
@@ -244,35 +267,47 @@
     half = rank // lax.axis_size("col")
     doc_count = SLOTS * ctx // 2
     part, mask, numbers = project(activations, gradients, proj_in, proj_out, doc_ids)
-    sums, tags = outer(part, swap(part, 0, 1), mask, numbers)
-    blocks, numbers = sums.astype(jnp.float16), tags.astype(jnp.float16)
+    sums, tags = outer(part, swap_cores(part), mask, numbers)
+    blocks, tags = sums.astype(jnp.float16), tags.astype(jnp.float16)
+    for distance in far_distances():
+        size = blocks.shape[0]
+        other = swap_far(jnp.concatenate([blocks, tags]), distance)
+        blocks = ordered(blocks, other[:size], distance)
+        tags = tags + other[size:]
     rows = inverse.shape[0] // 2
-    for distance in distances("ctx")[:-1]:
-        size = blocks.shape[0]
-        payload = jnp.concatenate([blocks, numbers])
-        other = swap(payload, distance, 1)
-        if distance == distances("ctx")[-2]:
-            upper = fetch(inverse, 0, rows, numbers.astype(jnp.float32))
-            other, upper = lax.optimization_barrier((other, upper))
-        blocks = ordered(blocks, other[:size], distance)
-        numbers = numbers + other[size:]
+    size = blocks.shape[0]
+    other = swap_near(jnp.concatenate([blocks, tags]), 0)
+    upper = fetch(inverse, 0, rows, tags.astype(jnp.float32))
+    other, upper = lax.optimization_barrier((other, upper))
+    blocks = jnp.concatenate([blocks, other[:size]])
+    tags = tags + jnp.roll(other[size:], 2, 0)
     halves = blocks.reshape(-1, 2, half * rank // LANES, LANES)
     first = lax.axis_index("col") == 0
     own = jnp.where(first, halves[:, 0], halves[:, 1]).reshape(-1, LANES)
     others = jnp.where(first, halves[:, 1], halves[:, 0]).reshape(-1, LANES)
-    payload = jnp.concatenate([own, numbers]).astype(jnp.float32)
-    other = swap(jnp.concatenate([others, numbers]), distances("ctx")[-1], 1)
+    payload = jnp.concatenate([own, tags]).astype(jnp.float32)
+    other = swap_near(jnp.concatenate([others, tags]), 1)
     lower = fetch(inverse, rows, rows, payload)
     other, lower = lax.optimization_barrier((other, lower))
     partial_q = precondition(payload, other.astype(jnp.float32), upper, lower, doc_count)
-    precond = (partial_q + swap(partial_q, 0, 1)).astype(jnp.bfloat16)
+    precond = (partial_q + swap_cores(partial_q)).astype(jnp.bfloat16)
     width = precond.shape[1]
     whole = precond.reshape(-1, min(width, LANES))
-    for distance in distances("ctx"):
-        whole = ordered(whole, swap(whole, distance, 1), distance)
-    bits = len(distances("ctx"))
-    whole = whole.reshape((2,) * bits + (doc_count, width))
-    whole = whole.transpose((bits,) + tuple(range(bits))[::-1] + (bits + 1,)).reshape(doc_count, -1)
+    for distance in far_distances():
+        whole = ordered(whole, swap_far(whole, distance), distance)
+    whole = jnp.stack([whole, swap_near(whole, 0)])
+    (own, near), (next_one, farthest) = whole, swap_near(whole, 1)
+    c, p = lax.axis_index("ctx"), lax.axis_index("col")
+    single = near_distance(c, p, 0) == 1
+    near, next_one = jnp.where(single, near, next_one), jnp.where(single, next_one, near)
+    whole = jnp.stack([own, near, next_one, farthest])
+    for bit in (1, 2):
+        pairs = whole.reshape((2 // bit, 2, bit) + whole.shape[1:])
+        whole = jnp.where((c & bit) != 0, pairs[:, ::-1], pairs).reshape(whole.shape)
+    bits = len(far_distances())
+    whole = whole.reshape((4,) + (2,) * bits + (doc_count, width))
+    whole = whole.transpose((bits + 1,) + tuple(range(1, bits + 1))[::-1] + (0, bits + 2))
+    whole = whole.reshape(doc_count, -1)
     return lax.dot_general(
         whole, store_rows, (((1,), (1,)), ((), ())), preferred_element_type=jnp.float32
     )

time: 33.5 us -> 32.8 us (0.979)
  starting transfers between devices: 14.9 us -> 14.1 us
    ppermute x8, starting transfers between devices: 14.9 us -> 14.1 us  [swap(): return lax.ppermute(block, ('ctx', 'col'), route)]
  transfers between devices with their start and end apart: 8 -> 8, of which waited for: 8 -> 8; matrix products, arithmetic and copies ran while one was open for 0% -> 0% of each run, Pallas kernels for 9% -> 10%
where the time goes in v5:
time: 32.8 us; the launch traced here: 32.7 us
  starting transfers between devices  14.1 us (43%)
  waiting for transfers between devices  9.29 us (28%)
  Pallas kernels  7.58 us (23%)
  matrix products  0.85 us (3%)
    ppermute x8, starting transfers between devices, swap(): return lax.ppermute(block, ('ctx', 'col'), route)  14.1 us
    ppermute x8, waiting for transfers between devices, swap(): return lax.ppermute(block, ('ctx', 'col'), route)  9.29 us
    pallas_call x2, Pallas kernels, fetch(): pl.pallas_call(functools.partial(fetch_kernel, start, pieces), out_shape=...  3.11 us
    pallas_call x1, Pallas kernels, project(): pl.pallas_call(functools.partial(project_kernel, chunks), out_shape=(pltp...  2.91 us
    pallas_call x1, Pallas kernels, precondition(): pl.pallas_call(precondition_kernel, out_shape=pltpu.VMEM((doc_count, widt...  1.2 us
    dot_general x1, matrix products, shards(): lax.dot_general(whole, store_rows, (((1,), (1,)), ((), ())), preferred_el...  0.85 us
  transfers between devices with their start and end apart: 8, of which 8 were waited for; matrix products, arithmetic and copies ran while one was open for 0% of the time, Pallas kernels for 10%

profile of v5, /device:TPU:0, one launch (start us, length us, event | category | flops | bytes accessed | tf_op | source)
XLA Modules:
  0.0 32.7 jit_solution(13924749080516747088)
XLA Ops:
  0.0 0.0 copy-start
  0.0 2.9 %shard_map.73 = (f32[128,128]{1,0:T(8,128)S(1)}, f32[8,128]{1,0:T(8,128)S(1)}, f32[8,128]{1,0:T(8,128)S(1)}) custom-call(s32[1,128]{1,0:T(1,128)} %bitcast.35, bf16[128,2048]{1,0:T(8,128)(2,1)} %act_hbm.1, bf16[64,2048]{1,0:T(8,128)(2,1)} %bitcast.30, bf16[128,7168]{1,0:T(8,128)(2,1)} %grad_hbm.1, bf16[64,7168]{1,0:T(8,128)(2,1)} %bitcast.26), custom_call_target="tpu_custom_call" | custom-call | tf_op jit(solution)/shard_map/pallas_call | solution.py:135
  2.9 0.6 %collective-permute-start = (f32[128,128]{1,0:T(8,128)S(1)}, f32[128,128]{1,0:T(8,128)S(1)}, u32[]{:S(2)}, u32[]{:S(2)}) collective-permute-start(f32[128,128]{1,0:T(8,128)S(1)} %get-tuple-element.14.part), channel_id=1, source_target_pairs={{0,1},{1,0},{2,3},{3,2},{4,5},{5,4},{6,7},{7,6},{8,9},{9,8},{10,11... | collective-permute-start | bytes 196616 | tf_op jit(solution)/shard_map/ppermute | solution.py:33
  3.5 0.9 %collective-permute-done.other = f32[128,128]{1,0:T(8,128)S(1)} collective-permute-done((f32[128,128]{1,0:T(8,128)S(1)}, f32[128,128]{1,0:T(8,128)S(1)}, u32[]{:S(2)}, u32[]{:S(2)}) %collective-permute-start) | collective-permute-done | bytes 65568 | tf_op jit(solution)/shard_map/ppermute | solution.py:33
  4.4 0.4 %shard_map.74 = (f32[96,128]{1,0:T(8,128)S(1)}, f32[8,128]{1,0:T(8,128)S(1)}) custom-call(f32[128,128]{1,0:T(8,128)S(1)} %get-tuple-element.14.part, f32[128,128]{1,0:T(8,128)S(1)} %collective-permute-done.other, f32[8,128]{1,0:T(8,128)S(1)} %get-tuple-element.15.mask, f32[8,128]{1,0:T(8,128)S(1)} %get-tuple-element.16.numbers), custom_call_target="tpu_custom_call" | custom-call | tf_op jit(solution)/shard_map/pallas_call | solution.py:185
  4.8 3.8 %collective-permute-start.1 = (f16[104,128]{1,0:T(8,128)(2,1)S(1)}, f16[104,128]{1,0:T(8,128)(2,1)S(1)}, u32[]{:S(2)}, u32[]{:S(2)}) collective-permute-start(f16[104,128]{1,0:T(8,128)(2,1)S(1)} %pad_maximum_fusion.6), channel_id=1, source_target_pairs={{0,9},{1,8},{2,11},{3,10},{4,13},{5,12},{6,15},{7,14},{8,1},{9,0},... | collective-permute-start | bytes 79880 | tf_op jit(solution)/shard_map/ppermute | solution.py:33
  8.6 1.5 %collective-permute-done.1 = f16[104,128]{1,0:T(8,128)(2,1)S(1)} collective-permute-done((f16[104,128]{1,0:T(8,128)(2,1)S(1)}, f16[104,128]{1,0:T(8,128)(2,1)S(1)}, u32[]{:S(2)}, u32[]{:S(2)}) %collective-permute-start.1) | collective-permute-done | bytes 26656 | tf_op jit(solution)/shard_map/ppermute | solution.py:33
  10.2 1.6 %collective-permute-start.2 = (f16[200,128]{1,0:T(8,128)(2,1)S(1)}, f16[200,128]{1,0:T(8,128)(2,1)S(1)}, u32[]{:S(2)}, u32[]{:S(2)}) collective-permute-start(f16[200,128]{1,0:T(8,128)(2,1)S(1)} %pad_maximum_fusion.4), channel_id=1, source_target_pairs={{0,3},{1,4},{2,7},{3,0},{4,1},{5,6},{6,5},{7,2},{8,11},{9,12},{10,... | collective-permute-start | bytes 153608 | tf_op jit(solution)/shard_map/ppermute | solution.py:33
  11.8 1.6 %shard_map.75.upper = f32[1024,512]{1,0:T(8,128)S(1)} custom-call(f32[2048,512]{1,0:T(8,128)} %array.3, f32[8,128]{1,0:T(8,128)S(1)} %get-tuple-element.23.after), custom_call_target="tpu_custom_call" | custom-call | tf_op jit(solution)/shard_map/pallas_call | solution.py:80
  13.3 0.4 %collective-permute-done.2 = f16[200,128]{1,0:T(8,128)(2,1)S(1)} collective-permute-done((f16[200,128]{1,0:T(8,128)(2,1)S(1)}, f16[200,128]{1,0:T(8,128)(2,1)S(1)}, u32[]{:S(2)}, u32[]{:S(2)}) %collective-permute-start.2) | collective-permute-done | bytes 51232 | tf_op jit(solution)/shard_map/ppermute | solution.py:33
  14.0 1.7 %collective-permute-start.3 = (f16[200,128]{1,0:T(8,128)(2,1)S(1)}, f16[200,128]{1,0:T(8,128)(2,1)S(1)}, u32[]{:S(2)}, u32[]{:S(2)}) collective-permute-start(f16[200,128]{1,0:T(8,128)(2,1)S(1)} %get-tuple-element.29), channel_id=1, source_target_pairs={{0,5},{1,2},{2,1},{3,6},{4,7},{5,0},{6,3},{7,4},{8,13},{9,10},{10,... | collective-permute-start | bytes 153608 | tf_op jit(solution)/shard_map/ppermute | solution.py:33
  15.6 1.6 %shard_map.76.lower = f32[1024,512]{1,0:T(8,128)S(1)} custom-call(f32[2048,512]{1,0:T(8,128)} %array.3, f32[200,128]{1,0:T(8,128)S(1)} %get-tuple-element.30.after.own), custom_call_target="tpu_custom_call" | custom-call | tf_op jit(solution)/shard_map/pallas_call | solution.py:80
  17.2 0.4 %collective-permute-done.3 = f16[200,128]{1,0:T(8,128)(2,1)S(1)} collective-permute-done((f16[200,128]{1,0:T(8,128)(2,1)S(1)}, f16[200,128]{1,0:T(8,128)(2,1)S(1)}, u32[]{:S(2)}, u32[]{:S(2)}) %collective-permute-start.3) | collective-permute-done | bytes 51232 | tf_op jit(solution)/shard_map/ppermute | solution.py:33
  17.6 1.2 %shard_map.77 = f32[12,512]{1,0:T(8,128)S(1)} custom-call(f32[200,128]{1,0:T(8,128)S(1)} %get-tuple-element.30.after.own, f32[200,128]{1,0:T(8,128)S(1)} %convert_element_type.22.other, f32[1024,512]{1,0:T(8,128)S(1)} %shard_map.75.upper, f32[1024,512]{1,0:T(8,128)S(1)} %shard_map.76.lower), custom_call_target="tpu_custom_call" | custom-call | tf_op jit(solution)/shard_map/pallas_call | solution.py:254
  18.8 0.4 %collective-permute-start.4 = (f32[12,512]{1,0:T(8,128)S(1)}, f32[12,512]{1,0:T(8,128)S(1)}, u32[]{:S(2)}, u32[]{:S(2)}) collective-permute-start(f32[12,512]{1,0:T(8,128)S(1)} %shard_map.77), channel_id=1, source_target_pairs={{0,1},{1,0},{2,3},{3,2},{4,5},{5,4},{6,7},{7,6},{8,9},{9,8},{10,11... | collective-permute-start | bytes 73736 | tf_op jit(solution)/shard_map/ppermute | solution.py:33
  19.1 0.9 %collective-permute-done.4 = f32[12,512]{1,0:T(8,128)S(1)} collective-permute-done((f32[12,512]{1,0:T(8,128)S(1)}, f32[12,512]{1,0:T(8,128)S(1)}, u32[]{:S(2)}, u32[]{:S(2)}) %collective-permute-start.4) | collective-permute-done | bytes 24608 | tf_op jit(solution)/shard_map/ppermute | solution.py:33
  20.0 3.2 %collective-permute-start.5 = (bf16[48,128]{1,0:T(8,128)(2,1)S(1)}, bf16[48,128]{1,0:T(8,128)(2,1)S(1)}, u32[]{:S(2)}, u32[]{:S(2)}) collective-permute-start(bf16[48,128]{1,0:T(8,128)(2,1)S(1)} %reshape.84), channel_id=1, source_target_pairs={{0,9},{1,8},{2,11},{3,10},{4,13},{5,12},{6,15},{7,14},{8,1},{9,0},... | collective-permute-start | bytes 36872 | tf_op jit(solution)/shard_map/ppermute | solution.py:33
  23.2 1.4 %collective-permute-done.5 = bf16[48,128]{1,0:T(8,128)(2,1)S(1)} collective-permute-done((bf16[48,128]{1,0:T(8,128)(2,1)S(1)}, bf16[48,128]{1,0:T(8,128)(2,1)S(1)}, u32[]{:S(2)}, u32[]{:S(2)}) %collective-permute-start.5) | collective-permute-done | bytes 12320 | tf_op jit(solution)/shard_map/ppermute | solution.py:33
  24.6 1.3 %collective-permute-start.6 = (bf16[96,128]{1,0:T(8,128)(2,1)S(1)}, bf16[96,128]{1,0:T(8,128)(2,1)S(1)}, u32[]{:S(2)}, u32[]{:S(2)}) collective-permute-start(bf16[96,128]{1,0:T(8,128)(2,1)S(1)} %maximum_select_fusion.2), channel_id=1, source_target_pairs={{0,3},{1,4},{2,7},{3,0},{4,1},{5,6},{6,5},{7,2},{8,11},{9,12},{10,... | collective-permute-start | bytes 73736 | tf_op jit(solution)/shard_map/ppermute | solution.py:33
  25.9 2.0 %collective-permute-done.6 = bf16[96,128]{1,0:T(8,128)(2,1)S(1)} collective-permute-done((bf16[96,128]{1,0:T(8,128)(2,1)S(1)}, bf16[96,128]{1,0:T(8,128)(2,1)S(1)}, u32[]{:S(2)}, u32[]{:S(2)}) %collective-permute-start.6) | collective-permute-done | bytes 24608 | tf_op jit(solution)/shard_map/ppermute | solution.py:33
  27.9 1.7 %collective-permute-start.7 = (bf16[2,96,128]{2,1,0:T(8,128)(2,1)S(1)}, bf16[2,96,128]{2,1,0:T(8,128)(2,1)S(1)}, u32[]{:S(2)}, u32[]{:S(2)}) collective-permute-start(bf16[2,96,128]{2,1,0:T(8,128)(2,1)S(1)} %pad_maximum_fusion.5), channel_id=1, source_target_pairs={{0,5},{1,2},{2,1},{3,6},{4,7},{5,0},{6,3},{7,4},{8,13},{9,10},{10,... | collective-permute-start | bytes 147464 | tf_op jit(solution)/shard_map/ppermute | solution.py:33
  29.6 1.8 %collective-permute-done.7 = bf16[2,96,128]{2,1,0:T(8,128)(2,1)S(1)} collective-permute-done((bf16[2,96,128]{2,1,0:T(8,128)(2,1)S(1)}, bf16[2,96,128]{2,1,0:T(8,128)(2,1)S(1)}, u32[]{:S(2)}, u32[]{:S(2)}) %collective-permute-start.7) | collective-permute-done | bytes 49184 | tf_op jit(solution)/shard_map/ppermute | solution.py:33
  31.6 0.1 reshape_reshape.7
  31.7 0.1 copy.8
  31.7 0.1 reshape.86
  31.8 0.0 copy-done
  31.8 0.9 %fusion.3 = f32[12,64]{1,0:T(8,128)} fusion(bf16[12,4096]{1,0:T(8,128)(2,1)S(1)} %reshape.86, bf16[64,4096]{1,0:T(8,128)(2,1)S(1)} %copy-done), kind=kOutput, calls=%fused_computation.23 | convolution fusion | flops 6291456 | bytes 625664 | tf_op jit(solution)/shard_map/dot_general | solution.py:311
  (26 shorter events, 0.4 us)
Async XLA Ops:
  0.0 31.8 %copy-start = (bf16[64,4096]{1,0:T(8,128)(2,1)S(1)}, bf16[64,4096]{1,0:T(8,128)(2,1)}, u32[]{:S(2)}) copy-start(bf16[64,4096]{1,0:T(8,128)(2,1)} %param.13) | copy-start | bytes 1572868
  2.9 1.5 %collective-permute-start = (f32[128,128]{1,0:T(8,128)S(1)}, f32[128,128]{1,0:T(8,128)S(1)}, u32[]{:S(2)}, u32[]{:S(2)}) collective-permute-start(f32[128,128]{1,0:T(8,128)S(1)} %get-tuple-element.14.part), channel_id=1, source_target_pairs={{0,1},{1,0},{2,3},{3,2},{4,5},{5,4},{6,7},{7,6},{8,9},{9,8},{10,11... | collective-permute-start | bytes 196616 | tf_op jit(solution)/shard_map/ppermute | solution.py:33
  4.8 5.3 %collective-permute-start.1 = (f16[104,128]{1,0:T(8,128)(2,1)S(1)}, f16[104,128]{1,0:T(8,128)(2,1)S(1)}, u32[]{:S(2)}, u32[]{:S(2)}) collective-permute-start(f16[104,128]{1,0:T(8,128)(2,1)S(1)} %pad_maximum_fusion.6), channel_id=1, source_target_pairs={{0,9},{1,8},{2,11},{3,10},{4,13},{5,12},{6,15},{7,14},{8,1},{9,0},... | collective-permute-start | bytes 79880 | tf_op jit(solution)/shard_map/ppermute | solution.py:33
  10.2 3.6 %collective-permute-start.2 = (f16[200,128]{1,0:T(8,128)(2,1)S(1)}, f16[200,128]{1,0:T(8,128)(2,1)S(1)}, u32[]{:S(2)}, u32[]{:S(2)}) collective-permute-start(f16[200,128]{1,0:T(8,128)(2,1)S(1)} %pad_maximum_fusion.4), channel_id=1, source_target_pairs={{0,3},{1,4},{2,7},{3,0},{4,1},{5,6},{6,5},{7,2},{8,11},{9,12},{10,... | collective-permute-start | bytes 153608 | tf_op jit(solution)/shard_map/ppermute | solution.py:33
  14.0 3.6 %collective-permute-start.3 = (f16[200,128]{1,0:T(8,128)(2,1)S(1)}, f16[200,128]{1,0:T(8,128)(2,1)S(1)}, u32[]{:S(2)}, u32[]{:S(2)}) collective-permute-start(f16[200,128]{1,0:T(8,128)(2,1)S(1)} %get-tuple-element.29), channel_id=1, source_target_pairs={{0,5},{1,2},{2,1},{3,6},{4,7},{5,0},{6,3},{7,4},{8,13},{9,10},{10,... | collective-permute-start | bytes 153608 | tf_op jit(solution)/shard_map/ppermute | solution.py:33
  18.8 1.2 %collective-permute-start.4 = (f32[12,512]{1,0:T(8,128)S(1)}, f32[12,512]{1,0:T(8,128)S(1)}, u32[]{:S(2)}, u32[]{:S(2)}) collective-permute-start(f32[12,512]{1,0:T(8,128)S(1)} %shard_map.77), channel_id=1, source_target_pairs={{0,1},{1,0},{2,3},{3,2},{4,5},{5,4},{6,7},{7,6},{8,9},{9,8},{10,11... | collective-permute-start | bytes 73736 | tf_op jit(solution)/shard_map/ppermute | solution.py:33
  20.0 4.6 %collective-permute-start.5 = (bf16[48,128]{1,0:T(8,128)(2,1)S(1)}, bf16[48,128]{1,0:T(8,128)(2,1)S(1)}, u32[]{:S(2)}, u32[]{:S(2)}) collective-permute-start(bf16[48,128]{1,0:T(8,128)(2,1)S(1)} %reshape.84), channel_id=1, source_target_pairs={{0,9},{1,8},{2,11},{3,10},{4,13},{5,12},{6,15},{7,14},{8,1},{9,0},... | collective-permute-start | bytes 36872 | tf_op jit(solution)/shard_map/ppermute | solution.py:33
  24.6 3.3 %collective-permute-start.6 = (bf16[96,128]{1,0:T(8,128)(2,1)S(1)}, bf16[96,128]{1,0:T(8,128)(2,1)S(1)}, u32[]{:S(2)}, u32[]{:S(2)}) collective-permute-start(bf16[96,128]{1,0:T(8,128)(2,1)S(1)} %maximum_select_fusion.2), channel_id=1, source_target_pairs={{0,3},{1,4},{2,7},{3,0},{4,1},{5,6},{6,5},{7,2},{8,11},{9,12},{10,... | collective-permute-start | bytes 73736 | tf_op jit(solution)/shard_map/ppermute | solution.py:33
  27.9 3.5 %collective-permute-start.7 = (bf16[2,96,128]{2,1,0:T(8,128)(2,1)S(1)}, bf16[2,96,128]{2,1,0:T(8,128)(2,1)S(1)}, u32[]{:S(2)}, u32[]{:S(2)}) collective-permute-start(bf16[2,96,128]{2,1,0:T(8,128)(2,1)S(1)} %pad_maximum_fusion.5), channel_id=1, source_target_pairs={{0,5},{1,2},{2,1},{3,6},{4,7},{5,0},{6,3},{7,4},{8,13},{9,10},{10,... | collective-permute-start | bytes 147464 | tf_op jit(solution)/shard_map/ppermute | solution.py:33

commit v6 on v5

--- a/solution.py
+++ b/solution.py
@@ -61,59 +61,57 @@
     return [pltpu.with_memory_space_constraint(array, space) for array in arrays]
 
 
-def fetch_kernel(start, pieces, array, after, out, sems):
-    rows = out.shape[0] // pieces
+def split(array):
+    high = array.astype(jnp.bfloat16)
+    return high, (array - high.astype(jnp.float32)).astype(jnp.bfloat16)
+
+
+def fetch_kernel(start, chunk, array, after, high, low, rows, sems):
+    parts = [pl.ds(n * chunk, chunk) for n in range(rows.shape[0] // chunk)]
     copies = [
-        pltpu.make_async_copy(
-            array.at[pl.ds(start + n * rows, rows), :], out.at[pl.ds(n * rows, rows), :], sems.at[n]
-        )
-        for n in range(pieces)
+        pltpu.make_async_copy(array.at[pl.ds(start + n * chunk, chunk), :], rows.at[part, :], sems.at[n])
+        for n, part in enumerate(parts)
     ]
     for copy in copies:
         copy.start()
-    for copy in copies:
+    for copy, part in zip(copies, parts):
         copy.wait()
+        high[part, :], low[part, :] = split(rows[part, :])
 
 
 def fetch(array, start, rows, after):
-    pieces = 2
-    return pl.pallas_call(
-        functools.partial(fetch_kernel, start, pieces),
-        out_shape=pltpu.VMEM((rows, array.shape[1]), array.dtype),
-        in_specs=[pl.BlockSpec(memory_space=pltpu.HBM), pl.BlockSpec(memory_space=pltpu.VMEM)],
-        out_specs=pl.BlockSpec(memory_space=pltpu.VMEM),
-        scratch_shapes=[pltpu.SemaphoreType.DMA((pieces,))],
+    chunk = LANES
+    vmem = pl.BlockSpec(memory_space=pltpu.VMEM)
+    shape = (rows, array.shape[1])
+    return pl.pallas_call(
+        functools.partial(fetch_kernel, start, chunk),
+        out_shape=(pltpu.VMEM(shape, jnp.bfloat16), pltpu.VMEM(shape, jnp.bfloat16)),
+        in_specs=[pl.BlockSpec(memory_space=pltpu.HBM), vmem],
+        out_specs=(vmem, vmem),
+        scratch_shapes=[
+            pltpu.VMEM(shape, array.dtype),
+            pltpu.SemaphoreType.DMA((rows // chunk,)),
+        ],
         compiler_params=pltpu.CompilerParams(vmem_limit_bytes=VMEM_LIMIT),
     )(*kept(pltpu.HBM, array), *kept(pltpu.VMEM, after))
 
 
-def project_kernel(chunks, ids_hbm, act_hbm, pin_hbm, grad_hbm, pout_hbm, out, mask, numbers, ids, act, pin, grad, pout, sems):
-    depth = grad.shape[1] // chunks
-    copies = [
-        pltpu.make_async_copy(act_hbm, act, sems.at[0]),
-        pltpu.make_async_copy(pin_hbm, pin, sems.at[1]),
+def project_kernel(cuts, ids_hbm, act_hbm, pin_hbm, grad_hbm, pout_hbm, out, mask, numbers, ids, act, pin, grad, pout, sems):
+    copies = []
+
+    def copy(source, target):
+        copies.append(pltpu.make_async_copy(source, target, sems.at[len(copies)]))
+        copies[-1].start()
+        return copies[-1]
+
+    tokens = copy(ids_hbm, ids)
+    left = (copy(pin_hbm, pin), copy(act_hbm, act))
+    parts = [pl.ds(start, stop - start) for start, stop in zip(cuts, cuts[1:])]
+    right = [
+        (copy(pout_hbm.at[:, part], pout.at[:, part]), copy(grad_hbm.at[:, part], grad.at[:, part]))
+        for part in parts
     ]
-    for n in range(chunks):
-        part = pl.ds(n * depth, depth)
-        copies.append(pltpu.make_async_copy(pout_hbm.at[:, part], pout.at[:, part], sems.at[2 + 2 * n]))
-        copies.append(pltpu.make_async_copy(grad_hbm.at[:, part], grad.at[:, part], sems.at[3 + 2 * n]))
-    copies.append(pltpu.make_async_copy(ids_hbm, ids, sems.at[2 + 2 * chunks]))
-    for copy in copies:
-        copy.start()
-    rank = pin.shape[0]
-    dims = (((1,), (1,)), ((), ()))
-    copies[0].wait()
-    copies[1].wait()
-    out[:rank, :] = lax.dot_general(pin[...], act[...], dims, preferred_element_type=jnp.float32)
-    total = None
-    for n in range(chunks):
-        copies[2 + 2 * n].wait()
-        copies[3 + 2 * n].wait()
-        part = pl.ds(n * depth, depth)
-        term = lax.dot_general(pout[:, part], grad[:, part], dims, preferred_element_type=jnp.float32)
-        total = term if total is None else total + term
-    out[rank:, :] = total
-    copies[-1].wait()
+    tokens.wait()
     rows = lax.broadcasted_iota(jnp.int32, mask.shape, 0)
     first = jnp.broadcast_to(ids[:, :1], mask.shape)
     mask[...] = (jnp.broadcast_to(ids[...], mask.shape) - first == rows).astype(jnp.float32)
@@ -124,16 +122,28 @@
     value = jnp.where(row < 4, first + place, 1)
     owned = (place >= 0) & (place < SLOTS) & (row % 4 < 2)
     numbers[...] = jnp.where(owned, value, 0).astype(jnp.float32)
+    rank = pin.shape[0]
+    dims = (((1,), (1,)), ((), ()))
+    for piece in left:
+        piece.wait()
+    out[:rank, :] = lax.dot_general(pin[...], act[...], dims, preferred_element_type=jnp.float32)
+    total = None
+    for part, pair in zip(parts, right):
+        for piece in pair:
+            piece.wait()
+        term = lax.dot_general(pout[:, part], grad[:, part], dims, preferred_element_type=jnp.float32)
+        total = term if total is None else total + term
+    out[rank:, :] = total
 
 
 def project(activations, gradients, proj_in, proj_out, doc_ids):
     tokens, depth = gradients.shape
     rank = proj_in.shape[1]
-    chunks = max(n for n in (4, 2, 1) if depth % (n * LANES) == 0)
+    cuts = [depth * n // 14 // LANES * LANES for n in (0, 5, 9, 12, 13, 14)]
     hbm = pl.BlockSpec(memory_space=pltpu.HBM)
     vmem = pl.BlockSpec(memory_space=pltpu.VMEM)
     return pl.pallas_call(
-        functools.partial(project_kernel, chunks),
+        functools.partial(project_kernel, cuts),
         out_shape=(
             pltpu.VMEM((2 * rank, tokens), jnp.float32),
             pltpu.VMEM((8, tokens), jnp.float32),
@@ -147,7 +157,7 @@
             pltpu.VMEM(proj_in.shape[::-1], jnp.bfloat16),
             pltpu.VMEM(gradients.shape, jnp.bfloat16),
             pltpu.VMEM(proj_out.shape[::-1], jnp.bfloat16),
-            pltpu.SemaphoreType.DMA((3 + 2 * chunks,)),
+            pltpu.SemaphoreType.DMA((1 + 2 * len(cuts),)),
         ],
         compiler_params=pltpu.CompilerParams(vmem_limit_bytes=VMEM_LIMIT),
     )(*kept(pltpu.HBM, doc_ids.reshape(1, tokens), activations, proj_in.T, gradients, proj_out.T))
@@ -195,13 +205,9 @@
     )(*kept(pltpu.VMEM, part, other, mask, numbers))
 
 
-def split(array):
-    high = array.astype(jnp.bfloat16)
-    return high, (array - high.astype(jnp.float32)).astype(jnp.bfloat16)
-
-
-def precondition_kernel(own, other, upper, lower, out, pieces):
-    depth = 2 * upper.shape[0]
+def precondition_kernel(windows, own, other, *refs):
+    highs, lows, (out, pieces) = refs[:windows], refs[windows : 2 * windows], refs[2 * windows :]
+    depth = pieces.shape[1]
     size = own.shape[0] - 8
     count = size * LANES // depth
     room = pieces.shape[0] // 2
@@ -211,18 +217,18 @@
             pieces[pl.ds(n * room, count), pl.ds(k * LANES, LANES)] = part[
                 pl.ds(k, count, stride=depth // LANES), :
             ]
-    step = 2 * LANES if depth % (4 * LANES) == 0 else LANES
-    total = None
-    for n in range(depth // step):
-        high, low = split(pieces[:, pl.ds(n * step, step)])
-        half, row = divmod(n * step, depth // 2)
-        weights_high, weights_low = split((upper, lower)[half][pl.ds(row, step), :])
-        first = jnp.dot(
-            jnp.concatenate([high, low]), weights_high, preferred_element_type=jnp.float32
+    first, second, at = None, None, 0
+    for weights_high, weights_low in zip(highs, lows):
+        rows = weights_high.shape[0]
+        high, low = split(pieces[:, pl.ds(at, rows)])
+        term = jnp.dot(
+            jnp.concatenate([high, low]), weights_high[...], preferred_element_type=jnp.float32
         )
-        second = jnp.dot(high, weights_low, preferred_element_type=jnp.float32)
-        term = first[: 2 * room] + (first[2 * room :] + second)
-        total = term if total is None else total + term
+        first = term if first is None else first + term
+        term = jnp.dot(high, weights_low[...], preferred_element_type=jnp.float32)
+        second = term if second is None else second + term
+        at += rows
+    total = first[: 2 * room] + (first[2 * room :] + second)
     docs = lax.broadcasted_iota(jnp.int32, (out.shape[0], count), 0).astype(jnp.float32)
     result = None
     for n, part in enumerate((own, other)):
@@ -247,18 +253,88 @@
     out[...] = result
 
 
-def precondition(own, other, upper, lower, doc_count):
-    vmem = pl.BlockSpec(memory_space=pltpu.VMEM)
-    depth, width = 2 * upper.shape[0], upper.shape[1]
+def precondition(own, other, highs, lows, doc_count):
+    vmem = pl.BlockSpec(memory_space=pltpu.VMEM)
+    depth, width = sum(high.shape[0] for high in highs), highs[0].shape[1]
     count = (own.shape[0] - 8) * LANES // depth
     return pl.pallas_call(
-        precondition_kernel,
+        functools.partial(precondition_kernel, len(highs)),
         out_shape=pltpu.VMEM((doc_count, width), jnp.float32),
-        in_specs=[vmem] * 4,
+        in_specs=[vmem] * (2 + 2 * len(highs)),
         out_specs=vmem,
         scratch_shapes=[pltpu.VMEM((2 * pl.cdiv(count, 8) * 8, depth), jnp.float32)],
         compiler_params=pltpu.CompilerParams(vmem_limit_bytes=VMEM_LIMIT),
-    )(*kept(pltpu.VMEM, own, other, upper, lower))
+    )(*kept(pltpu.VMEM, own, other, *highs, *lows))
+
+
+def load_kernel(source, after, target, sem):
+    copy = pltpu.make_async_copy(source, target, sem)
+    copy.start()
+    copy.wait()
+
+
+def load(array, after):
+    vmem = pl.BlockSpec(memory_space=pltpu.VMEM)
+    return pl.pallas_call(
+        load_kernel,
+        out_shape=pltpu.VMEM(array.shape, array.dtype),
+        in_specs=[pl.BlockSpec(memory_space=pltpu.HBM), vmem],
+        out_specs=vmem,
+        scratch_shapes=[pltpu.SemaphoreType.DMA],
+        compiler_params=pltpu.CompilerParams(vmem_limit_bytes=VMEM_LIMIT),
+    )(*kept(pltpu.HBM, array), *kept(pltpu.VMEM, after))
+
+
+def score_kernel(width, mine, theirs, store, out, products):
+    pieces = width // LANES
+    count = store.shape[0]
+    rows = out.shape[0] * pieces
+    chunk = mine.shape[0] // 2
+    held = chunk // rows
+    bits = held.bit_length() - 1
+    c, p = lax.axis_index("ctx"), lax.axis_index("col")
+    first, second = (near_distance(c, p, last) for last in (0, 1))
+    total = None
+    for part, n, offset in ((mine, 0, 0), (mine, 1, first), (theirs, 0, second), (theirs, 1, 3)):
+        low = (c & 3) ^ offset
+        blocks, columns = [], [[] for _ in range(pieces)]
+        for place in range(held):
+            high = sum(((place >> k) & 1) << (bits - 1 - k) for k in range(bits))
+            start = (high * 4 + low) * width
+            blocks.append(part[pl.ds(n * chunk + place * rows, rows), :])
+            for k in range(pieces):
+                at = pl.multiple_of(start + k * LANES, LANES)
+                columns[k].append(store[:, pl.ds(at, LANES)])
+        left = jnp.concatenate(blocks, 1)
+        right = jnp.concatenate([jnp.concatenate(column, 1) for column in columns])
+        term = lax.dot_general(
+            left, right, (((1,), (1,)), ((), ())), preferred_element_type=jnp.float32
+        )
+        total = term if total is None else total + term
+    for n in range(products.shape[0] // rows):
+        products[pl.ds(n * rows, rows), :] = total[:, n * LANES : (n + 1) * LANES]
+    result = None
+    for k in range(pieces):
+        slab, lane = divmod(k * count, LANES)
+        lines = products[pl.ds(slab * rows + k, rows // pieces, stride=pieces), :]
+        term = lines[:, lane : lane + count]
+        result = term if result is None else result + term
+    out[...] = result
+
+
+def score(mine, theirs, store, width, doc_count):
+    vmem = pl.BlockSpec(memory_space=pltpu.VMEM)
+    pieces = width // LANES
+    return pl.pallas_call(
+        functools.partial(score_kernel, width),
+        out_shape=jax.ShapeDtypeStruct((doc_count, store.shape[0]), jnp.float32),
+        in_specs=[vmem] * 3,
+        out_specs=vmem,
+        scratch_shapes=[
+            pltpu.VMEM((doc_count * pieces * (pieces * store.shape[0] // LANES), LANES), jnp.float32)
+        ],
+        compiler_params=pltpu.CompilerParams(vmem_limit_bytes=VMEM_LIMIT),
+    )(*kept(pltpu.VMEM, mine, theirs, store))
 
 
 def shards(activations, gradients, doc_ids, proj_in, proj_out, inverse, store_rows):
@@ -269,34 +345,57 @@
     part, mask, numbers = project(activations, gradients, proj_in, proj_out, doc_ids)
     sums, tags = outer(part, swap_cores(part), mask, numbers)
     blocks, tags = sums.astype(jnp.float16), tags.astype(jnp.float16)
+    depth = inverse.shape[0]
+    cuts = [0] + [depth * k // 8 // LANES * LANES for k in ((2, 5) if far_distances() else (4,))] + [depth]
+    highs, lows = [], []
+
+    def beside(exchange, payload, ready):
+        other, at = exchange(payload), len(highs)
+        pair = fetch(inverse, cuts[at], cuts[at + 1] - cuts[at], ready)
+        other, high, low = lax.optimization_barrier((other, *pair))
+        highs.append(high)
+        lows.append(low)
+        return other
+
     for distance in far_distances():
         size = blocks.shape[0]
-        other = swap_far(jnp.concatenate([blocks, tags]), distance)
+        exchange = functools.partial(swap_far, distance=distance)
+        payload = jnp.concatenate([blocks, tags])
+        if distance == far_distances()[-1]:
+            other = beside(exchange, payload, tags.astype(jnp.float32))
+        else:
+            other = exchange(payload)
         blocks = ordered(blocks, other[:size], distance)
         tags = tags + other[size:]
-    rows = inverse.shape[0] // 2
     size = blocks.shape[0]
-    other = swap_near(jnp.concatenate([blocks, tags]), 0)
-    upper = fetch(inverse, 0, rows, tags.astype(jnp.float32))
-    other, upper = lax.optimization_barrier((other, upper))
+    payload = jnp.concatenate([blocks, tags])
+    other = beside(functools.partial(swap_near, last=0), payload, tags.astype(jnp.float32))
     blocks = jnp.concatenate([blocks, other[:size]])
     tags = tags + jnp.roll(other[size:], 2, 0)
     halves = blocks.reshape(-1, 2, half * rank // LANES, LANES)
     first = lax.axis_index("col") == 0
     own = jnp.where(first, halves[:, 0], halves[:, 1]).reshape(-1, LANES)
     others = jnp.where(first, halves[:, 1], halves[:, 0]).reshape(-1, LANES)
-    payload = jnp.concatenate([own, tags]).astype(jnp.float32)
-    other = swap_near(jnp.concatenate([others, tags]), 1)
-    lower = fetch(inverse, rows, rows, payload)
-    other, lower = lax.optimization_barrier((other, lower))
-    partial_q = precondition(payload, other.astype(jnp.float32), upper, lower, doc_count)
+    own = jnp.concatenate([own, tags]).astype(jnp.float32)
+    other = beside(functools.partial(swap_near, last=1), jnp.concatenate([others, tags]), own)
+    partial_q = precondition(own, other.astype(jnp.float32), highs, lows, doc_count)
     precond = (partial_q + swap_cores(partial_q)).astype(jnp.bfloat16)
     width = precond.shape[1]
     whole = precond.reshape(-1, min(width, LANES))
-    for distance in far_distances():
-        whole = ordered(whole, swap_far(whole, distance), distance)
-    whole = jnp.stack([whole, swap_near(whole, 0)])
-    (own, near), (next_one, farthest) = whole, swap_near(whole, 1)
+    count = store_rows.shape[0]
+    direct = width % LANES == 0 and LANES % count == 0 and width * count % LANES**2 == 0
+    if direct:
+        store = load(store_rows, whole)
+    for step, distance in enumerate(far_distances()):
+        other = swap_far(whole, distance)
+        if direct and step == 0:
+            other, store = lax.optimization_barrier((other, store))
+        whole = ordered(whole, other, distance)
+    whole = jnp.concatenate([whole, swap_near(whole, 0)])
+    others = swap_near(whole, 1)
+    if direct:
+        return score(whole, others, store, width, doc_count)
+    (own, near), (next_one, farthest) = (x.reshape(2, -1, x.shape[1]) for x in (whole, others))
     c, p = lax.axis_index("ctx"), lax.axis_index("col")
     single = near_distance(c, p, 0) == 1
     near, next_one = jnp.where(single, near, next_one), jnp.where(single, next_one, near)

time: 32.8 us -> 32.4 us (0.988)
  Pallas kernels: 7.58 us -> 10.3 us
  waiting for transfers between devices: 9.29 us -> 7.23 us
  matrix products: 0.85 us -> 0 us
    pallas_call x4 -> x7, Pallas kernels: 7.22 us -> 9.99 us  [the longest x3 4.13 us: fetch(): pl.pallas_call(functools.partial(fetch_kernel, start, chunk), out_shape=(...]
    ppermute x8, waiting for transfers between devices: 9.29 us -> 7.23 us  [swap(): return lax.ppermute(block, ('ctx', 'col'), route)]
    dot_general x1 -> x0, matrix products: 0.85 us -> none  [shards(): lax.dot_general(whole, store_rows, (((1,), (1,)), ((), ())), preferred_el...]
  transfers between devices with their start and end apart: 8 -> 8, of which waited for: 8 -> 8; matrix products, arithmetic and copies ran while one was open for 0% -> 0% of each run, Pallas kernels for 10% -> 16%
where the time goes in v6:
time: 32.4 us; the launch traced here: 32.1 us
  starting transfers between devices  14.1 us (44%)
  Pallas kernels  10.3 us (32%)
  waiting for transfers between devices  7.23 us (22%)
    ppermute x8, starting transfers between devices, swap(): return lax.ppermute(block, ('ctx', 'col'), route)  14.1 us
    ppermute x8, waiting for transfers between devices, swap(): return lax.ppermute(block, ('ctx', 'col'), route)  7.23 us
    pallas_call x3, Pallas kernels, fetch(): pl.pallas_call(functools.partial(fetch_kernel, start, chunk), out_shape=(...  4.13 us
    pallas_call x1, Pallas kernels, project(): pl.pallas_call(functools.partial(project_kernel, cuts), out_shape=(pltpu....  2.83 us
    pallas_call x1, Pallas kernels, load(): pl.pallas_call(load_kernel, out_shape=pltpu.VMEM(array.shape, array.dtype...  1.05 us
    pallas_call x1, Pallas kernels, precondition(): pl.pallas_call(functools.partial(precondition_kernel, len(highs)), out_sh...  1.02 us
    pallas_call x1, Pallas kernels, score(): pl.pallas_call(functools.partial(score_kernel, width), out_shape=jax.Shap...  0.96 us
  transfers between devices with their start and end apart: 8, of which 8 were waited for; matrix products, arithmetic and copies ran while one was open for 0% of the time, Pallas kernels for 16%

profile of v6, /device:TPU:0, one launch (start us, length us, event | category | flops | bytes accessed | tf_op | source)
XLA Modules:
  0.0 32.1 jit_solution(9472627500680995884)
XLA Ops:
  0.0 2.8 %shard_map.73 = (f32[128,128]{1,0:T(8,128)S(1)}, f32[8,128]{1,0:T(8,128)S(1)}, f32[8,128]{1,0:T(8,128)S(1)}) custom-call(s32[1,128]{1,0:T(1,128)} %bitcast.11, bf16[128,2048]{1,0:T(8,128)(2,1)} %act_hbm.1, bf16[64,2048]{1,0:T(8,128)(2,1)} %bitcast.8, bf16[128,7168]{1,0:T(8,128)(2,1)} %grad_hbm.1, bf16[64,7168]{1,0:T(8,128)(2,1)} %bitcast.6), custom_call_target="tpu_custom_call" | custom-call | tf_op jit(solution)/shard_map/pallas_call | solution.py:145
  2.8 0.6 %collective-permute-start = (f32[128,128]{1,0:T(8,128)S(1)}, f32[128,128]{1,0:T(8,128)S(1)}, u32[]{:S(2)}, u32[]{:S(2)}) collective-permute-start(f32[128,128]{1,0:T(8,128)S(1)} %get-tuple-element.27.part), channel_id=1, source_target_pairs={{0,1},{1,0},{2,3},{3,2},{4,5},{5,4},{6,7},{7,6},{8,9},{9,8},{10,11... | collective-permute-start | bytes 196616 | tf_op jit(solution)/shard_map/ppermute | solution.py:33
  3.4 0.9 %collective-permute-done.other = f32[128,128]{1,0:T(8,128)S(1)} collective-permute-done((f32[128,128]{1,0:T(8,128)S(1)}, f32[128,128]{1,0:T(8,128)S(1)}, u32[]{:S(2)}, u32[]{:S(2)}) %collective-permute-start) | collective-permute-done | bytes 65568 | tf_op jit(solution)/shard_map/ppermute | solution.py:33
  4.3 0.4 %shard_map.74 = (f32[96,128]{1,0:T(8,128)S(1)}, f32[8,128]{1,0:T(8,128)S(1)}) custom-call(f32[128,128]{1,0:T(8,128)S(1)} %get-tuple-element.27.part, f32[128,128]{1,0:T(8,128)S(1)} %collective-permute-done.other, f32[8,128]{1,0:T(8,128)S(1)} %get-tuple-element.28.mask, f32[8,128]{1,0:T(8,128)S(1)} %get-tuple-element.29.numbers), custom_call_target="tpu_custom_call" | custom-call | tf_op jit(solution)/shard_map/pallas_call | solution.py:195
  4.7 3.8 %collective-permute-start.1 = (f16[104,128]{1,0:T(8,128)(2,1)S(1)}, f16[104,128]{1,0:T(8,128)(2,1)S(1)}, u32[]{:S(2)}, u32[]{:S(2)}) collective-permute-start(f16[104,128]{1,0:T(8,128)(2,1)S(1)} %pad_maximum_fusion.5), channel_id=1, source_target_pairs={{0,9},{1,8},{2,11},{3,10},{4,13},{5,12},{6,15},{7,14},{8,1},{9,0},... | collective-permute-start | bytes 79880 | tf_op jit(solution)/shard_map/ppermute | solution.py:33
  8.5 1.3 %shard_map.75 = (bf16[512,512]{1,0:T(8,128)(2,1)S(1)}, bf16[512,512]{1,0:T(8,128)(2,1)S(1)}) custom-call(f32[2048,512]{1,0:T(8,128)} %array.5, f32[8,128]{1,0:T(8,128)S(1)} %get-tuple-element.51.after), custom_call_target="tpu_custom_call" | custom-call | tf_op jit(solution)/shard_map/pallas_call | solution.py:86
  9.7 0.3 collective-permute-done.1
  10.1 1.6 %collective-permute-start.2 = (f16[200,128]{1,0:T(8,128)(2,1)S(1)}, f16[200,128]{1,0:T(8,128)(2,1)S(1)}, u32[]{:S(2)}, u32[]{:S(2)}) collective-permute-start(f16[200,128]{1,0:T(8,128)(2,1)S(1)} %pad_maximum_fusion.3), channel_id=1, source_target_pairs={{0,3},{1,4},{2,7},{3,0},{4,1},{5,6},{6,5},{7,2},{8,11},{9,12},{10,... | collective-permute-start | bytes 153608 | tf_op jit(solution)/shard_map/ppermute | solution.py:33
  11.7 1.4 %shard_map.76 = (bf16[768,512]{1,0:T(8,128)(2,1)S(1)}, bf16[768,512]{1,0:T(8,128)(2,1)S(1)}) custom-call(f32[2048,512]{1,0:T(8,128)} %array.5, f32[8,128]{1,0:T(8,128)S(1)} %get-tuple-element.49.after), custom_call_target="tpu_custom_call" | custom-call | tf_op jit(solution)/shard_map/pallas_call | solution.py:86
  13.1 0.6 %collective-permute-done.2 = f16[200,128]{1,0:T(8,128)(2,1)S(1)} collective-permute-done((f16[200,128]{1,0:T(8,128)(2,1)S(1)}, f16[200,128]{1,0:T(8,128)(2,1)S(1)}, u32[]{:S(2)}, u32[]{:S(2)}) %collective-permute-start.2) | collective-permute-done | bytes 51232 | tf_op jit(solution)/shard_map/ppermute | solution.py:33
  13.9 1.7 %collective-permute-start.3 = (f16[200,128]{1,0:T(8,128)(2,1)S(1)}, f16[200,128]{1,0:T(8,128)(2,1)S(1)}, u32[]{:S(2)}, u32[]{:S(2)}) collective-permute-start(f16[200,128]{1,0:T(8,128)(2,1)S(1)} %get-tuple-element.55), channel_id=1, source_target_pairs={{0,5},{1,2},{2,1},{3,6},{4,7},{5,0},{6,3},{7,4},{8,13},{9,10},{10,... | collective-permute-start | bytes 153608 | tf_op jit(solution)/shard_map/ppermute | solution.py:33
  15.5 1.4 %shard_map.77 = (bf16[768,512]{1,0:T(8,128)(2,1)S(1)}, bf16[768,512]{1,0:T(8,128)(2,1)S(1)}) custom-call(f32[2048,512]{1,0:T(8,128)} %array.5, f32[200,128]{1,0:T(8,128)S(1)} %get-tuple-element.56.after.own), custom_call_target="tpu_custom_call" | custom-call | tf_op jit(solution)/shard_map/pallas_call | solution.py:86
  17.0 0.5 %collective-permute-done.3 = f16[200,128]{1,0:T(8,128)(2,1)S(1)} collective-permute-done((f16[200,128]{1,0:T(8,128)(2,1)S(1)}, f16[200,128]{1,0:T(8,128)(2,1)S(1)}, u32[]{:S(2)}, u32[]{:S(2)}) %collective-permute-start.3) | collective-permute-done | bytes 51232 | tf_op jit(solution)/shard_map/ppermute | solution.py:33
  17.5 1.0 %shard_map.78 = f32[12,512]{1,0:T(8,128)S(1)} custom-call(f32[200,128]{1,0:T(8,128)S(1)} %get-tuple-element.56.after.own, f32[200,128]{1,0:T(8,128)S(1)} %convert_element_type.26.other, bf16[512,512]{1,0:T(8,128)(2,1)S(1)} %get-tuple-element.41.refs_0_, bf16[768,512]{1,0:T(8,128)(2,1)S(1)} %get-tuple-element.42.refs_1_, ...), custom_call_target="tpu_custom_call" | custom-call | tf_op jit(solution)/shard_map/pallas_call | solution.py:260
  18.5 0.4 %collective-permute-start.4 = (f32[12,512]{1,0:T(8,128)S(1)}, f32[12,512]{1,0:T(8,128)S(1)}, u32[]{:S(2)}, u32[]{:S(2)}) collective-permute-start(f32[12,512]{1,0:T(8,128)S(1)} %shard_map.78), channel_id=1, source_target_pairs={{0,1},{1,0},{2,3},{3,2},{4,5},{5,4},{6,7},{7,6},{8,9},{9,8},{10,11... | collective-permute-start | bytes 73736 | tf_op jit(solution)/shard_map/ppermute | solution.py:33
  18.9 0.9 %collective-permute-done.4 = f32[12,512]{1,0:T(8,128)S(1)} collective-permute-done((f32[12,512]{1,0:T(8,128)S(1)}, f32[12,512]{1,0:T(8,128)S(1)}, u32[]{:S(2)}, u32[]{:S(2)}) %collective-permute-start.4) | collective-permute-done | bytes 24608 | tf_op jit(solution)/shard_map/ppermute | solution.py:33
  19.8 3.2 %collective-permute-start.5 = (bf16[48,128]{1,0:T(8,128)(2,1)S(1)}, bf16[48,128]{1,0:T(8,128)(2,1)S(1)}, u32[]{:S(2)}, u32[]{:S(2)}) collective-permute-start(bf16[48,128]{1,0:T(8,128)(2,1)S(1)} %reshape.21.after), channel_id=1, source_target_pairs={{0,9},{1,8},{2,11},{3,10},{4,13},{5,12},{6,15},{7,14},{8,1},{9,0},... | collective-permute-start | bytes 36872 | tf_op jit(solution)/shard_map/ppermute | solution.py:33
  22.9 1.0 %shard_map.79.store = bf16[64,4096]{1,0:T(8,128)(2,1)S(1)} custom-call(bf16[64,4096]{1,0:T(8,128)(2,1)} %source.1, bf16[48,128]{1,0:T(8,128)(2,1)S(1)} %reshape.21.after), custom_call_target="tpu_custom_call" | custom-call | tf_op jit(solution)/shard_map/pallas_call | solution.py:278
  24.0 0.3 %collective-permute-done.5 = bf16[48,128]{1,0:T(8,128)(2,1)S(1)} collective-permute-done((bf16[48,128]{1,0:T(8,128)(2,1)S(1)}, bf16[48,128]{1,0:T(8,128)(2,1)S(1)}, u32[]{:S(2)}, u32[]{:S(2)}) %collective-permute-start.5) | collective-permute-done | bytes 12320 | tf_op jit(solution)/shard_map/ppermute | solution.py:33
  24.3 1.3 %collective-permute-start.6 = (bf16[96,128]{1,0:T(8,128)(2,1)S(1)}, bf16[96,128]{1,0:T(8,128)(2,1)S(1)}, u32[]{:S(2)}, u32[]{:S(2)}) collective-permute-start(bf16[96,128]{1,0:T(8,128)(2,1)S(1)} %maximum_select_fusion.1), channel_id=1, source_target_pairs={{0,3},{1,4},{2,7},{3,0},{4,1},{5,6},{6,5},{7,2},{8,11},{9,12},{10,... | collective-permute-start | bytes 73736 | tf_op jit(solution)/shard_map/ppermute | solution.py:33
  25.6 2.0 %collective-permute-done.6 = bf16[96,128]{1,0:T(8,128)(2,1)S(1)} collective-permute-done((bf16[96,128]{1,0:T(8,128)(2,1)S(1)}, bf16[96,128]{1,0:T(8,128)(2,1)S(1)}, u32[]{:S(2)}, u32[]{:S(2)}) %collective-permute-start.6) | collective-permute-done | bytes 24608 | tf_op jit(solution)/shard_map/ppermute | solution.py:33
  27.7 1.7 %collective-permute-start.7 = (bf16[192,128]{1,0:T(8,128)(2,1)S(1)}, bf16[192,128]{1,0:T(8,128)(2,1)S(1)}, u32[]{:S(2)}, u32[]{:S(2)}) collective-permute-start(bf16[192,128]{1,0:T(8,128)(2,1)S(1)} %pad_maximum_fusion.4.mine), channel_id=1, source_target_pairs={{0,5},{1,2},{2,1},{3,6},{4,7},{5,0},{6,3},{7,4},{8,13},{9,10},{10,... | collective-permute-start | bytes 147464 | tf_op jit(solution)/shard_map/ppermute | solution.py:33
  29.4 1.8 %collective-permute-done.7.theirs = bf16[192,128]{1,0:T(8,128)(2,1)S(1)} collective-permute-done((bf16[192,128]{1,0:T(8,128)(2,1)S(1)}, bf16[192,128]{1,0:T(8,128)(2,1)S(1)}, u32[]{:S(2)}, u32[]{:S(2)}) %collective-permute-start.7) | collective-permute-done | bytes 49184 | tf_op jit(solution)/shard_map/ppermute | solution.py:33
  31.2 1.0 %shard_map.80 = f32[12,64]{1,0:T(8,128)} custom-call(bf16[192,128]{1,0:T(8,128)(2,1)S(1)} %pad_maximum_fusion.4.mine, bf16[192,128]{1,0:T(8,128)(2,1)S(1)} %collective-permute-done.7.theirs, bf16[64,4096]{1,0:T(8,128)(2,1)S(1)} %shard_map.79.store), custom_call_target="tpu_custom_call" | custom-call | tf_op jit(solution)/shard_map/pallas_call | solution.py:328
  (19 shorter events, 0.3 us)
Async XLA Ops:
  2.8 1.5 %collective-permute-start = (f32[128,128]{1,0:T(8,128)S(1)}, f32[128,128]{1,0:T(8,128)S(1)}, u32[]{:S(2)}, u32[]{:S(2)}) collective-permute-start(f32[128,128]{1,0:T(8,128)S(1)} %get-tuple-element.27.part), channel_id=1, source_target_pairs={{0,1},{1,0},{2,3},{3,2},{4,5},{5,4},{6,7},{7,6},{8,9},{9,8},{10,11... | collective-permute-start | bytes 196616 | tf_op jit(solution)/shard_map/ppermute | solution.py:33
  4.7 5.3 %collective-permute-start.1 = (f16[104,128]{1,0:T(8,128)(2,1)S(1)}, f16[104,128]{1,0:T(8,128)(2,1)S(1)}, u32[]{:S(2)}, u32[]{:S(2)}) collective-permute-start(f16[104,128]{1,0:T(8,128)(2,1)S(1)} %pad_maximum_fusion.5), channel_id=1, source_target_pairs={{0,9},{1,8},{2,11},{3,10},{4,13},{5,12},{6,15},{7,14},{8,1},{9,0},... | collective-permute-start | bytes 79880 | tf_op jit(solution)/shard_map/ppermute | solution.py:33
  10.1 3.6 %collective-permute-start.2 = (f16[200,128]{1,0:T(8,128)(2,1)S(1)}, f16[200,128]{1,0:T(8,128)(2,1)S(1)}, u32[]{:S(2)}, u32[]{:S(2)}) collective-permute-start(f16[200,128]{1,0:T(8,128)(2,1)S(1)} %pad_maximum_fusion.3), channel_id=1, source_target_pairs={{0,3},{1,4},{2,7},{3,0},{4,1},{5,6},{6,5},{7,2},{8,11},{9,12},{10,... | collective-permute-start | bytes 153608 | tf_op jit(solution)/shard_map/ppermute | solution.py:33
  13.9 3.6 %collective-permute-start.3 = (f16[200,128]{1,0:T(8,128)(2,1)S(1)}, f16[200,128]{1,0:T(8,128)(2,1)S(1)}, u32[]{:S(2)}, u32[]{:S(2)}) collective-permute-start(f16[200,128]{1,0:T(8,128)(2,1)S(1)} %get-tuple-element.55), channel_id=1, source_target_pairs={{0,5},{1,2},{2,1},{3,6},{4,7},{5,0},{6,3},{7,4},{8,13},{9,10},{10,... | collective-permute-start | bytes 153608 | tf_op jit(solution)/shard_map/ppermute | solution.py:33
  18.5 1.2 %collective-permute-start.4 = (f32[12,512]{1,0:T(8,128)S(1)}, f32[12,512]{1,0:T(8,128)S(1)}, u32[]{:S(2)}, u32[]{:S(2)}) collective-permute-start(f32[12,512]{1,0:T(8,128)S(1)} %shard_map.78), channel_id=1, source_target_pairs={{0,1},{1,0},{2,3},{3,2},{4,5},{5,4},{6,7},{7,6},{8,9},{9,8},{10,11... | collective-permute-start | bytes 73736 | tf_op jit(solution)/shard_map/ppermute | solution.py:33
  19.8 4.6 %collective-permute-start.5 = (bf16[48,128]{1,0:T(8,128)(2,1)S(1)}, bf16[48,128]{1,0:T(8,128)(2,1)S(1)}, u32[]{:S(2)}, u32[]{:S(2)}) collective-permute-start(bf16[48,128]{1,0:T(8,128)(2,1)S(1)} %reshape.21.after), channel_id=1, source_target_pairs={{0,9},{1,8},{2,11},{3,10},{4,13},{5,12},{6,15},{7,14},{8,1},{9,0},... | collective-permute-start | bytes 36872 | tf_op jit(solution)/shard_map/ppermute | solution.py:33
  24.3 3.3 %collective-permute-start.6 = (bf16[96,128]{1,0:T(8,128)(2,1)S(1)}, bf16[96,128]{1,0:T(8,128)(2,1)S(1)}, u32[]{:S(2)}, u32[]{:S(2)}) collective-permute-start(bf16[96,128]{1,0:T(8,128)(2,1)S(1)} %maximum_select_fusion.1), channel_id=1, source_target_pairs={{0,3},{1,4},{2,7},{3,0},{4,1},{5,6},{6,5},{7,2},{8,11},{9,12},{10,... | collective-permute-start | bytes 73736 | tf_op jit(solution)/shard_map/ppermute | solution.py:33
  27.7 3.5 %collective-permute-start.7 = (bf16[192,128]{1,0:T(8,128)(2,1)S(1)}, bf16[192,128]{1,0:T(8,128)(2,1)S(1)}, u32[]{:S(2)}, u32[]{:S(2)}) collective-permute-start(bf16[192,128]{1,0:T(8,128)(2,1)S(1)} %pad_maximum_fusion.4.mine), channel_id=1, source_target_pairs={{0,5},{1,2},{2,1},{3,6},{4,7},{5,0},{6,3},{7,4},{8,13},{9,10},{10,... | collective-permute-start | bytes 147464 | tf_op jit(solution)/shard_map/ppermute | solution.py:33

commit v7 on v6

--- a/solution.py
+++ b/solution.py
@@ -139,7 +139,7 @@
 def project(activations, gradients, proj_in, proj_out, doc_ids):
     tokens, depth = gradients.shape
     rank = proj_in.shape[1]
-    cuts = [depth * n // 14 // LANES * LANES for n in (0, 5, 9, 12, 13, 14)]
+    cuts = sorted({depth * n // 14 // LANES * LANES for n in (0, 5, 9, 12, 13)} | {depth})
     hbm = pl.BlockSpec(memory_space=pltpu.HBM)
     vmem = pl.BlockSpec(memory_space=pltpu.VMEM)
     return pl.pallas_call(
@@ -285,25 +285,18 @@
     )(*kept(pltpu.HBM, array), *kept(pltpu.VMEM, after))
 
 
-def score_kernel(width, mine, theirs, store, out, products):
+def column_products(width, rows, held, pair, offsets, store):
     pieces = width // LANES
-    count = store.shape[0]
-    rows = out.shape[0] * pieces
-    chunk = mine.shape[0] // 2
-    held = chunk // rows
     bits = held.bit_length() - 1
-    c, p = lax.axis_index("ctx"), lax.axis_index("col")
-    first, second = (near_distance(c, p, last) for last in (0, 1))
     total = None
-    for part, n, offset in ((mine, 0, 0), (mine, 1, first), (theirs, 0, second), (theirs, 1, 3)):
-        low = (c & 3) ^ offset
+    for n, offset in enumerate(offsets):
+        low = (lax.axis_index("ctx") & 3) ^ offset
         blocks, columns = [], [[] for _ in range(pieces)]
         for place in range(held):
             high = sum(((place >> k) & 1) << (bits - 1 - k) for k in range(bits))
-            start = (high * 4 + low) * width
-            blocks.append(part[pl.ds(n * chunk + place * rows, rows), :])
+            blocks.append(pair[pl.ds((n * held + place) * rows, rows), :])
             for k in range(pieces):
-                at = pl.multiple_of(start + k * LANES, LANES)
+                at = pl.multiple_of((high * 4 + low) * width + k * LANES, LANES)
                 columns[k].append(store[:, pl.ds(at, LANES)])
         left = jnp.concatenate(blocks, 1)
         right = jnp.concatenate([jnp.concatenate(column, 1) for column in columns])
@@ -311,6 +304,22 @@
             left, right, (((1,), (1,)), ((), ())), preferred_element_type=jnp.float32
         )
         total = term if total is None else total + term
+    return total
+
+
+def held_kernel(width, mine, store, out):
+    rows = out.shape[0]
+    first = near_distance(lax.axis_index("ctx"), lax.axis_index("col"), 0)
+    held = mine.shape[0] // (2 * rows)
+    out[...] = column_products(width, rows, held, mine, (0, first), store)
+
+
+def score_kernel(width, known, theirs, store, out, products):
+    rows, count = known.shape[0], store.shape[0]
+    pieces = width // LANES
+    second = near_distance(lax.axis_index("ctx"), lax.axis_index("col"), 1)
+    held = theirs.shape[0] // (2 * rows)
+    total = known[...] + column_products(width, rows, held, theirs, (second, 3), store)
     for n in range(products.shape[0] // rows):
         products[pl.ds(n * rows, rows), :] = total[:, n * LANES : (n + 1) * LANES]
     result = None
@@ -322,19 +331,29 @@
     out[...] = result
 
 
-def score(mine, theirs, store, width, doc_count):
+def score_held(mine, store, width, doc_count):
     vmem = pl.BlockSpec(memory_space=pltpu.VMEM)
     pieces = width // LANES
+    return pl.pallas_call(
+        functools.partial(held_kernel, width),
+        out_shape=pltpu.VMEM((doc_count * pieces, pieces * store.shape[0]), jnp.float32),
+        in_specs=[vmem] * 2,
+        out_specs=vmem,
+        compiler_params=pltpu.CompilerParams(vmem_limit_bytes=VMEM_LIMIT),
+    )(*kept(pltpu.VMEM, mine, store))
+
+
+def score(known, theirs, store, width, doc_count):
+    vmem = pl.BlockSpec(memory_space=pltpu.VMEM)
+    slabs = width // LANES * store.shape[0] // LANES
     return pl.pallas_call(
         functools.partial(score_kernel, width),
         out_shape=jax.ShapeDtypeStruct((doc_count, store.shape[0]), jnp.float32),
         in_specs=[vmem] * 3,
         out_specs=vmem,
-        scratch_shapes=[
-            pltpu.VMEM((doc_count * pieces * (pieces * store.shape[0] // LANES), LANES), jnp.float32)
-        ],
-        compiler_params=pltpu.CompilerParams(vmem_limit_bytes=VMEM_LIMIT),
-    )(*kept(pltpu.VMEM, mine, theirs, store))
+        scratch_shapes=[pltpu.VMEM((slabs * known.shape[0], LANES), jnp.float32)],
+        compiler_params=pltpu.CompilerParams(vmem_limit_bytes=VMEM_LIMIT),
+    )(*kept(pltpu.VMEM, known, theirs, store))
 
 
 def shards(activations, gradients, doc_ids, proj_in, proj_out, inverse, store_rows):
@@ -394,7 +413,9 @@
     whole = jnp.concatenate([whole, swap_near(whole, 0)])
     others = swap_near(whole, 1)
     if direct:
-        return score(whole, others, store, width, doc_count)
+        known = score_held(whole, store, width, doc_count)
+        others, known = lax.optimization_barrier((others, known))
+        return score(known, others, store, width, doc_count)
     (own, near), (next_one, farthest) = (x.reshape(2, -1, x.shape[1]) for x in (whole, others))
     c, p = lax.axis_index("ctx"), lax.axis_index("col")
     single = near_distance(c, p, 0) == 1

time: 32.4 us -> 32.3 us (level)
  transfers between devices with their start and end apart: 8 -> 8, of which waited for: 8 -> 8; matrix products, arithmetic and copies ran while one was open for 0% -> 0% of each run, Pallas kernels for 16% -> 17%
where the time goes in v7:
time: 32.3 us; the launch traced here: 32.1 us
  starting transfers between devices  14.1 us (44%)
  Pallas kernels  10.5 us (33%)
  waiting for transfers between devices  7.03 us (22%)
    ppermute x8, starting transfers between devices, swap(): return lax.ppermute(block, ('ctx', 'col'), route)  14.1 us
    ppermute x8, waiting for transfers between devices, swap(): return lax.ppermute(block, ('ctx', 'col'), route)  7.03 us
    pallas_call x3, Pallas kernels, fetch(): pl.pallas_call(functools.partial(fetch_kernel, start, chunk), out_shape=(...  4.13 us
    pallas_call x1, Pallas kernels, project(): pl.pallas_call(functools.partial(project_kernel, cuts), out_shape=(pltpu....  2.83 us
    pallas_call x1, Pallas kernels, load(): pl.pallas_call(load_kernel, out_shape=pltpu.VMEM(array.shape, array.dtype...  1.05 us
    pallas_call x1, Pallas kernels, precondition(): pl.pallas_call(functools.partial(precondition_kernel, len(highs)), out_sh...  1.02 us
    pallas_call x1, Pallas kernels, score(): pl.pallas_call(functools.partial(score_kernel, width), out_shape=jax.Shap...  0.88 us
  transfers between devices with their start and end apart: 8, of which 8 were waited for; matrix products, arithmetic and copies ran while one was open for 0% of the time, Pallas kernels for 17%

profile of v7, /device:TPU:0, one launch (start us, length us, event | category | flops | bytes accessed | tf_op | source)
XLA Modules:
  0.0 32.1 jit_solution(5302296652996537900)
XLA Ops:
  0.0 2.8 %shard_map.73 = (f32[128,128]{1,0:T(8,128)S(1)}, f32[8,128]{1,0:T(8,128)S(1)}, f32[8,128]{1,0:T(8,128)S(1)}) custom-call(s32[1,128]{1,0:T(1,128)} %bitcast.11, bf16[128,2048]{1,0:T(8,128)(2,1)} %act_hbm.1, bf16[64,2048]{1,0:T(8,128)(2,1)} %bitcast.8, bf16[128,7168]{1,0:T(8,128)(2,1)} %grad_hbm.1, bf16[64,7168]{1,0:T(8,128)(2,1)} %bitcast.6), custom_call_target="tpu_custom_call" | custom-call | tf_op jit(solution)/shard_map/pallas_call | solution.py:145
  2.8 0.6 %collective-permute-start = (f32[128,128]{1,0:T(8,128)S(1)}, f32[128,128]{1,0:T(8,128)S(1)}, u32[]{:S(2)}, u32[]{:S(2)}) collective-permute-start(f32[128,128]{1,0:T(8,128)S(1)} %get-tuple-element.29.part), channel_id=1, source_target_pairs={{0,1},{1,0},{2,3},{3,2},{4,5},{5,4},{6,7},{7,6},{8,9},{9,8},{10,11... | collective-permute-start | bytes 196616 | tf_op jit(solution)/shard_map/ppermute | solution.py:33
  3.4 0.9 %collective-permute-done.other = f32[128,128]{1,0:T(8,128)S(1)} collective-permute-done((f32[128,128]{1,0:T(8,128)S(1)}, f32[128,128]{1,0:T(8,128)S(1)}, u32[]{:S(2)}, u32[]{:S(2)}) %collective-permute-start) | collective-permute-done | bytes 65568 | tf_op jit(solution)/shard_map/ppermute | solution.py:33
  4.3 0.4 %shard_map.74 = (f32[96,128]{1,0:T(8,128)S(1)}, f32[8,128]{1,0:T(8,128)S(1)}) custom-call(f32[128,128]{1,0:T(8,128)S(1)} %get-tuple-element.29.part, f32[128,128]{1,0:T(8,128)S(1)} %collective-permute-done.other, f32[8,128]{1,0:T(8,128)S(1)} %get-tuple-element.30.mask, f32[8,128]{1,0:T(8,128)S(1)} %get-tuple-element.31.numbers), custom_call_target="tpu_custom_call" | custom-call | tf_op jit(solution)/shard_map/pallas_call | solution.py:195
  4.7 3.8 %collective-permute-start.1 = (f16[104,128]{1,0:T(8,128)(2,1)S(1)}, f16[104,128]{1,0:T(8,128)(2,1)S(1)}, u32[]{:S(2)}, u32[]{:S(2)}) collective-permute-start(f16[104,128]{1,0:T(8,128)(2,1)S(1)} %pad_maximum_fusion.5), channel_id=1, source_target_pairs={{0,9},{1,8},{2,11},{3,10},{4,13},{5,12},{6,15},{7,14},{8,1},{9,0},... | collective-permute-start | bytes 79880 | tf_op jit(solution)/shard_map/ppermute | solution.py:33
  8.5 1.3 %shard_map.75 = (bf16[512,512]{1,0:T(8,128)(2,1)S(1)}, bf16[512,512]{1,0:T(8,128)(2,1)S(1)}) custom-call(f32[2048,512]{1,0:T(8,128)} %array.5, f32[8,128]{1,0:T(8,128)S(1)} %get-tuple-element.55.after), custom_call_target="tpu_custom_call" | custom-call | tf_op jit(solution)/shard_map/pallas_call | solution.py:86
  9.7 0.3 collective-permute-done.1
  10.1 1.6 %collective-permute-start.2 = (f16[200,128]{1,0:T(8,128)(2,1)S(1)}, f16[200,128]{1,0:T(8,128)(2,1)S(1)}, u32[]{:S(2)}, u32[]{:S(2)}) collective-permute-start(f16[200,128]{1,0:T(8,128)(2,1)S(1)} %pad_maximum_fusion.3), channel_id=1, source_target_pairs={{0,3},{1,4},{2,7},{3,0},{4,1},{5,6},{6,5},{7,2},{8,11},{9,12},{10,... | collective-permute-start | bytes 153608 | tf_op jit(solution)/shard_map/ppermute | solution.py:33
  11.7 1.4 %shard_map.76 = (bf16[768,512]{1,0:T(8,128)(2,1)S(1)}, bf16[768,512]{1,0:T(8,128)(2,1)S(1)}) custom-call(f32[2048,512]{1,0:T(8,128)} %array.5, f32[8,128]{1,0:T(8,128)S(1)} %get-tuple-element.53.after), custom_call_target="tpu_custom_call" | custom-call | tf_op jit(solution)/shard_map/pallas_call | solution.py:86
  13.1 0.6 %collective-permute-done.2 = f16[200,128]{1,0:T(8,128)(2,1)S(1)} collective-permute-done((f16[200,128]{1,0:T(8,128)(2,1)S(1)}, f16[200,128]{1,0:T(8,128)(2,1)S(1)}, u32[]{:S(2)}, u32[]{:S(2)}) %collective-permute-start.2) | collective-permute-done | bytes 51232 | tf_op jit(solution)/shard_map/ppermute | solution.py:33
  13.9 1.7 %collective-permute-start.3 = (f16[200,128]{1,0:T(8,128)(2,1)S(1)}, f16[200,128]{1,0:T(8,128)(2,1)S(1)}, u32[]{:S(2)}, u32[]{:S(2)}) collective-permute-start(f16[200,128]{1,0:T(8,128)(2,1)S(1)} %get-tuple-element.59), channel_id=1, source_target_pairs={{0,5},{1,2},{2,1},{3,6},{4,7},{5,0},{6,3},{7,4},{8,13},{9,10},{10,... | collective-permute-start | bytes 153608 | tf_op jit(solution)/shard_map/ppermute | solution.py:33
  15.5 1.4 %shard_map.77 = (bf16[768,512]{1,0:T(8,128)(2,1)S(1)}, bf16[768,512]{1,0:T(8,128)(2,1)S(1)}) custom-call(f32[2048,512]{1,0:T(8,128)} %array.5, f32[200,128]{1,0:T(8,128)S(1)} %get-tuple-element.60.after.own), custom_call_target="tpu_custom_call" | custom-call | tf_op jit(solution)/shard_map/pallas_call | solution.py:86
  17.0 0.5 %collective-permute-done.3 = f16[200,128]{1,0:T(8,128)(2,1)S(1)} collective-permute-done((f16[200,128]{1,0:T(8,128)(2,1)S(1)}, f16[200,128]{1,0:T(8,128)(2,1)S(1)}, u32[]{:S(2)}, u32[]{:S(2)}) %collective-permute-start.3) | collective-permute-done | bytes 51232 | tf_op jit(solution)/shard_map/ppermute | solution.py:33
  17.5 1.0 %shard_map.78 = f32[12,512]{1,0:T(8,128)S(1)} custom-call(f32[200,128]{1,0:T(8,128)S(1)} %get-tuple-element.60.after.own, f32[200,128]{1,0:T(8,128)S(1)} %convert_element_type.26.other, bf16[512,512]{1,0:T(8,128)(2,1)S(1)} %get-tuple-element.43.refs_0_, bf16[768,512]{1,0:T(8,128)(2,1)S(1)} %get-tuple-element.44.refs_1_, ...), custom_call_target="tpu_custom_call" | custom-call | tf_op jit(solution)/shard_map/pallas_call | solution.py:260
  18.5 0.4 %collective-permute-start.4 = (f32[12,512]{1,0:T(8,128)S(1)}, f32[12,512]{1,0:T(8,128)S(1)}, u32[]{:S(2)}, u32[]{:S(2)}) collective-permute-start(f32[12,512]{1,0:T(8,128)S(1)} %shard_map.78), channel_id=1, source_target_pairs={{0,1},{1,0},{2,3},{3,2},{4,5},{5,4},{6,7},{7,6},{8,9},{9,8},{10,11... | collective-permute-start | bytes 73736 | tf_op jit(solution)/shard_map/ppermute | solution.py:33
  18.9 0.9 %collective-permute-done.4 = f32[12,512]{1,0:T(8,128)S(1)} collective-permute-done((f32[12,512]{1,0:T(8,128)S(1)}, f32[12,512]{1,0:T(8,128)S(1)}, u32[]{:S(2)}, u32[]{:S(2)}) %collective-permute-start.4) | collective-permute-done | bytes 24608 | tf_op jit(solution)/shard_map/ppermute | solution.py:33
  19.8 3.2 %collective-permute-start.5 = (bf16[48,128]{1,0:T(8,128)(2,1)S(1)}, bf16[48,128]{1,0:T(8,128)(2,1)S(1)}, u32[]{:S(2)}, u32[]{:S(2)}) collective-permute-start(bf16[48,128]{1,0:T(8,128)(2,1)S(1)} %reshape.21.after), channel_id=1, source_target_pairs={{0,9},{1,8},{2,11},{3,10},{4,13},{5,12},{6,15},{7,14},{8,1},{9,0},... | collective-permute-start | bytes 36872 | tf_op jit(solution)/shard_map/ppermute | solution.py:33
  22.9 1.0 %shard_map.79.store = bf16[64,4096]{1,0:T(8,128)(2,1)S(1)} custom-call(bf16[64,4096]{1,0:T(8,128)(2,1)} %source.1, bf16[48,128]{1,0:T(8,128)(2,1)S(1)} %reshape.21.after), custom_call_target="tpu_custom_call" | custom-call | tf_op jit(solution)/shard_map/pallas_call | solution.py:278
  24.0 0.3 %collective-permute-done.5 = bf16[48,128]{1,0:T(8,128)(2,1)S(1)} collective-permute-done((bf16[48,128]{1,0:T(8,128)(2,1)S(1)}, bf16[48,128]{1,0:T(8,128)(2,1)S(1)}, u32[]{:S(2)}, u32[]{:S(2)}) %collective-permute-start.5) | collective-permute-done | bytes 12320 | tf_op jit(solution)/shard_map/ppermute | solution.py:33
  24.3 1.3 %collective-permute-start.6 = (bf16[96,128]{1,0:T(8,128)(2,1)S(1)}, bf16[96,128]{1,0:T(8,128)(2,1)S(1)}, u32[]{:S(2)}, u32[]{:S(2)}) collective-permute-start(bf16[96,128]{1,0:T(8,128)(2,1)S(1)} %maximum_select_fusion.1), channel_id=1, source_target_pairs={{0,3},{1,4},{2,7},{3,0},{4,1},{5,6},{6,5},{7,2},{8,11},{9,12},{10,... | collective-permute-start | bytes 73736 | tf_op jit(solution)/shard_map/ppermute | solution.py:33
  25.6 2.0 %collective-permute-done.6 = bf16[96,128]{1,0:T(8,128)(2,1)S(1)} collective-permute-done((bf16[96,128]{1,0:T(8,128)(2,1)S(1)}, bf16[96,128]{1,0:T(8,128)(2,1)S(1)}, u32[]{:S(2)}, u32[]{:S(2)}) %collective-permute-start.6) | collective-permute-done | bytes 24608 | tf_op jit(solution)/shard_map/ppermute | solution.py:33
  27.7 1.7 %collective-permute-start.7 = (bf16[192,128]{1,0:T(8,128)(2,1)S(1)}, bf16[192,128]{1,0:T(8,128)(2,1)S(1)}, u32[]{:S(2)}, u32[]{:S(2)}) collective-permute-start(bf16[192,128]{1,0:T(8,128)(2,1)S(1)} %pad_maximum_fusion.4.mine), channel_id=1, source_target_pairs={{0,5},{1,2},{2,1},{3,6},{4,7},{5,0},{6,3},{7,4},{8,13},{9,10},{10,... | collective-permute-start | bytes 147464 | tf_op jit(solution)/shard_map/ppermute | solution.py:33
  29.4 0.2 shard_map.80.known
  29.6 1.6 %collective-permute-done.7.theirs = bf16[192,128]{1,0:T(8,128)(2,1)S(1)} collective-permute-done((bf16[192,128]{1,0:T(8,128)(2,1)S(1)}, bf16[192,128]{1,0:T(8,128)(2,1)S(1)}, u32[]{:S(2)}, u32[]{:S(2)}) %collective-permute-start.7) | collective-permute-done | bytes 49184 | tf_op jit(solution)/shard_map/ppermute | solution.py:33
  31.2 0.9 %shard_map.81 = f32[12,64]{1,0:T(8,128)} custom-call(f32[48,256]{1,0:T(8,128)S(1)} %shard_map.80.known, bf16[192,128]{1,0:T(8,128)(2,1)S(1)} %collective-permute-done.7.theirs, bf16[64,4096]{1,0:T(8,128)(2,1)S(1)} %shard_map.79.store), custom_call_target="tpu_custom_call" | custom-call | tf_op jit(solution)/shard_map/pallas_call | solution.py:349
  (19 shorter events, 0.3 us)
Async XLA Ops:
  2.8 1.5 %collective-permute-start = (f32[128,128]{1,0:T(8,128)S(1)}, f32[128,128]{1,0:T(8,128)S(1)}, u32[]{:S(2)}, u32[]{:S(2)}) collective-permute-start(f32[128,128]{1,0:T(8,128)S(1)} %get-tuple-element.29.part), channel_id=1, source_target_pairs={{0,1},{1,0},{2,3},{3,2},{4,5},{5,4},{6,7},{7,6},{8,9},{9,8},{10,11... | collective-permute-start | bytes 196616 | tf_op jit(solution)/shard_map/ppermute | solution.py:33
  4.7 5.3 %collective-permute-start.1 = (f16[104,128]{1,0:T(8,128)(2,1)S(1)}, f16[104,128]{1,0:T(8,128)(2,1)S(1)}, u32[]{:S(2)}, u32[]{:S(2)}) collective-permute-start(f16[104,128]{1,0:T(8,128)(2,1)S(1)} %pad_maximum_fusion.5), channel_id=1, source_target_pairs={{0,9},{1,8},{2,11},{3,10},{4,13},{5,12},{6,15},{7,14},{8,1},{9,0},... | collective-permute-start | bytes 79880 | tf_op jit(solution)/shard_map/ppermute | solution.py:33
  10.1 3.6 %collective-permute-start.2 = (f16[200,128]{1,0:T(8,128)(2,1)S(1)}, f16[200,128]{1,0:T(8,128)(2,1)S(1)}, u32[]{:S(2)}, u32[]{:S(2)}) collective-permute-start(f16[200,128]{1,0:T(8,128)(2,1)S(1)} %pad_maximum_fusion.3), channel_id=1, source_target_pairs={{0,3},{1,4},{2,7},{3,0},{4,1},{5,6},{6,5},{7,2},{8,11},{9,12},{10,... | collective-permute-start | bytes 153608 | tf_op jit(solution)/shard_map/ppermute | solution.py:33
  13.9 3.6 %collective-permute-start.3 = (f16[200,128]{1,0:T(8,128)(2,1)S(1)}, f16[200,128]{1,0:T(8,128)(2,1)S(1)}, u32[]{:S(2)}, u32[]{:S(2)}) collective-permute-start(f16[200,128]{1,0:T(8,128)(2,1)S(1)} %get-tuple-element.59), channel_id=1, source_target_pairs={{0,5},{1,2},{2,1},{3,6},{4,7},{5,0},{6,3},{7,4},{8,13},{9,10},{10,... | collective-permute-start | bytes 153608 | tf_op jit(solution)/shard_map/ppermute | solution.py:33
  18.5 1.2 %collective-permute-start.4 = (f32[12,512]{1,0:T(8,128)S(1)}, f32[12,512]{1,0:T(8,128)S(1)}, u32[]{:S(2)}, u32[]{:S(2)}) collective-permute-start(f32[12,512]{1,0:T(8,128)S(1)} %shard_map.78), channel_id=1, source_target_pairs={{0,1},{1,0},{2,3},{3,2},{4,5},{5,4},{6,7},{7,6},{8,9},{9,8},{10,11... | collective-permute-start | bytes 73736 | tf_op jit(solution)/shard_map/ppermute | solution.py:33
  19.8 4.6 %collective-permute-start.5 = (bf16[48,128]{1,0:T(8,128)(2,1)S(1)}, bf16[48,128]{1,0:T(8,128)(2,1)S(1)}, u32[]{:S(2)}, u32[]{:S(2)}) collective-permute-start(bf16[48,128]{1,0:T(8,128)(2,1)S(1)} %reshape.21.after), channel_id=1, source_target_pairs={{0,9},{1,8},{2,11},{3,10},{4,13},{5,12},{6,15},{7,14},{8,1},{9,0},... | collective-permute-start | bytes 36872 | tf_op jit(solution)/shard_map/ppermute | solution.py:33
  24.3 3.3 %collective-permute-start.6 = (bf16[96,128]{1,0:T(8,128)(2,1)S(1)}, bf16[96,128]{1,0:T(8,128)(2,1)S(1)}, u32[]{:S(2)}, u32[]{:S(2)}) collective-permute-start(bf16[96,128]{1,0:T(8,128)(2,1)S(1)} %maximum_select_fusion.1), channel_id=1, source_target_pairs={{0,3},{1,4},{2,7},{3,0},{4,1},{5,6},{6,5},{7,2},{8,11},{9,12},{10,... | collective-permute-start | bytes 73736 | tf_op jit(solution)/shard_map/ppermute | solution.py:33
  27.7 3.5 %collective-permute-start.7 = (bf16[192,128]{1,0:T(8,128)(2,1)S(1)}, bf16[192,128]{1,0:T(8,128)(2,1)S(1)}, u32[]{:S(2)}, u32[]{:S(2)}) collective-permute-start(bf16[192,128]{1,0:T(8,128)(2,1)S(1)} %pad_maximum_fusion.4.mine), channel_id=1, source_target_pairs={{0,5},{1,2},{2,1},{3,6},{4,7},{5,0},{6,3},{7,4},{8,13},{9,10},{10,... | collective-permute-start | bytes 147464 | tf_op jit(solution)/shard_map/ppermute | solution.py:33

commit v8 on v7

--- a/solution.py
+++ b/solution.py
@@ -175,13 +175,15 @@
     paired = jnp.concatenate(
         [jnp.concatenate([right, none], 1), jnp.concatenate([none, right], 1)]
     )
+    dims = (((1,), (1,)), ((), ()))
+    high, low = split(weighted)
+    right_high, right_low = split(paired)
+    rows = weighted.shape[0]
     found = lax.dot_general(
-        weighted,
-        paired,
-        (((1,), (1,)), ((), ())),
-        precision=lax.Precision.HIGHEST,
-        preferred_element_type=jnp.float32,
+        jnp.concatenate([high, low]), right_high, dims, preferred_element_type=jnp.float32
     )
+    small = lax.dot_general(high, right_low, dims, preferred_element_type=jnp.float32)
+    found = found[:rows] + (found[rows:] + small)
     largest = jnp.max(jnp.max(jnp.abs(found), 0, keepdims=True), 1, keepdims=True)
     power = jnp.floor(jnp.log2(jnp.maximum(largest, 1e-30)))
     sums[...] = found * jnp.exp2(TOP - power)
@@ -207,50 +209,43 @@
 
 def precondition_kernel(windows, own, other, *refs):
     highs, lows, (out, pieces) = refs[:windows], refs[windows : 2 * windows], refs[2 * windows :]
-    depth = pieces.shape[1]
+    rows, depth = pieces.shape
     size = own.shape[0] - 8
     count = size * LANES // depth
-    room = pieces.shape[0] // 2
     pieces[...] = jnp.zeros_like(pieces)
     for k in range(depth // LANES):
         for n, part in enumerate((own, other)):
-            pieces[pl.ds(n * room, count), pl.ds(k * LANES, LANES)] = part[
+            pieces[pl.ds(n * count, count), pl.ds(k * LANES, LANES)] = part[
                 pl.ds(k, count, stride=depth // LANES), :
             ]
     first, second, at = None, None, 0
     for weights_high, weights_low in zip(highs, lows):
-        rows = weights_high.shape[0]
-        high, low = split(pieces[:, pl.ds(at, rows)])
-        term = jnp.dot(
-            jnp.concatenate([high, low]), weights_high[...], preferred_element_type=jnp.float32
-        )
+        block = pieces[:, pl.ds(at, weights_high.shape[0])]
+        high = block.astype(jnp.bfloat16).astype(jnp.float32)
+        both = jnp.concatenate([high, block - high]).astype(jnp.bfloat16)
+        term = jnp.dot(both, weights_high[...], preferred_element_type=jnp.float32)
         first = term if first is None else first + term
-        term = jnp.dot(high, weights_low[...], preferred_element_type=jnp.float32)
+        upper = both[: pl.cdiv(rows, 16) * 16]
+        term = jnp.dot(upper, weights_low[...], preferred_element_type=jnp.float32)
         second = term if second is None else second + term
-        at += rows
-    total = first[: 2 * room] + (first[2 * room :] + second)
-    docs = lax.broadcasted_iota(jnp.int32, (out.shape[0], count), 0).astype(jnp.float32)
-    result = None
-    for n, part in enumerate((own, other)):
-        rows = []
-        for at in (0, 4):
-            lanes = [
-                jnp.concatenate(
-                    [part[size + r : size + r + 1, :] for r in range(k, k + pl.cdiv(count // 2, LANES))], 1
-                )[:, : count // 2]
-                for k in (at, at + 2)
-            ]
-            rows.append(jnp.broadcast_to(jnp.concatenate(lanes, 1), docs.shape))
-        lanes, powers = rows
-        pick = jnp.where(lanes == docs, jnp.exp2(powers - TOP), 0.0)
-        term = jnp.dot(
-            pick,
-            total[n * room : n * room + count],
-            precision=lax.Precision.HIGHEST,
-            preferred_element_type=jnp.float32,
-        )
-        result = term if result is None else result + term
-    out[...] = result
+        at += weights_high.shape[0]
+    total = first[:rows] + (first[rows:] + second[:rows])
+    marks = []
+    for at in (0, 4):
+        lanes = [
+            jnp.concatenate(
+                [part[size + r : size + r + 1, :] for r in range(k, k + pl.cdiv(count // 2, LANES))], 1
+            )[:, : count // 2]
+            for part in (own, other)
+            for k in (at, at + 2)
+        ]
+        if rows > 2 * count:
+            lanes.append(jnp.full((1, rows - 2 * count), -1.0, jnp.float32))
+        marks.append(jnp.broadcast_to(jnp.concatenate(lanes, 1), (out.shape[0], rows)))
+    numbers, powers = marks
+    docs = lax.broadcasted_iota(jnp.int32, numbers.shape, 0).astype(jnp.float32)
+    pick = jnp.where(numbers == docs, jnp.exp2(powers - TOP), 0.0).astype(jnp.bfloat16)
+    out[...] = sum(jnp.dot(pick, part, preferred_element_type=jnp.float32) for part in split(total))
 
 
 def precondition(own, other, highs, lows, doc_count):
@@ -262,7 +257,7 @@
         out_shape=pltpu.VMEM((doc_count, width), jnp.float32),
         in_specs=[vmem] * (2 + 2 * len(highs)),
         out_specs=vmem,
-        scratch_shapes=[pltpu.VMEM((2 * pl.cdiv(count, 8) * 8, depth), jnp.float32)],
+        scratch_shapes=[pltpu.VMEM((pl.cdiv(2 * count, 8) * 8, depth), jnp.float32)],
         compiler_params=pltpu.CompilerParams(vmem_limit_bytes=VMEM_LIMIT),
     )(*kept(pltpu.VMEM, own, other, *highs, *lows))
 

time: 32.3 us -> 32.2 us (level)
  no operation moved by 1% of the time
where the time goes in v8:
time: 32.2 us; the launch traced here: 31.9 us
  starting transfers between devices  14.1 us (44%)
  Pallas kernels  10.4 us (32%)
  waiting for transfers between devices  7.03 us (22%)
    ppermute x8, starting transfers between devices, swap(): return lax.ppermute(block, ('ctx', 'col'), route)  14.1 us
    ppermute x8, waiting for transfers between devices, swap(): return lax.ppermute(block, ('ctx', 'col'), route)  7.03 us
    pallas_call x3, Pallas kernels, fetch(): pl.pallas_call(functools.partial(fetch_kernel, start, chunk), out_shape=(...  4.13 us
    pallas_call x1, Pallas kernels, project(): pl.pallas_call(functools.partial(project_kernel, cuts), out_shape=(pltpu....  2.83 us
    pallas_call x1, Pallas kernels, load(): pl.pallas_call(load_kernel, out_shape=pltpu.VMEM(array.shape, array.dtype...  1.05 us
    pallas_call x1, Pallas kernels, precondition(): pl.pallas_call(functools.partial(precondition_kernel, len(highs)), out_sh...  0.98 us
    pallas_call x1, Pallas kernels, score(): pl.pallas_call(functools.partial(score_kernel, width), out_shape=jax.Shap...  0.88 us
  transfers between devices with their start and end apart: 8, of which 8 were waited for; matrix products, arithmetic and copies ran while one was open for 0% of the time, Pallas kernels for 17%

profile of v8, /device:TPU:0, one launch (start us, length us, event | category | flops | bytes accessed | tf_op | source)
XLA Modules:
  0.0 31.9 jit_solution(8851334772771292)
XLA Ops:
  0.0 2.8 %shard_map.73 = (f32[128,128]{1,0:T(8,128)S(1)}, f32[8,128]{1,0:T(8,128)S(1)}, f32[8,128]{1,0:T(8,128)S(1)}) custom-call(s32[1,128]{1,0:T(1,128)} %bitcast.11, bf16[128,2048]{1,0:T(8,128)(2,1)} %act_hbm.1, bf16[64,2048]{1,0:T(8,128)(2,1)} %bitcast.8, bf16[128,7168]{1,0:T(8,128)(2,1)} %grad_hbm.1, bf16[64,7168]{1,0:T(8,128)(2,1)} %bitcast.6), custom_call_target="tpu_custom_call" | custom-call | tf_op jit(solution)/shard_map/pallas_call | solution.py:145
  2.8 0.6 %collective-permute-start = (f32[128,128]{1,0:T(8,128)S(1)}, f32[128,128]{1,0:T(8,128)S(1)}, u32[]{:S(2)}, u32[]{:S(2)}) collective-permute-start(f32[128,128]{1,0:T(8,128)S(1)} %get-tuple-element.29.part), channel_id=1, source_target_pairs={{0,1},{1,0},{2,3},{3,2},{4,5},{5,4},{6,7},{7,6},{8,9},{9,8},{10,11... | collective-permute-start | bytes 196616 | tf_op jit(solution)/shard_map/ppermute | solution.py:33
  3.4 0.9 %collective-permute-done.other = f32[128,128]{1,0:T(8,128)S(1)} collective-permute-done((f32[128,128]{1,0:T(8,128)S(1)}, f32[128,128]{1,0:T(8,128)S(1)}, u32[]{:S(2)}, u32[]{:S(2)}) %collective-permute-start) | collective-permute-done | bytes 65568 | tf_op jit(solution)/shard_map/ppermute | solution.py:33
  4.3 0.3 shard_map.74
  4.7 3.8 %collective-permute-start.1 = (f16[104,128]{1,0:T(8,128)(2,1)S(1)}, f16[104,128]{1,0:T(8,128)(2,1)S(1)}, u32[]{:S(2)}, u32[]{:S(2)}) collective-permute-start(f16[104,128]{1,0:T(8,128)(2,1)S(1)} %pad_maximum_fusion.5), channel_id=1, source_target_pairs={{0,9},{1,8},{2,11},{3,10},{4,13},{5,12},{6,15},{7,14},{8,1},{9,0},... | collective-permute-start | bytes 79880 | tf_op jit(solution)/shard_map/ppermute | solution.py:33
  8.4 1.3 %shard_map.75 = (bf16[512,512]{1,0:T(8,128)(2,1)S(1)}, bf16[512,512]{1,0:T(8,128)(2,1)S(1)}) custom-call(f32[2048,512]{1,0:T(8,128)} %array.5, f32[8,128]{1,0:T(8,128)S(1)} %get-tuple-element.55.after), custom_call_target="tpu_custom_call" | custom-call | tf_op jit(solution)/shard_map/pallas_call | solution.py:86
  9.7 0.3 collective-permute-done.1
  10.0 1.6 %collective-permute-start.2 = (f16[200,128]{1,0:T(8,128)(2,1)S(1)}, f16[200,128]{1,0:T(8,128)(2,1)S(1)}, u32[]{:S(2)}, u32[]{:S(2)}) collective-permute-start(f16[200,128]{1,0:T(8,128)(2,1)S(1)} %pad_maximum_fusion.3), channel_id=1, source_target_pairs={{0,3},{1,4},{2,7},{3,0},{4,1},{5,6},{6,5},{7,2},{8,11},{9,12},{10,... | collective-permute-start | bytes 153608 | tf_op jit(solution)/shard_map/ppermute | solution.py:33
  11.6 1.4 %shard_map.76 = (bf16[768,512]{1,0:T(8,128)(2,1)S(1)}, bf16[768,512]{1,0:T(8,128)(2,1)S(1)}) custom-call(f32[2048,512]{1,0:T(8,128)} %array.5, f32[8,128]{1,0:T(8,128)S(1)} %get-tuple-element.53.after), custom_call_target="tpu_custom_call" | custom-call | tf_op jit(solution)/shard_map/pallas_call | solution.py:86
  13.1 0.6 %collective-permute-done.2 = f16[200,128]{1,0:T(8,128)(2,1)S(1)} collective-permute-done((f16[200,128]{1,0:T(8,128)(2,1)S(1)}, f16[200,128]{1,0:T(8,128)(2,1)S(1)}, u32[]{:S(2)}, u32[]{:S(2)}) %collective-permute-start.2) | collective-permute-done | bytes 51232 | tf_op jit(solution)/shard_map/ppermute | solution.py:33
  13.8 1.7 %collective-permute-start.3 = (f16[200,128]{1,0:T(8,128)(2,1)S(1)}, f16[200,128]{1,0:T(8,128)(2,1)S(1)}, u32[]{:S(2)}, u32[]{:S(2)}) collective-permute-start(f16[200,128]{1,0:T(8,128)(2,1)S(1)} %get-tuple-element.59), channel_id=1, source_target_pairs={{0,5},{1,2},{2,1},{3,6},{4,7},{5,0},{6,3},{7,4},{8,13},{9,10},{10,... | collective-permute-start | bytes 153608 | tf_op jit(solution)/shard_map/ppermute | solution.py:33
  15.5 1.4 %shard_map.77 = (bf16[768,512]{1,0:T(8,128)(2,1)S(1)}, bf16[768,512]{1,0:T(8,128)(2,1)S(1)}) custom-call(f32[2048,512]{1,0:T(8,128)} %array.5, f32[200,128]{1,0:T(8,128)S(1)} %get-tuple-element.60.after.own), custom_call_target="tpu_custom_call" | custom-call | tf_op jit(solution)/shard_map/pallas_call | solution.py:86
  16.9 0.5 %collective-permute-done.3 = f16[200,128]{1,0:T(8,128)(2,1)S(1)} collective-permute-done((f16[200,128]{1,0:T(8,128)(2,1)S(1)}, f16[200,128]{1,0:T(8,128)(2,1)S(1)}, u32[]{:S(2)}, u32[]{:S(2)}) %collective-permute-start.3) | collective-permute-done | bytes 51232 | tf_op jit(solution)/shard_map/ppermute | solution.py:33
  17.4 1.0 %shard_map.78 = f32[12,512]{1,0:T(8,128)S(1)} custom-call(f32[200,128]{1,0:T(8,128)S(1)} %get-tuple-element.60.after.own, f32[200,128]{1,0:T(8,128)S(1)} %convert_element_type.26.other, bf16[512,512]{1,0:T(8,128)(2,1)S(1)} %get-tuple-element.43.refs_0_, bf16[768,512]{1,0:T(8,128)(2,1)S(1)} %get-tuple-element.44.refs_1_, ...), custom_call_target="tpu_custom_call" | custom-call | tf_op jit(solution)/shard_map/pallas_call | solution.py:255
  18.4 0.4 %collective-permute-start.4 = (f32[12,512]{1,0:T(8,128)S(1)}, f32[12,512]{1,0:T(8,128)S(1)}, u32[]{:S(2)}, u32[]{:S(2)}) collective-permute-start(f32[12,512]{1,0:T(8,128)S(1)} %shard_map.78), channel_id=1, source_target_pairs={{0,1},{1,0},{2,3},{3,2},{4,5},{5,4},{6,7},{7,6},{8,9},{9,8},{10,11... | collective-permute-start | bytes 73736 | tf_op jit(solution)/shard_map/ppermute | solution.py:33
  18.7 0.9 %collective-permute-done.4 = f32[12,512]{1,0:T(8,128)S(1)} collective-permute-done((f32[12,512]{1,0:T(8,128)S(1)}, f32[12,512]{1,0:T(8,128)S(1)}, u32[]{:S(2)}, u32[]{:S(2)}) %collective-permute-start.4) | collective-permute-done | bytes 24608 | tf_op jit(solution)/shard_map/ppermute | solution.py:33
  19.6 3.2 %collective-permute-start.5 = (bf16[48,128]{1,0:T(8,128)(2,1)S(1)}, bf16[48,128]{1,0:T(8,128)(2,1)S(1)}, u32[]{:S(2)}, u32[]{:S(2)}) collective-permute-start(bf16[48,128]{1,0:T(8,128)(2,1)S(1)} %reshape.21.after), channel_id=1, source_target_pairs={{0,9},{1,8},{2,11},{3,10},{4,13},{5,12},{6,15},{7,14},{8,1},{9,0},... | collective-permute-start | bytes 36872 | tf_op jit(solution)/shard_map/ppermute | solution.py:33
  22.8 1.0 %shard_map.79.store = bf16[64,4096]{1,0:T(8,128)(2,1)S(1)} custom-call(bf16[64,4096]{1,0:T(8,128)(2,1)} %source.1, bf16[48,128]{1,0:T(8,128)(2,1)S(1)} %reshape.21.after), custom_call_target="tpu_custom_call" | custom-call | tf_op jit(solution)/shard_map/pallas_call | solution.py:273
  23.9 0.3 %collective-permute-done.5 = bf16[48,128]{1,0:T(8,128)(2,1)S(1)} collective-permute-done((bf16[48,128]{1,0:T(8,128)(2,1)S(1)}, bf16[48,128]{1,0:T(8,128)(2,1)S(1)}, u32[]{:S(2)}, u32[]{:S(2)}) %collective-permute-start.5) | collective-permute-done | bytes 12320 | tf_op jit(solution)/shard_map/ppermute | solution.py:33
  24.2 1.3 %collective-permute-start.6 = (bf16[96,128]{1,0:T(8,128)(2,1)S(1)}, bf16[96,128]{1,0:T(8,128)(2,1)S(1)}, u32[]{:S(2)}, u32[]{:S(2)}) collective-permute-start(bf16[96,128]{1,0:T(8,128)(2,1)S(1)} %maximum_select_fusion.1), channel_id=1, source_target_pairs={{0,3},{1,4},{2,7},{3,0},{4,1},{5,6},{6,5},{7,2},{8,11},{9,12},{10,... | collective-permute-start | bytes 73736 | tf_op jit(solution)/shard_map/ppermute | solution.py:33
  25.5 2.0 %collective-permute-done.6 = bf16[96,128]{1,0:T(8,128)(2,1)S(1)} collective-permute-done((bf16[96,128]{1,0:T(8,128)(2,1)S(1)}, bf16[96,128]{1,0:T(8,128)(2,1)S(1)}, u32[]{:S(2)}, u32[]{:S(2)}) %collective-permute-start.6) | collective-permute-done | bytes 24608 | tf_op jit(solution)/shard_map/ppermute | solution.py:33
  27.5 1.7 %collective-permute-start.7 = (bf16[192,128]{1,0:T(8,128)(2,1)S(1)}, bf16[192,128]{1,0:T(8,128)(2,1)S(1)}, u32[]{:S(2)}, u32[]{:S(2)}) collective-permute-start(bf16[192,128]{1,0:T(8,128)(2,1)S(1)} %pad_maximum_fusion.4.mine), channel_id=1, source_target_pairs={{0,5},{1,2},{2,1},{3,6},{4,7},{5,0},{6,3},{7,4},{8,13},{9,10},{10,... | collective-permute-start | bytes 147464 | tf_op jit(solution)/shard_map/ppermute | solution.py:33
  29.3 0.2 shard_map.80.known
  29.5 1.6 %collective-permute-done.7.theirs = bf16[192,128]{1,0:T(8,128)(2,1)S(1)} collective-permute-done((bf16[192,128]{1,0:T(8,128)(2,1)S(1)}, bf16[192,128]{1,0:T(8,128)(2,1)S(1)}, u32[]{:S(2)}, u32[]{:S(2)}) %collective-permute-start.7) | collective-permute-done | bytes 49184 | tf_op jit(solution)/shard_map/ppermute | solution.py:33
  31.1 0.9 %shard_map.81 = f32[12,64]{1,0:T(8,128)} custom-call(f32[48,256]{1,0:T(8,128)S(1)} %shard_map.80.known, bf16[192,128]{1,0:T(8,128)(2,1)S(1)} %collective-permute-done.7.theirs, bf16[64,4096]{1,0:T(8,128)(2,1)S(1)} %shard_map.79.store), custom_call_target="tpu_custom_call" | custom-call | tf_op jit(solution)/shard_map/pallas_call | solution.py:344
  (19 shorter events, 0.3 us)
Async XLA Ops:
  2.8 1.5 %collective-permute-start = (f32[128,128]{1,0:T(8,128)S(1)}, f32[128,128]{1,0:T(8,128)S(1)}, u32[]{:S(2)}, u32[]{:S(2)}) collective-permute-start(f32[128,128]{1,0:T(8,128)S(1)} %get-tuple-element.29.part), channel_id=1, source_target_pairs={{0,1},{1,0},{2,3},{3,2},{4,5},{5,4},{6,7},{7,6},{8,9},{9,8},{10,11... | collective-permute-start | bytes 196616 | tf_op jit(solution)/shard_map/ppermute | solution.py:33
  4.7 5.3 %collective-permute-start.1 = (f16[104,128]{1,0:T(8,128)(2,1)S(1)}, f16[104,128]{1,0:T(8,128)(2,1)S(1)}, u32[]{:S(2)}, u32[]{:S(2)}) collective-permute-start(f16[104,128]{1,0:T(8,128)(2,1)S(1)} %pad_maximum_fusion.5), channel_id=1, source_target_pairs={{0,9},{1,8},{2,11},{3,10},{4,13},{5,12},{6,15},{7,14},{8,1},{9,0},... | collective-permute-start | bytes 79880 | tf_op jit(solution)/shard_map/ppermute | solution.py:33
  10.0 3.6 %collective-permute-start.2 = (f16[200,128]{1,0:T(8,128)(2,1)S(1)}, f16[200,128]{1,0:T(8,128)(2,1)S(1)}, u32[]{:S(2)}, u32[]{:S(2)}) collective-permute-start(f16[200,128]{1,0:T(8,128)(2,1)S(1)} %pad_maximum_fusion.3), channel_id=1, source_target_pairs={{0,3},{1,4},{2,7},{3,0},{4,1},{5,6},{6,5},{7,2},{8,11},{9,12},{10,... | collective-permute-start | bytes 153608 | tf_op jit(solution)/shard_map/ppermute | solution.py:33
  13.8 3.6 %collective-permute-start.3 = (f16[200,128]{1,0:T(8,128)(2,1)S(1)}, f16[200,128]{1,0:T(8,128)(2,1)S(1)}, u32[]{:S(2)}, u32[]{:S(2)}) collective-permute-start(f16[200,128]{1,0:T(8,128)(2,1)S(1)} %get-tuple-element.59), channel_id=1, source_target_pairs={{0,5},{1,2},{2,1},{3,6},{4,7},{5,0},{6,3},{7,4},{8,13},{9,10},{10,... | collective-permute-start | bytes 153608 | tf_op jit(solution)/shard_map/ppermute | solution.py:33
  18.4 1.2 %collective-permute-start.4 = (f32[12,512]{1,0:T(8,128)S(1)}, f32[12,512]{1,0:T(8,128)S(1)}, u32[]{:S(2)}, u32[]{:S(2)}) collective-permute-start(f32[12,512]{1,0:T(8,128)S(1)} %shard_map.78), channel_id=1, source_target_pairs={{0,1},{1,0},{2,3},{3,2},{4,5},{5,4},{6,7},{7,6},{8,9},{9,8},{10,11... | collective-permute-start | bytes 73736 | tf_op jit(solution)/shard_map/ppermute | solution.py:33
  19.6 4.6 %collective-permute-start.5 = (bf16[48,128]{1,0:T(8,128)(2,1)S(1)}, bf16[48,128]{1,0:T(8,128)(2,1)S(1)}, u32[]{:S(2)}, u32[]{:S(2)}) collective-permute-start(bf16[48,128]{1,0:T(8,128)(2,1)S(1)} %reshape.21.after), channel_id=1, source_target_pairs={{0,9},{1,8},{2,11},{3,10},{4,13},{5,12},{6,15},{7,14},{8,1},{9,0},... | collective-permute-start | bytes 36872 | tf_op jit(solution)/shard_map/ppermute | solution.py:33
  24.2 3.3 %collective-permute-start.6 = (bf16[96,128]{1,0:T(8,128)(2,1)S(1)}, bf16[96,128]{1,0:T(8,128)(2,1)S(1)}, u32[]{:S(2)}, u32[]{:S(2)}) collective-permute-start(bf16[96,128]{1,0:T(8,128)(2,1)S(1)} %maximum_select_fusion.1), channel_id=1, source_target_pairs={{0,3},{1,4},{2,7},{3,0},{4,1},{5,6},{6,5},{7,2},{8,11},{9,12},{10,... | collective-permute-start | bytes 73736 | tf_op jit(solution)/shard_map/ppermute | solution.py:33
  27.5 3.5 %collective-permute-start.7 = (bf16[192,128]{1,0:T(8,128)(2,1)S(1)}, bf16[192,128]{1,0:T(8,128)(2,1)S(1)}, u32[]{:S(2)}, u32[]{:S(2)}) collective-permute-start(bf16[192,128]{1,0:T(8,128)(2,1)S(1)} %pad_maximum_fusion.4.mine), channel_id=1, source_target_pairs={{0,5},{1,2},{2,1},{3,6},{4,7},{5,0},{6,3},{7,4},{8,13},{9,10},{10,... | collective-permute-start | bytes 147464 | tf_op jit(solution)/shard_map/ppermute | solution.py:33

commit v9 on v8

--- a/solution.py
+++ b/solution.py
@@ -13,14 +13,17 @@
 VMEM_LIMIT = 16 << 20
 
 
-def far_distances():
+def plans():
     size = lax.axis_size("ctx")
-    return [size >> step for step in range(1, size.bit_length() - 2)]
-
-
-def near_distance(c, p, last):
-    even = (c ^ (c >> 1) ^ p ^ last) & 1
-    return 1 + even
+    far = [size >> step for step in range(1, size.bit_length() - 3)]
+    return far + [4, 1, 2], far + [2, 4, 1]
+
+
+def family(c, p):
+    total = p
+    for step in range(lax.axis_size("ctx").bit_length() - 1):
+        total = total ^ (c >> step)
+    return total & 1
 
 
 def swap(block, partner):
@@ -37,24 +40,18 @@
     return swap(block, lambda c, p: (c, p ^ 1))
 
 
-def swap_far(block, distance):
-    return swap(block, lambda c, p: (c ^ distance, p ^ 1))
-
-
-def swap_near(block, last):
-    return swap(block, lambda c, p: (c ^ near_distance(c, p, last), p ^ 1))
-
-
-def ordered(own, other, distance):
-    upper = (lax.axis_index("ctx") & distance) != 0
-    return jnp.where(upper, jnp.concatenate([other, own]), jnp.concatenate([own, other]))
-
-
-def position():
-    index, place = lax.axis_index("ctx"), 0
-    for step, distance in enumerate(far_distances()):
-        place = place + jnp.where((index & distance) != 0, 1 << step, 0)
-    return place
+def exchange(block, turn):
+    both = plans()
+    return swap(block, lambda c, p: (c ^ both[family(c, p)][turn], p ^ 1))
+
+
+def owner(place):
+    c = lax.axis_index("ctx")
+    second = family(c, lax.axis_index("col"))
+    for turn, (one, two) in enumerate(zip(*plans())):
+        if (place >> turn) & 1:
+            c = c ^ (one + (two - one) * second)
+    return c
 
 
 def kept(space, *arrays):
@@ -117,7 +114,7 @@
     mask[...] = (jnp.broadcast_to(ids[...], mask.shape) - first == rows).astype(jnp.float32)
     shape = numbers.shape
     row = lax.broadcasted_iota(jnp.int32, shape, 0)
-    place = row % 2 * LANES + lax.broadcasted_iota(jnp.int32, shape, 1) - SLOTS * position()
+    place = row % 2 * LANES + lax.broadcasted_iota(jnp.int32, shape, 1)
     first = jnp.broadcast_to(ids[:, :1], shape)
     value = jnp.where(row < 4, first + place, 1)
     owned = (place >= 0) & (place < SLOTS) & (row % 4 < 2)
@@ -280,20 +277,17 @@
     )(*kept(pltpu.HBM, array), *kept(pltpu.VMEM, after))
 
 
-def column_products(width, rows, held, pair, offsets, store):
+def column_products(width, rows, start, blocks, store):
     pieces = width // LANES
-    bits = held.bit_length() - 1
     total = None
-    for n, offset in enumerate(offsets):
-        low = (lax.axis_index("ctx") & 3) ^ offset
-        blocks, columns = [], [[] for _ in range(pieces)]
-        for place in range(held):
-            high = sum(((place >> k) & 1) << (bits - 1 - k) for k in range(bits))
-            blocks.append(pair[pl.ds((n * held + place) * rows, rows), :])
+    for pair in range(0, blocks.shape[0] // rows, 2):
+        columns = [[] for _ in range(pieces)]
+        for place in (pair, pair + 1):
+            shard = owner(start + place)
             for k in range(pieces):
-                at = pl.multiple_of((high * 4 + low) * width + k * LANES, LANES)
+                at = pl.multiple_of(shard * width + k * LANES, LANES)
                 columns[k].append(store[:, pl.ds(at, LANES)])
-        left = jnp.concatenate(blocks, 1)
+        left = jnp.concatenate([blocks[pl.ds((pair + n) * rows, rows), :] for n in range(2)], 1)
         right = jnp.concatenate([jnp.concatenate(column, 1) for column in columns])
         term = lax.dot_general(
             left, right, (((1,), (1,)), ((), ())), preferred_element_type=jnp.float32
@@ -303,18 +297,13 @@
 
 
 def held_kernel(width, mine, store, out):
-    rows = out.shape[0]
-    first = near_distance(lax.axis_index("ctx"), lax.axis_index("col"), 0)
-    held = mine.shape[0] // (2 * rows)
-    out[...] = column_products(width, rows, held, mine, (0, first), store)
+    out[...] = column_products(width, out.shape[0], 0, mine, store)
 
 
 def score_kernel(width, known, theirs, store, out, products):
     rows, count = known.shape[0], store.shape[0]
     pieces = width // LANES
-    second = near_distance(lax.axis_index("ctx"), lax.axis_index("col"), 1)
-    held = theirs.shape[0] // (2 * rows)
-    total = known[...] + column_products(width, rows, held, theirs, (second, 3), store)
+    total = known[...] + column_products(width, rows, theirs.shape[0] // rows, theirs, store)
     for n in range(products.shape[0] // rows):
         products[pl.ds(n * rows, rows), :] = total[:, n * LANES : (n + 1) * LANES]
     result = None
@@ -360,38 +349,36 @@
     sums, tags = outer(part, swap_cores(part), mask, numbers)
     blocks, tags = sums.astype(jnp.float16), tags.astype(jnp.float16)
     depth = inverse.shape[0]
-    cuts = [0] + [depth * k // 8 // LANES * LANES for k in ((2, 5) if far_distances() else (4,))] + [depth]
+    turns = len(plans()[0])
+    cuts = [0] + [depth * k // 8 // LANES * LANES for k in (2, 5)] + [depth]
     highs, lows = [], []
 
-    def beside(exchange, payload, ready):
-        other, at = exchange(payload), len(highs)
+    def beside(payload, turn, ready):
+        other, at = exchange(payload, turn), len(highs)
         pair = fetch(inverse, cuts[at], cuts[at + 1] - cuts[at], ready)
         other, high, low = lax.optimization_barrier((other, *pair))
         highs.append(high)
         lows.append(low)
         return other
 
-    for distance in far_distances():
+    for turn in range(turns - 1):
         size = blocks.shape[0]
-        exchange = functools.partial(swap_far, distance=distance)
         payload = jnp.concatenate([blocks, tags])
-        if distance == far_distances()[-1]:
-            other = beside(exchange, payload, tags.astype(jnp.float32))
+        if turn < turns - 3:
+            other = exchange(payload, turn)
         else:
-            other = exchange(payload)
-        blocks = ordered(blocks, other[:size], distance)
-        tags = tags + other[size:]
-    size = blocks.shape[0]
-    payload = jnp.concatenate([blocks, tags])
-    other = beside(functools.partial(swap_near, last=0), payload, tags.astype(jnp.float32))
-    blocks = jnp.concatenate([blocks, other[:size]])
-    tags = tags + jnp.roll(other[size:], 2, 0)
+            other = beside(payload, turn, tags.astype(jnp.float32))
+        blocks = jnp.concatenate([blocks, other[:size]])
+        if turn < turns - 2:
+            tags = tags + jnp.roll(other[size:], SLOTS << turn, 1)
+        else:
+            tags = tags + jnp.roll(other[size:], 2, 0)
     halves = blocks.reshape(-1, 2, half * rank // LANES, LANES)
     first = lax.axis_index("col") == 0
     own = jnp.where(first, halves[:, 0], halves[:, 1]).reshape(-1, LANES)
     others = jnp.where(first, halves[:, 1], halves[:, 0]).reshape(-1, LANES)
     own = jnp.concatenate([own, tags]).astype(jnp.float32)
-    other = beside(functools.partial(swap_near, last=1), jnp.concatenate([others, tags]), own)
+    other = beside(jnp.concatenate([others, tags]), turns - 1, own)
     partial_q = precondition(own, other.astype(jnp.float32), highs, lows, doc_count)
     precond = (partial_q + swap_cores(partial_q)).astype(jnp.bfloat16)
     width = precond.shape[1]
@@ -400,29 +387,21 @@
     direct = width % LANES == 0 and LANES % count == 0 and width * count % LANES**2 == 0
     if direct:
         store = load(store_rows, whole)
-    for step, distance in enumerate(far_distances()):
-        other = swap_far(whole, distance)
-        if direct and step == 0:
+    for turn in range(turns - 1):
+        other = exchange(whole, turn)
+        if direct and turn == 0:
             other, store = lax.optimization_barrier((other, store))
-        whole = ordered(whole, other, distance)
-    whole = jnp.concatenate([whole, swap_near(whole, 0)])
-    others = swap_near(whole, 1)
+        whole = jnp.concatenate([whole, other])
+    others = exchange(whole, turns - 1)
     if direct:
         known = score_held(whole, store, width, doc_count)
         others, known = lax.optimization_barrier((others, known))
         return score(known, others, store, width, doc_count)
-    (own, near), (next_one, farthest) = (x.reshape(2, -1, x.shape[1]) for x in (whole, others))
-    c, p = lax.axis_index("ctx"), lax.axis_index("col")
-    single = near_distance(c, p, 0) == 1
-    near, next_one = jnp.where(single, near, next_one), jnp.where(single, next_one, near)
-    whole = jnp.stack([own, near, next_one, farthest])
-    for bit in (1, 2):
-        pairs = whole.reshape((2 // bit, 2, bit) + whole.shape[1:])
-        whole = jnp.where((c & bit) != 0, pairs[:, ::-1], pairs).reshape(whole.shape)
-    bits = len(far_distances())
-    whole = whole.reshape((4,) + (2,) * bits + (doc_count, width))
-    whole = whole.transpose((bits + 1,) + tuple(range(1, bits + 1))[::-1] + (0, bits + 2))
-    whole = whole.reshape(doc_count, -1)
+    whole = jnp.concatenate([whole, others]).reshape(ctx, doc_count, width)
+    owners = jnp.stack([owner(place) for place in range(ctx)])
+    found = owners[None, :] == jnp.arange(ctx, dtype=owners.dtype)[:, None]
+    whole = jnp.take(whole, jnp.argmax(found, axis=1), axis=0)
+    whole = whole.transpose(1, 0, 2).reshape(doc_count, -1)
     return lax.dot_general(
         whole, store_rows, (((1,), (1,)), ((), ())), preferred_element_type=jnp.float32
     )

time: 32.2 us -> 32 us (level)
  no operation moved by 1% of the time
where the time goes in v9:
time: 32 us; the launch traced here: 31.6 us
  starting transfers between devices  14 us (44%)
  Pallas kernels  10.4 us (32%)
  waiting for transfers between devices  6.71 us (21%)
    ppermute x8, starting transfers between devices, swap(): return lax.ppermute(block, ('ctx', 'col'), route)  14 us
    ppermute x8, waiting for transfers between devices, swap(): return lax.ppermute(block, ('ctx', 'col'), route)  6.71 us
    pallas_call x3, Pallas kernels, fetch(): pl.pallas_call(functools.partial(fetch_kernel, start, chunk), out_shape=(...  4.13 us
    pallas_call x1, Pallas kernels, project(): pl.pallas_call(functools.partial(project_kernel, cuts), out_shape=(pltpu....  2.83 us
    pallas_call x1, Pallas kernels, load(): pl.pallas_call(load_kernel, out_shape=pltpu.VMEM(array.shape, array.dtype...  1.05 us
    pallas_call x1, Pallas kernels, precondition(): pl.pallas_call(functools.partial(precondition_kernel, len(highs)), out_sh...  0.97 us
    pallas_call x1, Pallas kernels, score(): pl.pallas_call(functools.partial(score_kernel, width), out_shape=jax.Shap...  0.88 us
  transfers between devices with their start and end apart: 8, of which 8 were waited for; matrix products, arithmetic and copies ran while one was open for 0% of the time, Pallas kernels for 17%

profile of v9, /device:TPU:0, one launch (start us, length us, event | category | flops | bytes accessed | tf_op | source)
XLA Modules:
  0.0 31.6 jit_solution(10411838642731506127)
XLA Ops:
  0.0 2.8 %shard_map.73 = (f32[128,128]{1,0:T(8,128)S(1)}, f32[8,128]{1,0:T(8,128)S(1)}, f32[8,128]{1,0:T(8,128)S(1)}) custom-call(s32[1,128]{1,0:T(1,128)} %bitcast.11, bf16[128,2048]{1,0:T(8,128)(2,1)} %act_hbm.1, bf16[64,2048]{1,0:T(8,128)(2,1)} %bitcast.8, bf16[128,7168]{1,0:T(8,128)(2,1)} %grad_hbm.1, bf16[64,7168]{1,0:T(8,128)(2,1)} %bitcast.6), custom_call_target="tpu_custom_call" | custom-call | tf_op jit(solution)/shard_map/pallas_call | solution.py:142
  2.8 0.6 %collective-permute-start = (f32[128,128]{1,0:T(8,128)S(1)}, f32[128,128]{1,0:T(8,128)S(1)}, u32[]{:S(2)}, u32[]{:S(2)}) collective-permute-start(f32[128,128]{1,0:T(8,128)S(1)} %get-tuple-element.29.part), channel_id=1, source_target_pairs={{0,1},{1,0},{2,3},{3,2},{4,5},{5,4},{6,7},{7,6},{8,9},{9,8},{10,11... | collective-permute-start | bytes 196616 | tf_op jit(solution)/shard_map/ppermute | solution.py:36
  3.4 0.9 %collective-permute-done.other = f32[128,128]{1,0:T(8,128)S(1)} collective-permute-done((f32[128,128]{1,0:T(8,128)S(1)}, f32[128,128]{1,0:T(8,128)S(1)}, u32[]{:S(2)}, u32[]{:S(2)}) %collective-permute-start) | collective-permute-done | bytes 65568 | tf_op jit(solution)/shard_map/ppermute | solution.py:36
  4.3 0.3 shard_map.74
  4.7 3.8 %collective-permute-start.1 = (f16[104,128]{1,0:T(8,128)(2,1)S(1)}, f16[104,128]{1,0:T(8,128)(2,1)S(1)}, u32[]{:S(2)}, u32[]{:S(2)}) collective-permute-start(f16[104,128]{1,0:T(8,128)(2,1)S(1)} %pad_maximum_fusion.4), channel_id=1, source_target_pairs={{0,9},{1,4},{2,7},{3,10},{4,1},{5,12},{6,15},{7,2},{8,13},{9,0},{1... | collective-permute-start | bytes 79880 | tf_op jit(solution)/shard_map/ppermute | solution.py:36
  8.4 1.3 %shard_map.75 = (bf16[512,512]{1,0:T(8,128)(2,1)S(1)}, bf16[512,512]{1,0:T(8,128)(2,1)S(1)}) custom-call(f32[2048,512]{1,0:T(8,128)} %array.5, f32[8,128]{1,0:T(8,128)S(1)} %get-tuple-element.55.after), custom_call_target="tpu_custom_call" | custom-call | tf_op jit(solution)/shard_map/pallas_call | solution.py:83
  9.7 0.3 collective-permute-done.1
  10.0 0.1 slice.37
  10.0 0.1 fusion.1
  10.2 1.6 %collective-permute-start.2 = (f16[200,128]{1,0:T(8,128)(2,1)S(1)}, f16[200,128]{1,0:T(8,128)(2,1)S(1)}, u32[]{:S(2)}, u32[]{:S(2)}) collective-permute-start(f16[200,128]{1,0:T(8,128)(2,1)S(1)} %pad_maximum_fusion.3), channel_id=1, source_target_pairs={{0,3},{1,8},{2,11},{3,0},{4,13},{5,6},{6,5},{7,14},{8,1},{9,10},{1... | collective-permute-start | bytes 153608 | tf_op jit(solution)/shard_map/ppermute | solution.py:36
  11.8 1.4 %shard_map.76 = (bf16[768,512]{1,0:T(8,128)(2,1)S(1)}, bf16[768,512]{1,0:T(8,128)(2,1)S(1)}) custom-call(f32[2048,512]{1,0:T(8,128)} %array.5, f32[8,128]{1,0:T(8,128)S(1)} %get-tuple-element.53.after), custom_call_target="tpu_custom_call" | custom-call | tf_op jit(solution)/shard_map/pallas_call | solution.py:83
  13.2 0.6 %collective-permute-done.2 = f16[200,128]{1,0:T(8,128)(2,1)S(1)} collective-permute-done((f16[200,128]{1,0:T(8,128)(2,1)S(1)}, f16[200,128]{1,0:T(8,128)(2,1)S(1)}, u32[]{:S(2)}, u32[]{:S(2)}) %collective-permute-start.2) | collective-permute-done | bytes 51232 | tf_op jit(solution)/shard_map/ppermute | solution.py:36
  13.9 1.7 %collective-permute-start.3 = (f16[200,128]{1,0:T(8,128)(2,1)S(1)}, f16[200,128]{1,0:T(8,128)(2,1)S(1)}, u32[]{:S(2)}, u32[]{:S(2)}) collective-permute-start(f16[200,128]{1,0:T(8,128)(2,1)S(1)} %get-tuple-element.59), channel_id=1, source_target_pairs={{0,5},{1,2},{2,1},{3,6},{4,7},{5,0},{6,3},{7,4},{8,11},{9,12},{10,... | collective-permute-start | bytes 153608 | tf_op jit(solution)/shard_map/ppermute | solution.py:36
  15.7 1.4 %shard_map.77 = (bf16[768,512]{1,0:T(8,128)(2,1)S(1)}, bf16[768,512]{1,0:T(8,128)(2,1)S(1)}) custom-call(f32[2048,512]{1,0:T(8,128)} %array.5, f32[200,128]{1,0:T(8,128)S(1)} %get-tuple-element.60.after.own), custom_call_target="tpu_custom_call" | custom-call | tf_op jit(solution)/shard_map/pallas_call | solution.py:83
  17.1 0.4 %collective-permute-done.3 = f16[200,128]{1,0:T(8,128)(2,1)S(1)} collective-permute-done((f16[200,128]{1,0:T(8,128)(2,1)S(1)}, f16[200,128]{1,0:T(8,128)(2,1)S(1)}, u32[]{:S(2)}, u32[]{:S(2)}) %collective-permute-start.3) | collective-permute-done | bytes 51232 | tf_op jit(solution)/shard_map/ppermute | solution.py:36
  17.5 1.0 %shard_map.78 = f32[12,512]{1,0:T(8,128)S(1)} custom-call(f32[200,128]{1,0:T(8,128)S(1)} %get-tuple-element.60.after.own, f32[200,128]{1,0:T(8,128)S(1)} %convert_element_type.26.other, bf16[512,512]{1,0:T(8,128)(2,1)S(1)} %get-tuple-element.43.refs_0_, bf16[768,512]{1,0:T(8,128)(2,1)S(1)} %get-tuple-element.44.refs_1_, ...), custom_call_target="tpu_custom_call" | custom-call | tf_op jit(solution)/shard_map/pallas_call | solution.py:252
  18.5 0.4 %collective-permute-start.4 = (f32[12,512]{1,0:T(8,128)S(1)}, f32[12,512]{1,0:T(8,128)S(1)}, u32[]{:S(2)}, u32[]{:S(2)}) collective-permute-start(f32[12,512]{1,0:T(8,128)S(1)} %shard_map.78), channel_id=1, source_target_pairs={{0,1},{1,0},{2,3},{3,2},{4,5},{5,4},{6,7},{7,6},{8,9},{9,8},{10,11... | collective-permute-start | bytes 73736 | tf_op jit(solution)/shard_map/ppermute | solution.py:36
  18.9 0.9 %collective-permute-done.4 = f32[12,512]{1,0:T(8,128)S(1)} collective-permute-done((f32[12,512]{1,0:T(8,128)S(1)}, f32[12,512]{1,0:T(8,128)S(1)}, u32[]{:S(2)}, u32[]{:S(2)}) %collective-permute-start.4) | collective-permute-done | bytes 24608 | tf_op jit(solution)/shard_map/ppermute | solution.py:36
  19.8 2.7 %collective-permute-start.5 = (bf16[48,128]{1,0:T(8,128)(2,1)S(1)}, bf16[48,128]{1,0:T(8,128)(2,1)S(1)}, u32[]{:S(2)}, u32[]{:S(2)}) collective-permute-start(bf16[48,128]{1,0:T(8,128)(2,1)S(1)} %reshape.21.after), channel_id=1, source_target_pairs={{0,9},{1,4},{2,7},{3,10},{4,1},{5,12},{6,15},{7,2},{8,13},{9,0},{1... | collective-permute-start | bytes 36872 | tf_op jit(solution)/shard_map/ppermute | solution.py:36
  22.5 1.0 %shard_map.79.store = bf16[64,4096]{1,0:T(8,128)(2,1)S(1)} custom-call(bf16[64,4096]{1,0:T(8,128)(2,1)} %source.1, bf16[48,128]{1,0:T(8,128)(2,1)S(1)} %reshape.21.after), custom_call_target="tpu_custom_call" | custom-call | tf_op jit(solution)/shard_map/pallas_call | solution.py:270
  23.6 0.3 %collective-permute-done.5 = bf16[48,128]{1,0:T(8,128)(2,1)S(1)} collective-permute-done((bf16[48,128]{1,0:T(8,128)(2,1)S(1)}, bf16[48,128]{1,0:T(8,128)(2,1)S(1)}, u32[]{:S(2)}, u32[]{:S(2)}) %collective-permute-start.5) | collective-permute-done | bytes 12320 | tf_op jit(solution)/shard_map/ppermute | solution.py:36
  23.9 1.4 %collective-permute-start.6 = (bf16[96,128]{1,0:T(8,128)(2,1)S(1)}, bf16[96,128]{1,0:T(8,128)(2,1)S(1)}, u32[]{:S(2)}, u32[]{:S(2)}) collective-permute-start(bf16[96,128]{1,0:T(8,128)(2,1)S(1)} %pad_maximum_fusion.5), channel_id=1, source_target_pairs={{0,3},{1,8},{2,11},{3,0},{4,13},{5,6},{6,5},{7,14},{8,1},{9,10},{1... | collective-permute-start | bytes 73736 | tf_op jit(solution)/shard_map/ppermute | solution.py:36
  25.4 1.8 %collective-permute-done.6 = bf16[96,128]{1,0:T(8,128)(2,1)S(1)} collective-permute-done((bf16[96,128]{1,0:T(8,128)(2,1)S(1)}, bf16[96,128]{1,0:T(8,128)(2,1)S(1)}, u32[]{:S(2)}, u32[]{:S(2)}) %collective-permute-start.6) | collective-permute-done | bytes 24608 | tf_op jit(solution)/shard_map/ppermute | solution.py:36
  27.2 1.7 %collective-permute-start.7 = (bf16[192,128]{1,0:T(8,128)(2,1)S(1)}, bf16[192,128]{1,0:T(8,128)(2,1)S(1)}, u32[]{:S(2)}, u32[]{:S(2)}) collective-permute-start(bf16[192,128]{1,0:T(8,128)(2,1)S(1)} %constant_dynamic-update-slice_fusion.mine), channel_id=1, source_target_pairs={{0,5},{1,2},{2,1},{3,6},{4,7},{5,0},{6,3},{7,4},{8,11},{9,12},{10,... | collective-permute-start | bytes 147464 | tf_op jit(solution)/shard_map/ppermute | solution.py:36
  28.9 0.2 shard_map.80.known
  29.2 1.6 %collective-permute-done.7.theirs = bf16[192,128]{1,0:T(8,128)(2,1)S(1)} collective-permute-done((bf16[192,128]{1,0:T(8,128)(2,1)S(1)}, bf16[192,128]{1,0:T(8,128)(2,1)S(1)}, u32[]{:S(2)}, u32[]{:S(2)}) %collective-permute-start.7) | collective-permute-done | bytes 49184 | tf_op jit(solution)/shard_map/ppermute | solution.py:36
  30.7 0.9 %shard_map.81 = f32[12,64]{1,0:T(8,128)} custom-call(f32[48,256]{1,0:T(8,128)S(1)} %shard_map.80.known, bf16[192,128]{1,0:T(8,128)(2,1)S(1)} %collective-permute-done.7.theirs, bf16[64,4096]{1,0:T(8,128)(2,1)S(1)} %shard_map.79.store), custom_call_target="tpu_custom_call" | custom-call | tf_op jit(solution)/shard_map/pallas_call | solution.py:333
  (20 shorter events, 0.3 us)
Async XLA Ops:
  2.8 1.5 %collective-permute-start = (f32[128,128]{1,0:T(8,128)S(1)}, f32[128,128]{1,0:T(8,128)S(1)}, u32[]{:S(2)}, u32[]{:S(2)}) collective-permute-start(f32[128,128]{1,0:T(8,128)S(1)} %get-tuple-element.29.part), channel_id=1, source_target_pairs={{0,1},{1,0},{2,3},{3,2},{4,5},{5,4},{6,7},{7,6},{8,9},{9,8},{10,11... | collective-permute-start | bytes 196616 | tf_op jit(solution)/shard_map/ppermute | solution.py:36
  4.7 5.3 %collective-permute-start.1 = (f16[104,128]{1,0:T(8,128)(2,1)S(1)}, f16[104,128]{1,0:T(8,128)(2,1)S(1)}, u32[]{:S(2)}, u32[]{:S(2)}) collective-permute-start(f16[104,128]{1,0:T(8,128)(2,1)S(1)} %pad_maximum_fusion.4), channel_id=1, source_target_pairs={{0,9},{1,4},{2,7},{3,10},{4,1},{5,12},{6,15},{7,2},{8,13},{9,0},{1... | collective-permute-start | bytes 79880 | tf_op jit(solution)/shard_map/ppermute | solution.py:36
  10.2 3.6 %collective-permute-start.2 = (f16[200,128]{1,0:T(8,128)(2,1)S(1)}, f16[200,128]{1,0:T(8,128)(2,1)S(1)}, u32[]{:S(2)}, u32[]{:S(2)}) collective-permute-start(f16[200,128]{1,0:T(8,128)(2,1)S(1)} %pad_maximum_fusion.3), channel_id=1, source_target_pairs={{0,3},{1,8},{2,11},{3,0},{4,13},{5,6},{6,5},{7,14},{8,1},{9,10},{1... | collective-permute-start | bytes 153608 | tf_op jit(solution)/shard_map/ppermute | solution.py:36
  13.9 3.6 %collective-permute-start.3 = (f16[200,128]{1,0:T(8,128)(2,1)S(1)}, f16[200,128]{1,0:T(8,128)(2,1)S(1)}, u32[]{:S(2)}, u32[]{:S(2)}) collective-permute-start(f16[200,128]{1,0:T(8,128)(2,1)S(1)} %get-tuple-element.59), channel_id=1, source_target_pairs={{0,5},{1,2},{2,1},{3,6},{4,7},{5,0},{6,3},{7,4},{8,11},{9,12},{10,... | collective-permute-start | bytes 153608 | tf_op jit(solution)/shard_map/ppermute | solution.py:36
  18.5 1.3 %collective-permute-start.4 = (f32[12,512]{1,0:T(8,128)S(1)}, f32[12,512]{1,0:T(8,128)S(1)}, u32[]{:S(2)}, u32[]{:S(2)}) collective-permute-start(f32[12,512]{1,0:T(8,128)S(1)} %shard_map.78), channel_id=1, source_target_pairs={{0,1},{1,0},{2,3},{3,2},{4,5},{5,4},{6,7},{7,6},{8,9},{9,8},{10,11... | collective-permute-start | bytes 73736 | tf_op jit(solution)/shard_map/ppermute | solution.py:36
  19.8 4.1 %collective-permute-start.5 = (bf16[48,128]{1,0:T(8,128)(2,1)S(1)}, bf16[48,128]{1,0:T(8,128)(2,1)S(1)}, u32[]{:S(2)}, u32[]{:S(2)}) collective-permute-start(bf16[48,128]{1,0:T(8,128)(2,1)S(1)} %reshape.21.after), channel_id=1, source_target_pairs={{0,9},{1,4},{2,7},{3,10},{4,1},{5,12},{6,15},{7,2},{8,13},{9,0},{1... | collective-permute-start | bytes 36872 | tf_op jit(solution)/shard_map/ppermute | solution.py:36
  23.9 3.3 %collective-permute-start.6 = (bf16[96,128]{1,0:T(8,128)(2,1)S(1)}, bf16[96,128]{1,0:T(8,128)(2,1)S(1)}, u32[]{:S(2)}, u32[]{:S(2)}) collective-permute-start(bf16[96,128]{1,0:T(8,128)(2,1)S(1)} %pad_maximum_fusion.5), channel_id=1, source_target_pairs={{0,3},{1,8},{2,11},{3,0},{4,13},{5,6},{6,5},{7,14},{8,1},{9,10},{1... | collective-permute-start | bytes 73736 | tf_op jit(solution)/shard_map/ppermute | solution.py:36
  27.2 3.5 %collective-permute-start.7 = (bf16[192,128]{1,0:T(8,128)(2,1)S(1)}, bf16[192,128]{1,0:T(8,128)(2,1)S(1)}, u32[]{:S(2)}, u32[]{:S(2)}) collective-permute-start(bf16[192,128]{1,0:T(8,128)(2,1)S(1)} %constant_dynamic-update-slice_fusion.mine), channel_id=1, source_target_pairs={{0,5},{1,2},{2,1},{3,6},{4,7},{5,0},{6,3},{7,4},{8,11},{9,12},{10,... | collective-permute-start | bytes 147464 | tf_op jit(solution)/shard_map/ppermute | solution.py:36

commit v10 on v9

--- a/solution.py
+++ b/solution.py
@@ -209,7 +209,8 @@
     rows, depth = pieces.shape
     size = own.shape[0] - 8
     count = size * LANES // depth
-    pieces[...] = jnp.zeros_like(pieces)
+    if rows > 2 * count:
+        pieces[...] = jnp.zeros_like(pieces)
     for k in range(depth // LANES):
         for n, part in enumerate((own, other)):
             pieces[pl.ds(n * count, count), pl.ds(k * LANES, LANES)] = part[
@@ -368,15 +369,18 @@
             other = exchange(payload, turn)
         else:
             other = beside(payload, turn, tags.astype(jnp.float32))
-        blocks = jnp.concatenate([blocks, other[:size]])
         if turn < turns - 2:
+            blocks = jnp.concatenate([blocks, other[:size]])
             tags = tags + jnp.roll(other[size:], SLOTS << turn, 1)
         else:
             tags = tags + jnp.roll(other[size:], 2, 0)
-    halves = blocks.reshape(-1, 2, half * rank // LANES, LANES)
     first = lax.axis_index("col") == 0
-    own = jnp.where(first, halves[:, 0], halves[:, 1]).reshape(-1, LANES)
-    others = jnp.where(first, halves[:, 1], halves[:, 0]).reshape(-1, LANES)
+    own, others = [], []
+    for part in (blocks, other[:size]):
+        halves = part.reshape(-1, 2, half * rank // LANES, LANES)
+        own.append(jnp.where(first, halves[:, 0], halves[:, 1]).reshape(-1, LANES))
+        others.append(jnp.where(first, halves[:, 1], halves[:, 0]).reshape(-1, LANES))
+    own, others = jnp.concatenate(own), jnp.concatenate(others)
     own = jnp.concatenate([own, tags]).astype(jnp.float32)
     other = beside(jnp.concatenate([others, tags]), turns - 1, own)
     partial_q = precondition(own, other.astype(jnp.float32), highs, lows, doc_count)

time: 32 us -> 31.9 us (level)
  no operation moved by 1% of the time
where the time goes in v10:
time: 31.9 us; the launch traced here: 31.6 us
  starting transfers between devices  14 us (44%)
  Pallas kernels  10.4 us (33%)
  waiting for transfers between devices  6.68 us (21%)
    ppermute x8, starting transfers between devices, swap(): return lax.ppermute(block, ('ctx', 'col'), route)  14 us
    ppermute x8, waiting for transfers between devices, swap(): return lax.ppermute(block, ('ctx', 'col'), route)  6.68 us
    pallas_call x3, Pallas kernels, fetch(): pl.pallas_call(functools.partial(fetch_kernel, start, chunk), out_shape=(...  4.14 us
    pallas_call x1, Pallas kernels, project(): pl.pallas_call(functools.partial(project_kernel, cuts), out_shape=(pltpu....  2.83 us
    pallas_call x1, Pallas kernels, load(): pl.pallas_call(load_kernel, out_shape=pltpu.VMEM(array.shape, array.dtype...  1.05 us
    pallas_call x1, Pallas kernels, precondition(): pl.pallas_call(functools.partial(precondition_kernel, len(highs)), out_sh...  0.97 us
    pallas_call x1, Pallas kernels, score(): pl.pallas_call(functools.partial(score_kernel, width), out_shape=jax.Shap...  0.88 us
  transfers between devices with their start and end apart: 8, of which 8 were waited for; matrix products, arithmetic and copies ran while one was open for 0% of the time, Pallas kernels for 17%

profile of v10, /device:TPU:0, one launch (start us, length us, event | category | flops | bytes accessed | tf_op | source)
XLA Modules:
  0.0 31.6 jit_solution(9650055805519047735)
XLA Ops:
  0.0 2.8 %shard_map.73 = (f32[128,128]{1,0:T(8,128)S(1)}, f32[8,128]{1,0:T(8,128)S(1)}, f32[8,128]{1,0:T(8,128)S(1)}) custom-call(s32[1,128]{1,0:T(1,128)} %bitcast.17, bf16[128,2048]{1,0:T(8,128)(2,1)} %act_hbm.1, bf16[64,2048]{1,0:T(8,128)(2,1)} %bitcast.10, bf16[128,7168]{1,0:T(8,128)(2,1)} %grad_hbm.1, bf16[64,7168]{1,0:T(8,128)(2,1)} %bitcast.9), custom_call_target="tpu_custom_call" | custom-call | tf_op jit(solution)/shard_map/pallas_call | solution.py:142
  2.8 0.6 %collective-permute-start = (f32[128,128]{1,0:T(8,128)S(1)}, f32[128,128]{1,0:T(8,128)S(1)}, u32[]{:S(2)}, u32[]{:S(2)}) collective-permute-start(f32[128,128]{1,0:T(8,128)S(1)} %get-tuple-element.29.part), channel_id=1, source_target_pairs={{0,1},{1,0},{2,3},{3,2},{4,5},{5,4},{6,7},{7,6},{8,9},{9,8},{10,11... | collective-permute-start | bytes 196616 | tf_op jit(solution)/shard_map/ppermute | solution.py:36
  3.4 0.9 %collective-permute-done.other = f32[128,128]{1,0:T(8,128)S(1)} collective-permute-done((f32[128,128]{1,0:T(8,128)S(1)}, f32[128,128]{1,0:T(8,128)S(1)}, u32[]{:S(2)}, u32[]{:S(2)}) %collective-permute-start) | collective-permute-done | bytes 65568 | tf_op jit(solution)/shard_map/ppermute | solution.py:36
  4.3 0.3 shard_map.74
  4.7 3.8 %collective-permute-start.1 = (f16[104,128]{1,0:T(8,128)(2,1)S(1)}, f16[104,128]{1,0:T(8,128)(2,1)S(1)}, u32[]{:S(2)}, u32[]{:S(2)}) collective-permute-start(f16[104,128]{1,0:T(8,128)(2,1)S(1)} %pad_maximum_fusion.4), channel_id=1, source_target_pairs={{0,9},{1,4},{2,7},{3,10},{4,1},{5,12},{6,15},{7,2},{8,13},{9,0},{1... | collective-permute-start | bytes 79880 | tf_op jit(solution)/shard_map/ppermute | solution.py:36
  8.4 1.3 %shard_map.75 = (bf16[512,512]{1,0:T(8,128)(2,1)S(1)}, bf16[512,512]{1,0:T(8,128)(2,1)S(1)}) custom-call(f32[2048,512]{1,0:T(8,128)} %array.5, f32[8,128]{1,0:T(8,128)S(1)} %get-tuple-element.55.after), custom_call_target="tpu_custom_call" | custom-call | tf_op jit(solution)/shard_map/pallas_call | solution.py:83
  9.7 0.3 collective-permute-done.1
  10.0 0.1 slice.47
  10.0 0.1 fusion.1
  10.2 1.6 %collective-permute-start.2 = (f16[200,128]{1,0:T(8,128)(2,1)S(1)}, f16[200,128]{1,0:T(8,128)(2,1)S(1)}, u32[]{:S(2)}, u32[]{:S(2)}) collective-permute-start(f16[200,128]{1,0:T(8,128)(2,1)S(1)} %pad_maximum_fusion.2), channel_id=1, source_target_pairs={{0,3},{1,8},{2,11},{3,0},{4,13},{5,6},{6,5},{7,14},{8,1},{9,10},{1... | collective-permute-start | bytes 153608 | tf_op jit(solution)/shard_map/ppermute | solution.py:36
  11.8 1.4 %shard_map.76 = (bf16[768,512]{1,0:T(8,128)(2,1)S(1)}, bf16[768,512]{1,0:T(8,128)(2,1)S(1)}) custom-call(f32[2048,512]{1,0:T(8,128)} %array.5, f32[8,128]{1,0:T(8,128)S(1)} %get-tuple-element.53.after), custom_call_target="tpu_custom_call" | custom-call | tf_op jit(solution)/shard_map/pallas_call | solution.py:83
  13.2 0.5 %collective-permute-done.2 = f16[200,128]{1,0:T(8,128)(2,1)S(1)} collective-permute-done((f16[200,128]{1,0:T(8,128)(2,1)S(1)}, f16[200,128]{1,0:T(8,128)(2,1)S(1)}, u32[]{:S(2)}, u32[]{:S(2)}) %collective-permute-start.2) | collective-permute-done | bytes 51232 | tf_op jit(solution)/shard_map/ppermute | solution.py:36
  13.9 1.7 %collective-permute-start.3 = (f16[200,128]{1,0:T(8,128)(2,1)S(1)}, f16[200,128]{1,0:T(8,128)(2,1)S(1)}, u32[]{:S(2)}, u32[]{:S(2)}) collective-permute-start(f16[200,128]{1,0:T(8,128)(2,1)S(1)} %get-tuple-element.61), channel_id=1, source_target_pairs={{0,5},{1,2},{2,1},{3,6},{4,7},{5,0},{6,3},{7,4},{8,11},{9,12},{10,... | collective-permute-start | bytes 153608 | tf_op jit(solution)/shard_map/ppermute | solution.py:36
  15.6 1.4 %shard_map.77 = (bf16[768,512]{1,0:T(8,128)(2,1)S(1)}, bf16[768,512]{1,0:T(8,128)(2,1)S(1)}) custom-call(f32[2048,512]{1,0:T(8,128)} %array.5, f32[200,128]{1,0:T(8,128)S(1)} %get-tuple-element.62.after.own), custom_call_target="tpu_custom_call" | custom-call | tf_op jit(solution)/shard_map/pallas_call | solution.py:83
  17.1 0.4 %collective-permute-done.3 = f16[200,128]{1,0:T(8,128)(2,1)S(1)} collective-permute-done((f16[200,128]{1,0:T(8,128)(2,1)S(1)}, f16[200,128]{1,0:T(8,128)(2,1)S(1)}, u32[]{:S(2)}, u32[]{:S(2)}) %collective-permute-start.3) | collective-permute-done | bytes 51232 | tf_op jit(solution)/shard_map/ppermute | solution.py:36
  17.5 1.0 %shard_map.78 = f32[12,512]{1,0:T(8,128)S(1)} custom-call(f32[200,128]{1,0:T(8,128)S(1)} %get-tuple-element.62.after.own, f32[200,128]{1,0:T(8,128)S(1)} %convert_element_type.26.other, bf16[512,512]{1,0:T(8,128)(2,1)S(1)} %get-tuple-element.43.refs_0_, bf16[768,512]{1,0:T(8,128)(2,1)S(1)} %get-tuple-element.44.refs_1_, ...), custom_call_target="tpu_custom_call" | custom-call | tf_op jit(solution)/shard_map/pallas_call | solution.py:253
  18.5 0.4 %collective-permute-start.4 = (f32[12,512]{1,0:T(8,128)S(1)}, f32[12,512]{1,0:T(8,128)S(1)}, u32[]{:S(2)}, u32[]{:S(2)}) collective-permute-start(f32[12,512]{1,0:T(8,128)S(1)} %shard_map.78), channel_id=1, source_target_pairs={{0,1},{1,0},{2,3},{3,2},{4,5},{5,4},{6,7},{7,6},{8,9},{9,8},{10,11... | collective-permute-start | bytes 73736 | tf_op jit(solution)/shard_map/ppermute | solution.py:36
  18.9 0.9 %collective-permute-done.4 = f32[12,512]{1,0:T(8,128)S(1)} collective-permute-done((f32[12,512]{1,0:T(8,128)S(1)}, f32[12,512]{1,0:T(8,128)S(1)}, u32[]{:S(2)}, u32[]{:S(2)}) %collective-permute-start.4) | collective-permute-done | bytes 24608 | tf_op jit(solution)/shard_map/ppermute | solution.py:36
  19.8 2.7 %collective-permute-start.5 = (bf16[48,128]{1,0:T(8,128)(2,1)S(1)}, bf16[48,128]{1,0:T(8,128)(2,1)S(1)}, u32[]{:S(2)}, u32[]{:S(2)}) collective-permute-start(bf16[48,128]{1,0:T(8,128)(2,1)S(1)} %reshape.35.after), channel_id=1, source_target_pairs={{0,9},{1,4},{2,7},{3,10},{4,1},{5,12},{6,15},{7,2},{8,13},{9,0},{1... | collective-permute-start | bytes 36872 | tf_op jit(solution)/shard_map/ppermute | solution.py:36
  22.5 1.0 %shard_map.79.store = bf16[64,4096]{1,0:T(8,128)(2,1)S(1)} custom-call(bf16[64,4096]{1,0:T(8,128)(2,1)} %source.1, bf16[48,128]{1,0:T(8,128)(2,1)S(1)} %reshape.35.after), custom_call_target="tpu_custom_call" | custom-call | tf_op jit(solution)/shard_map/pallas_call | solution.py:271
  23.6 0.3 %collective-permute-done.5 = bf16[48,128]{1,0:T(8,128)(2,1)S(1)} collective-permute-done((bf16[48,128]{1,0:T(8,128)(2,1)S(1)}, bf16[48,128]{1,0:T(8,128)(2,1)S(1)}, u32[]{:S(2)}, u32[]{:S(2)}) %collective-permute-start.5) | collective-permute-done | bytes 12320 | tf_op jit(solution)/shard_map/ppermute | solution.py:36
  23.9 1.4 %collective-permute-start.6 = (bf16[96,128]{1,0:T(8,128)(2,1)S(1)}, bf16[96,128]{1,0:T(8,128)(2,1)S(1)}, u32[]{:S(2)}, u32[]{:S(2)}) collective-permute-start(bf16[96,128]{1,0:T(8,128)(2,1)S(1)} %pad_maximum_fusion.5), channel_id=1, source_target_pairs={{0,3},{1,8},{2,11},{3,0},{4,13},{5,6},{6,5},{7,14},{8,1},{9,10},{1... | collective-permute-start | bytes 73736 | tf_op jit(solution)/shard_map/ppermute | solution.py:36
  25.4 1.8 %collective-permute-done.6 = bf16[96,128]{1,0:T(8,128)(2,1)S(1)} collective-permute-done((bf16[96,128]{1,0:T(8,128)(2,1)S(1)}, bf16[96,128]{1,0:T(8,128)(2,1)S(1)}, u32[]{:S(2)}, u32[]{:S(2)}) %collective-permute-start.6) | collective-permute-done | bytes 24608 | tf_op jit(solution)/shard_map/ppermute | solution.py:36
  27.2 1.7 %collective-permute-start.7 = (bf16[192,128]{1,0:T(8,128)(2,1)S(1)}, bf16[192,128]{1,0:T(8,128)(2,1)S(1)}, u32[]{:S(2)}, u32[]{:S(2)}) collective-permute-start(bf16[192,128]{1,0:T(8,128)(2,1)S(1)} %constant_dynamic-update-slice_fusion.mine), channel_id=1, source_target_pairs={{0,5},{1,2},{2,1},{3,6},{4,7},{5,0},{6,3},{7,4},{8,11},{9,12},{10,... | collective-permute-start | bytes 147464 | tf_op jit(solution)/shard_map/ppermute | solution.py:36
  28.9 0.2 shard_map.80.known
  29.1 1.6 %collective-permute-done.7.theirs = bf16[192,128]{1,0:T(8,128)(2,1)S(1)} collective-permute-done((bf16[192,128]{1,0:T(8,128)(2,1)S(1)}, bf16[192,128]{1,0:T(8,128)(2,1)S(1)}, u32[]{:S(2)}, u32[]{:S(2)}) %collective-permute-start.7) | collective-permute-done | bytes 49184 | tf_op jit(solution)/shard_map/ppermute | solution.py:36
  30.7 0.9 %shard_map.81 = f32[12,64]{1,0:T(8,128)} custom-call(f32[48,256]{1,0:T(8,128)S(1)} %shard_map.80.known, bf16[192,128]{1,0:T(8,128)(2,1)S(1)} %collective-permute-done.7.theirs, bf16[64,4096]{1,0:T(8,128)(2,1)S(1)} %shard_map.79.store), custom_call_target="tpu_custom_call" | custom-call | tf_op jit(solution)/shard_map/pallas_call | solution.py:334
  (20 shorter events, 0.2 us)
Async XLA Ops:
  2.8 1.5 %collective-permute-start = (f32[128,128]{1,0:T(8,128)S(1)}, f32[128,128]{1,0:T(8,128)S(1)}, u32[]{:S(2)}, u32[]{:S(2)}) collective-permute-start(f32[128,128]{1,0:T(8,128)S(1)} %get-tuple-element.29.part), channel_id=1, source_target_pairs={{0,1},{1,0},{2,3},{3,2},{4,5},{5,4},{6,7},{7,6},{8,9},{9,8},{10,11... | collective-permute-start | bytes 196616 | tf_op jit(solution)/shard_map/ppermute | solution.py:36
  4.7 5.3 %collective-permute-start.1 = (f16[104,128]{1,0:T(8,128)(2,1)S(1)}, f16[104,128]{1,0:T(8,128)(2,1)S(1)}, u32[]{:S(2)}, u32[]{:S(2)}) collective-permute-start(f16[104,128]{1,0:T(8,128)(2,1)S(1)} %pad_maximum_fusion.4), channel_id=1, source_target_pairs={{0,9},{1,4},{2,7},{3,10},{4,1},{5,12},{6,15},{7,2},{8,13},{9,0},{1... | collective-permute-start | bytes 79880 | tf_op jit(solution)/shard_map/ppermute | solution.py:36
  10.2 3.6 %collective-permute-start.2 = (f16[200,128]{1,0:T(8,128)(2,1)S(1)}, f16[200,128]{1,0:T(8,128)(2,1)S(1)}, u32[]{:S(2)}, u32[]{:S(2)}) collective-permute-start(f16[200,128]{1,0:T(8,128)(2,1)S(1)} %pad_maximum_fusion.2), channel_id=1, source_target_pairs={{0,3},{1,8},{2,11},{3,0},{4,13},{5,6},{6,5},{7,14},{8,1},{9,10},{1... | collective-permute-start | bytes 153608 | tf_op jit(solution)/shard_map/ppermute | solution.py:36
  13.9 3.6 %collective-permute-start.3 = (f16[200,128]{1,0:T(8,128)(2,1)S(1)}, f16[200,128]{1,0:T(8,128)(2,1)S(1)}, u32[]{:S(2)}, u32[]{:S(2)}) collective-permute-start(f16[200,128]{1,0:T(8,128)(2,1)S(1)} %get-tuple-element.61), channel_id=1, source_target_pairs={{0,5},{1,2},{2,1},{3,6},{4,7},{5,0},{6,3},{7,4},{8,11},{9,12},{10,... | collective-permute-start | bytes 153608 | tf_op jit(solution)/shard_map/ppermute | solution.py:36
  18.5 1.3 %collective-permute-start.4 = (f32[12,512]{1,0:T(8,128)S(1)}, f32[12,512]{1,0:T(8,128)S(1)}, u32[]{:S(2)}, u32[]{:S(2)}) collective-permute-start(f32[12,512]{1,0:T(8,128)S(1)} %shard_map.78), channel_id=1, source_target_pairs={{0,1},{1,0},{2,3},{3,2},{4,5},{5,4},{6,7},{7,6},{8,9},{9,8},{10,11... | collective-permute-start | bytes 73736 | tf_op jit(solution)/shard_map/ppermute | solution.py:36
  19.8 4.1 %collective-permute-start.5 = (bf16[48,128]{1,0:T(8,128)(2,1)S(1)}, bf16[48,128]{1,0:T(8,128)(2,1)S(1)}, u32[]{:S(2)}, u32[]{:S(2)}) collective-permute-start(bf16[48,128]{1,0:T(8,128)(2,1)S(1)} %reshape.35.after), channel_id=1, source_target_pairs={{0,9},{1,4},{2,7},{3,10},{4,1},{5,12},{6,15},{7,2},{8,13},{9,0},{1... | collective-permute-start | bytes 36872 | tf_op jit(solution)/shard_map/ppermute | solution.py:36
  23.9 3.3 %collective-permute-start.6 = (bf16[96,128]{1,0:T(8,128)(2,1)S(1)}, bf16[96,128]{1,0:T(8,128)(2,1)S(1)}, u32[]{:S(2)}, u32[]{:S(2)}) collective-permute-start(bf16[96,128]{1,0:T(8,128)(2,1)S(1)} %pad_maximum_fusion.5), channel_id=1, source_target_pairs={{0,3},{1,8},{2,11},{3,0},{4,13},{5,6},{6,5},{7,14},{8,1},{9,10},{1... | collective-permute-start | bytes 73736 | tf_op jit(solution)/shard_map/ppermute | solution.py:36
  27.2 3.5 %collective-permute-start.7 = (bf16[192,128]{1,0:T(8,128)(2,1)S(1)}, bf16[192,128]{1,0:T(8,128)(2,1)S(1)}, u32[]{:S(2)}, u32[]{:S(2)}) collective-permute-start(bf16[192,128]{1,0:T(8,128)(2,1)S(1)} %constant_dynamic-update-slice_fusion.mine), channel_id=1, source_target_pairs={{0,5},{1,2},{2,1},{3,6},{4,7},{5,0},{6,3},{7,4},{8,11},{9,12},{10,... | collective-permute-start | bytes 147464 | tf_op jit(solution)/shard_map/ppermute | solution.py:36
